TPU v7x, 512 devices: a whole 4x4x16 slice. The times are simulated.
512 devices in a mesh: dp: 16 (over x_lo, y, core), seq: 32 (over z, x_hi).
Axes of the slice: x: 4 (x_hi: 2, x_lo: 2; x = x_hi * 2 + x_lo), y: 4, z: 16, core: 2. Of those that a mesh axis runs over, the one named last changes fastest.
Arguments:
- tokens: bfloat16 [8192, 6144], P('seq'), may hold values from -6 to 6
- qkv_weight: bfloat16 [6144, 3, 4096], P('seq', None, 'dp'), may hold values from -0.078125 to 0.078125
- out_weight: bfloat16 [6144, 4096], P('seq', 'dp'), may hold values from -0.1875 to 0.1875
- log_decay: float32 [32, 8192], P('dp', 'seq'), may hold values from -1.5 to 0, as said below
- norm_gain: float32 [4096], P('dp'), may hold values from 0.25 to 1.75
Outputs:
- mixed: bfloat16 [8192, 6144], P('seq', 'dp')
Inputs may be any that keep to these rules, and one draw needn't show every extreme that they name: `log_decay`: each entry is the logarithm of one head's decay factor at one position.
All inputs are finite; a program needn't handle non-finite values.
Results may differ from a plain program's by a relative error of at most 0.023.
Values may be sent and summed in bfloat16 or wider, within the bound.
No kernel may reach another device: no remote copies, remote signals or barrier semaphores. Data moves between devices by JAX's collectives and lax.ppermute only.
A program may use at most 64 MiB of HBM per device.

v0:
```python
import jax
import jax.numpy as jnp
from jax import lax
from jax.sharding import PartitionSpec as P


def ring_perm(n, step):
    return [(s, (s + step) % n) for s in range(n)]


def pair_perm(n):
    return [(s, s ^ 1) for s in range(n)]


def three_parts(x):
    high = lax.reduce_precision(x, 8, 7)
    middle = lax.reduce_precision(x - high, 8, 7)
    return jnp.stack([high, middle, x - high - middle], axis=-1).astype(jnp.bfloat16)


def exclusive_state(local, log_fall, half, n):
    f32 = jnp.float32
    heads, hsize, _ = local.shape
    n_z = n // 2
    rows = heads * hsize * hsize // (n_z * 128)
    flat = local.astype(jnp.bfloat16).reshape(heads * hsize, hsize)
    tail = jnp.pad(three_parts(log_fall), ((0, 16 - heads), (0, hsize - 3)))
    got = lax.ppermute(jnp.concatenate([flat, tail], axis=0), "seq", pair_perm(n))
    other = got[: heads * hsize].astype(f32).reshape(heads, hsize, hsize)
    other_fall = jnp.sum(got[heads * hsize : heads * hsize + heads, :3].astype(f32), axis=1)
    joined = jnp.where(
        half == 0,
        jnp.exp(other_fall)[:, None, None] * local + other,
        jnp.exp(log_fall)[:, None, None] * other + local,
    )
    slices = joined.astype(jnp.bfloat16).reshape(n_z, rows, 128)
    falls = jnp.repeat(three_parts(log_fall + other_fall), n_z // heads, axis=0)
    falls = jnp.pad(falls[:, None, :], ((0, 0), (0, 7), (0, 128 - 3)))
    groups = [[2 * i + x for i in range(n_z)] for x in range(2)]
    sent = jnp.concatenate([slices, falls], axis=1)
    got = lax.all_to_all(sent, "seq", 0, 0, axis_index_groups=groups, tiled=True)
    fall_of = jnp.sum(got[:, rows, :3].astype(f32), axis=1)
    at = jnp.arange(n_z)
    between = (at[None, None, :] > at[None, :, None]) & (at[None, None, :] < at[:, None, None])
    total = jnp.sum(jnp.where(between, fall_of[None, None, :], 0.0), axis=2)
    mix = jnp.where(at[None, :] < at[:, None], jnp.exp(total), 0.0)
    slices = got[:, :rows, :].reshape(n_z, rows * 128).astype(f32)
    earlier = jnp.dot(mix, slices, precision=lax.Precision.HIGHEST)
    earlier = earlier.astype(jnp.bfloat16).reshape(n_z, rows, 128)
    back = lax.all_to_all(earlier, "seq", 0, 0, axis_index_groups=groups, tiled=True)
    back = back.reshape(heads, hsize, hsize)
    after = jnp.exp(other_fall)[:, None, None] * back.astype(f32) + other
    return jnp.where(half == 0, back, after.astype(jnp.bfloat16))


def make_body(n_seq, n_dp):
    n_z = n_seq // 2
    up, down, flip = ring_perm(n_seq, 2), ring_perm(n_seq, -2), pair_perm(n_seq)

    def layer(tokens, qkv_weight, out_weight, log_decay, norm_gain):
        rows, _ = tokens.shape
        width = qkv_weight.shape[2]
        heads = log_decay.shape[0]
        hsize = width // heads
        shard = qkv_weight.shape[0]
        place = lax.axis_index("seq")
        z, half = place // 2, place % 2
        core = lax.axis_index("dp") % 2
        f32 = jnp.float32

        parts = jnp.transpose(qkv_weight, (1, 0, 2))
        own = jnp.concatenate([parts[1], parts[2], parts[0], out_weight], axis=1)
        pieces = {0: own}
        last = n_z // 2
        ahead = behind = own
        for k in range(1, last):
            ahead = lax.ppermute(ahead, "seq", up)
            behind = lax.ppermute(behind, "seq", down)
            pieces[-k], pieces[k] = ahead, behind
        top = lax.ppermute(ahead[: shard // 2], "seq", up)
        bottom = lax.ppermute(behind[shard // 2 :], "seq", down)
        pieces[last] = jnp.concatenate([top, bottom], axis=0)
        order = sorted(pieces, key=lambda o: (abs(o), o))

        by_z = tokens.T.reshape(n_z, 2, shard, rows)
        mine = lax.dynamic_index_in_dim(by_z, half, 1, False)
        theirs = lax.dynamic_index_in_dim(by_z, 1 - half, 1, False)
        theirs = lax.ppermute(theirs, "seq", flip)
        both = jnp.concatenate([mine, theirs], axis=2)

        def times(o):
            tok = lax.dynamic_index_in_dim(both, (z + o) % n_z, 0, False)
            weight = pieces[o][:, : 3 * width]
            return lax.dot_general(tok, weight, (((0,), (0,)), ((), ())), preferred_element_type=f32)

        def combine(partial):
            sent = lax.ppermute(partial[rows:].astype(jnp.bfloat16), "seq", flip)
            return partial[:rows] + sent.astype(f32)

        proj = sum(times(o) for o in order)
        kv_proj = combine(proj[:, : 2 * width])
        q_proj = combine(proj[:, 2 * width :])

        other_outs = {}
        for batch in (order[:7], order[7:13], order[13:]):
            joined = jnp.concatenate([pieces[o][:, 3 * width :] for o in batch], axis=0)
            swapped = lax.ppermute(joined, "seq", flip)
            for i, o in enumerate(batch):
                other_outs[o] = swapped[i * shard : (i + 1) * shard]
        in_order = list(range(0, last + 1)) + list(range(-last + 1, 0))
        outs = jnp.stack(
            [
                jnp.stack([pieces[o][:, 3 * width :], other_outs[o], pieces[o][:, 3 * width :]])
                for o in in_order
            ]
        )
        outs = lax.dynamic_slice_in_dim(outs, half, 2, axis=1)
        outs = jnp.roll(outs, z, axis=0).reshape(n_z // 2, 2, 2 * shard, width)
        out_mine = lax.dynamic_index_in_dim(outs, core, 1, False)
        out_theirs = lax.dynamic_index_in_dim(outs, 1 - core, 1, False)

        key = jax.nn.silu(kv_proj[:, :width]).astype(jnp.bfloat16).reshape(rows, heads, hsize)
        value = kv_proj[:, width:].astype(jnp.bfloat16).reshape(rows, heads, hsize)
        query = jax.nn.silu(q_proj).astype(jnp.bfloat16).reshape(rows, heads, hsize)
        cum = jnp.cumsum(log_decay, axis=1)
        scaled_key = (key.astype(f32) * jnp.exp(cum[:, -1:] - cum).T[:, :, None]).astype(jnp.bfloat16)
        local = jnp.einsum("thd,the->hde", scaled_key, value, preferred_element_type=f32)
        earlier_state = exclusive_state(local, cum[:, -1], half, n_seq)

        later = jnp.arange(rows)[:, None] >= jnp.arange(rows)[None, :]
        scores = jnp.einsum("thd,shd->hts", query, key, preferred_element_type=f32)
        spread = cum[:, :, None] - cum[:, None, :]
        factor = jnp.where(later[None], jnp.exp(jnp.minimum(spread, 0.0)), 0.0)
        weights = (scores * factor).astype(jnp.bfloat16)
        intra = jnp.einsum("hts,shd->thd", weights, value, preferred_element_type=f32)
        carried = jnp.einsum("thd,hde->the", query, earlier_state, preferred_element_type=f32)
        attn = intra + carried * jnp.exp(cum).T[:, :, None]
        power = jnp.mean(attn * attn, axis=-1, keepdims=True)
        gain = norm_gain.reshape(heads, hsize)
        normed = (attn / jnp.sqrt(power + 1e-05) * gain[None]).astype(jnp.bfloat16).reshape(rows, width)

        wide = jnp.broadcast_to(normed[None], (n_dp // 2, rows, width))
        give = jnp.einsum("itg,idg->itd", wide, out_theirs, preferred_element_type=f32)
        taken = lax.ppermute(give.astype(jnp.bfloat16), "dp", pair_perm(n_dp))
        keep = jnp.einsum("itg,idg->itd", wide, out_mine, preferred_element_type=f32)
        keep = keep.astype(jnp.bfloat16).astype(f32) + taken.astype(f32)
        groups = [[2 * i + c for i in range(n_dp // 2)] for c in range(2)]
        spread_out = lax.all_to_all(keep.astype(jnp.bfloat16), "dp", 0, 0, axis_index_groups=groups, tiled=True)
        return jnp.sum(spread_out.astype(f32), axis=0).astype(jnp.bfloat16)

    return layer


def solution(mesh):
    body = make_body(mesh.shape["seq"], mesh.shape["dp"])
    in_specs = (P("seq", None), P("seq", None, "dp"), P("seq", "dp"), P("dp", "seq"), P("dp"))
    return jax.shard_map(body, mesh=mesh, in_specs=in_specs, out_specs=P("seq", "dp"), check_vma=False)
```

profile of v0, /device:TPU:4, one launch (start us, length us, event | category | flops | bytes accessed | tf_op | source)
XLA Modules:
  0.0 246.2 jit_solution(11166528664191532159)
XLA Ops:
  1.0 1.7 pad_maximum_fusion
  2.7 11.4 %collective-permute-start.2 = (bf16[192,1024]{1,0:T(8,128)(2,1)}, bf16[192,1024]{1,0:T(8,128)(2,1)}, u32[]{:S(2)}, u32[]{:S(2)}) collective-permute-start(bf16[192,1024]{1,0:T(8,128)(2,1)} %pad_maximum_fusion), channel_id=1, source_target_pairs={{0,30},{1,31},{2,0},{3,1},{4,2},{5,3},{6,4},{7,5},{8,6},{9,7},{10,... | collective-permute-start | bytes 1179656 | tf_op jit(solution)/shard_map/ppermute | solution.py:78
  14.1 1.9 collective-permute-start.1
  16.1 4.7 %copy.25 = bf16[256,6144]{0,1:T(8,128)(2,1)} copy(bf16[256,6144]{1,0:T(8,128)(2,1)} %param.5) | data formatting | bytes 6291456 | tf_op args[0]
  20.7 3.4 %dynamic-slice_bitcast_fusion = (bf16[16,192,256]{2,1,0:T(8,128)(2,1)}, bf16[16,192,256]{2,1,0:T(8,128)(2,1)S(1)}) fusion(bf16[16,2,192,256]{3,2,1,0:T(8,128)(2,1)} %bitcast.282, s32[]{:T(128)S(6)} %select_n.183, s32[]{:T(128)S(6)} %select_n.182), kind=kLoop, calls=%fused_computation.44 | loop fusion | bytes 6291464 | tf_op jit(solution)/shard_map/jit(dynamic_index_in_dim)/squeeze | solution.py:87
  24.2 2.4 collective-permute-start
  32.6 5.1 %collective-permute-start.4 = (bf16[192,1024]{1,0:T(8,128)(2,1)}, bf16[192,1024]{1,0:T(8,128)(2,1)S(1)}, u32[]{:S(2)}, u32[]{:S(2)}) collective-permute-start(bf16[192,1024]{1,0:T(8,128)(2,1)} %collective-permute-done.2), channel_id=1, source_target_pairs={{0,30},{1,31},{2,0},{3,1},{4,2},{5,3},{6,4},{7,5},{8,6},{9,7},{10,... | collective-permute-start | bytes 1179656 | tf_op jit(solution)/shard_map/ppermute | solution.py:78
  37.7 1.9 collective-permute-start.3
  39.7 1.5 slice_bitcast_fusion.30
  42.1 3.4 %collective-permute-done.4 = bf16[192,1024]{1,0:T(8,128)(2,1)S(1)} collective-permute-done((bf16[192,1024]{1,0:T(8,128)(2,1)}, bf16[192,1024]{1,0:T(8,128)(2,1)S(1)}, u32[]{:S(2)}, u32[]{:S(2)}) %collective-permute-start.4) | collective-permute-done | bytes 393248 | tf_op jit(solution)/shard_map/ppermute | solution.py:78
  45.6 5.5 %collective-permute-start.6 = (bf16[192,1024]{1,0:T(8,128)(2,1)S(1)}, bf16[192,1024]{1,0:T(8,128)(2,1)S(1)}, u32[]{:S(2)}, u32[]{:S(2)}) collective-permute-start(bf16[192,1024]{1,0:T(8,128)(2,1)S(1)} %collective-permute-done.4), channel_id=1, source_target_pairs={{0,30},{1,31},{2,0},{3,1},{4,2},{5,3},{6,4},{7,5},{8,6},{9,7},{10,... | collective-permute-start | bytes 1179656 | tf_op jit(solution)/shard_map/ppermute | solution.py:78
  51.1 1.9 collective-permute-start.5
  53.6 4.0 %collective-permute-done.6 = bf16[192,1024]{1,0:T(8,128)(2,1)S(1)} collective-permute-done((bf16[192,1024]{1,0:T(8,128)(2,1)S(1)}, bf16[192,1024]{1,0:T(8,128)(2,1)S(1)}, u32[]{:S(2)}, u32[]{:S(2)}) %collective-permute-start.6) | collective-permute-done | bytes 393248 | tf_op jit(solution)/shard_map/ppermute | solution.py:78
  57.7 5.6 %collective-permute-start.8 = (bf16[192,1024]{1,0:T(8,128)(2,1)S(1)}, bf16[192,1024]{1,0:T(8,128)(2,1)S(1)}, u32[]{:S(2)}, u32[]{:S(2)}) collective-permute-start(bf16[192,1024]{1,0:T(8,128)(2,1)S(1)} %collective-permute-done.6), channel_id=1, source_target_pairs={{0,30},{1,31},{2,0},{3,1},{4,2},{5,3},{6,4},{7,5},{8,6},{9,7},{10,... | collective-permute-start | bytes 1179656 | tf_op jit(solution)/shard_map/ppermute | solution.py:78
  63.3 1.9 collective-permute-start.7
  65.9 4.9 %collective-permute-start.20 = (bf16[1344,256]{1,0:T(8,128)(2,1)S(1)}, bf16[1344,256]{1,0:T(8,128)(2,1)S(1)}, u32[]{:S(2)}, u32[]{:S(2)}) collective-permute-start(bf16[1344,256]{1,0:T(8,128)(2,1)S(1)} %get-tuple-element.45), channel_id=1, source_target_pairs={{0,1},{1,0},{2,3},{3,2},{4,5},{5,4},{6,7},{7,6},{8,9},{9,8},{10,11... | collective-permute-start | bytes 2064392 | tf_op jit(solution)/shard_map/ppermute | solution.py:107
  70.8 5.1 %collective-permute-start.10 = (bf16[192,1024]{1,0:T(8,128)(2,1)S(1)}, bf16[192,1024]{1,0:T(8,128)(2,1)S(1)}, u32[]{:S(2)}, u32[]{:S(2)}) collective-permute-start(bf16[192,1024]{1,0:T(8,128)(2,1)S(1)} %collective-permute-done.8), channel_id=1, source_target_pairs={{0,30},{1,31},{2,0},{3,1},{4,2},{5,3},{6,4},{7,5},{8,6},{9,7},{10,... | collective-permute-start | bytes 1179656 | tf_op jit(solution)/shard_map/ppermute | solution.py:78
  76.0 1.9 collective-permute-start.9
  80.7 1.4 fusion.47
  88.8 5.1 %collective-permute-start.12 = (bf16[192,1024]{1,0:T(8,128)(2,1)S(1)}, bf16[192,1024]{1,0:T(8,128)(2,1)S(1)}, u32[]{:S(2)}, u32[]{:S(2)}) collective-permute-start(bf16[192,1024]{1,0:T(8,128)(2,1)S(1)} %collective-permute-done.10), channel_id=1, source_target_pairs={{0,30},{1,31},{2,0},{3,1},{4,2},{5,3},{6,4},{7,5},{8,6},{9,7},{10,... | collective-permute-start | bytes 1179656 | tf_op jit(solution)/shard_map/ppermute | solution.py:78
  93.9 1.9 collective-permute-start.11
  98.1 6.7 %collective-permute-done.11 = bf16[192,1024]{1,0:T(8,128)(2,1)S(1)} collective-permute-done((bf16[192,1024]{1,0:T(8,128)(2,1)S(1)}, bf16[192,1024]{1,0:T(8,128)(2,1)S(1)}, u32[]{:S(2)}, u32[]{:S(2)}) %collective-permute-start.11) | collective-permute-done | bytes 393248 | tf_op jit(solution)/shard_map/ppermute | solution.py:77
  106.2 3.6 %collective-permute-start.21 = (bf16[1152,256]{1,0:T(8,128)(2,1)}, bf16[1152,256]{1,0:T(8,128)(2,1)}, u32[]{:S(2)}, u32[]{:S(2)}) collective-permute-start(bf16[1152,256]{1,0:T(8,128)(2,1)} %get-tuple-element.39), channel_id=1, source_target_pairs={{0,1},{1,0},{2,3},{3,2},{4,5},{5,4},{6,7},{7,6},{8,9},{9,8},{10,11... | collective-permute-start | bytes 1769480 | tf_op jit(solution)/shard_map/ppermute | solution.py:107
  109.8 1.9 collective-permute-start.14
  111.7 3.9 %collective-permute-start.13 = (bf16[192,1024]{1,0:T(8,128)(2,1)S(1)}, bf16[192,1024]{1,0:T(8,128)(2,1)S(1)}, u32[]{:S(2)}, u32[]{:S(2)}) collective-permute-start(bf16[192,1024]{1,0:T(8,128)(2,1)S(1)} %collective-permute-done.11), channel_id=1, source_target_pairs={{0,2},{1,3},{2,4},{3,5},{4,6},{5,7},{6,8},{7,9},{8,10},{9,11},{10,... | collective-permute-start | bytes 1179656 | tf_op jit(solution)/shard_map/ppermute | solution.py:77
  116.5 5.1 %collective-permute-done.14 = bf16[192,1024]{1,0:T(8,128)(2,1)S(1)} collective-permute-done((bf16[192,1024]{1,0:T(8,128)(2,1)S(1)}, bf16[192,1024]{1,0:T(8,128)(2,1)S(1)}, u32[]{:S(2)}, u32[]{:S(2)}) %collective-permute-start.14) | collective-permute-done | bytes 393248 | tf_op jit(solution)/shard_map/ppermute | solution.py:78
  121.6 1.9 collective-permute-start.16
  123.6 3.8 %collective-permute-start.15 = (bf16[96,1024]{1,0:T(8,128)(2,1)S(1)}, bf16[96,1024]{1,0:T(8,128)(2,1)S(1)}, u32[]{:S(2)}, u32[]{:S(2)}) collective-permute-start(bf16[96,1024]{1,0:T(8,128)(2,1)S(1)} %slice.315), channel_id=1, source_target_pairs={{0,2},{1,3},{2,4},{3,5},{4,6},{5,7},{6,8},{7,9},{8,10},{9,11},{10,... | collective-permute-start | bytes 589832 | tf_op jit(solution)/shard_map/ppermute | solution.py:80
  129.2 3.2 %collective-permute-done.15 = bf16[96,1024]{1,0:T(8,128)(2,1)S(1)} collective-permute-done((bf16[96,1024]{1,0:T(8,128)(2,1)S(1)}, bf16[96,1024]{1,0:T(8,128)(2,1)S(1)}, u32[]{:S(2)}, u32[]{:S(2)}) %collective-permute-start.15) | collective-permute-done | bytes 196640 | tf_op jit(solution)/shard_map/ppermute | solution.py:80
  133.7 2.1 fusion.196
  135.8 1.7 slice.322
  139.5 3.6 %collective-permute-start.22 = (bf16[576,256]{1,0:T(8,128)(2,1)S(1)}, bf16[576,256]{1,0:T(8,128)(2,1)S(1)}, u32[]{:S(2)}, u32[]{:S(2)}) collective-permute-start(bf16[576,256]{1,0:T(8,128)(2,1)S(1)} %pad_maximum_fusion.1), channel_id=1, source_target_pairs={{0,1},{1,0},{2,3},{3,2},{4,5},{5,4},{6,7},{7,6},{8,9},{9,8},{10,11... | collective-permute-start | bytes 884744 | tf_op jit(solution)/shard_map/ppermute | solution.py:107
  143.2 3.7 %collective-permute-start.18 = (bf16[256,256]{1,0:T(8,128)(2,1)}, bf16[256,256]{1,0:T(8,128)(2,1)}, u32[]{:S(2)}, u32[]{:S(2)}) collective-permute-start(bf16[256,256]{1,0:T(8,128)(2,1)} %slice.322), channel_id=1, source_target_pairs={{0,1},{1,0},{2,3},{3,2},{4,5},{5,4},{6,7},{7,6},{8,9},{9,8},{10,11... | collective-permute-start | bytes 393224 | tf_op jit(solution)/shard_map/ppermute | solution.py:97
  146.9 3.6 %collective-permute-start.17 = (bf16[256,512]{1,0:T(8,128)(2,1)S(1)}, bf16[256,512]{1,0:T(8,128)(2,1)S(1)}, u32[]{:S(2)}, u32[]{:S(2)}) collective-permute-start(bf16[256,512]{1,0:T(8,128)(2,1)S(1)} %slice.319), channel_id=1, source_target_pairs={{0,1},{1,0},{2,3},{3,2},{4,5},{5,4},{6,7},{7,6},{8,9},{9,8},{10,11... | collective-permute-start | bytes 786440 | tf_op jit(solution)/shard_map/ppermute | solution.py:97
  153.9 3.5 %collective-permute-done.17 = bf16[256,512]{1,0:T(8,128)(2,1)S(1)} collective-permute-done((bf16[256,512]{1,0:T(8,128)(2,1)S(1)}, bf16[256,512]{1,0:T(8,128)(2,1)S(1)}, u32[]{:S(2)}, u32[]{:S(2)}) %collective-permute-start.17) | collective-permute-done | bytes 262176 | tf_op jit(solution)/shard_map/ppermute | solution.py:97
  157.9 3.6 %collective-permute-start.19 = (bf16[272,128]{1,0:T(8,128)(2,1)S(1)}, bf16[272,128]{1,0:T(8,128)(2,1)S(1)}, u32[]{:S(2)}, u32[]{:S(2)}) collective-permute-start(bf16[272,128]{1,0:T(8,128)(2,1)S(1)} %fusion.147), channel_id=1, source_target_pairs={{0,1},{1,0},{2,3},{3,2},{4,5},{5,4},{6,7},{7,6},{8,9},{9,8},{10,11... | collective-permute-start | bytes 208904 | tf_op jit(solution)/shard_map/ppermute | solution.py:28
  166.8 6.3 %all-to-all-start = ((bf16[16,24,128]{2,1,0:T(8,128)(2,1)}), bf16[16,24,128]{2,1,0:T(8,128)(2,1)S(1)}, u32[]{:S(2)}, u32[]{:S(2)}) async-start(bf16[16,24,128]{2,1,0:T(8,128)(2,1)} %fusion.146), calls=%async_computation | async-start | bytes 196608 | tf_op jit(solution)/shard_map/all_to_all | solution.py:41
  176.1 10.1 %all-to-all-done = bf16[16,24,128]{2,1,0:T(8,128)(2,1)S(1)} async-done(((bf16[16,24,128]{2,1,0:T(8,128)(2,1)}), bf16[16,24,128]{2,1,0:T(8,128)(2,1)S(1)}, u32[]{:S(2)}, u32[]{:S(2)}) %all-to-all-start) | async-done | bytes 98336 | tf_op jit(solution)/shard_map/all_to_all | solution.py:41
  187.4 3.5 %all-to-all-start.1 = ((bf16[16,16,128]{2,1,0:T(8,128)(2,1)}), bf16[16,16,128]{2,1,0:T(8,128)(2,1)S(1)}, u32[]{:S(2)}, u32[]{:S(2)}) async-start(bf16[16,16,128]{2,1,0:T(8,128)(2,1)} %bitcast.100), calls=%async_computation.1 | async-start | bytes 131072 | tf_op jit(solution)/shard_map/all_to_all | solution.py:50
  190.9 2.1 constant_dynamic-slice_fusion
  194.2 9.4 %all-to-all-done.1 = bf16[16,16,128]{2,1,0:T(8,128)(2,1)S(1)} async-done(((bf16[16,16,128]{2,1,0:T(8,128)(2,1)}), bf16[16,16,128]{2,1,0:T(8,128)(2,1)S(1)}, u32[]{:S(2)}, u32[]{:S(2)}) %all-to-all-start.1) | async-done | bytes 65568 | tf_op jit(solution)/shard_map/all_to_all | solution.py:50
  203.6 2.0 fusion.11
  205.7 2.3 multiply_reduce_fusion
  209.1 1.9 convolution_convert_fusion.1
  211.0 1.9 collective-permute-start.23
  213.0 3.7 %collective-permute-done.23 = bf16[8,256,384]{2,1,0:T(8,128)(2,1)} collective-permute-done((bf16[8,256,384]{2,1,0:T(8,128)(2,1)}, bf16[8,256,384]{2,1,0:T(8,128)(2,1)}, u32[]{:S(2)}, u32[]{:S(2)}) %collective-permute-start.23) | collective-permute-done | bytes 1572896 | tf_op jit(solution)/shard_map/ppermute | solution.py:144
  216.7 2.1 add_convert_fusion
  218.8 26.5 %all_to_all.15 = bf16[8,256,384]{2,1,0:T(8,128)(2,1)S(1)} all-to-all(bf16[8,256,384]{2,1,0:T(8,128)(2,1)S(1)} %add_convert_fusion), channel_id=1, replica_groups={{0,64,128,192,256,320,384,448},{32,96,160,224,288,352,416,480},{1,65,12..., dimensions={0} | all-to-all | bytes 3145728 | tf_op jit(solution)/shard_map/all_to_all | solution.py:148
  (168 shorter events, 44.6 us)
Async XLA Ops:
  2.7 29.9 %collective-permute-start.2 = (bf16[192,1024]{1,0:T(8,128)(2,1)}, bf16[192,1024]{1,0:T(8,128)(2,1)}, u32[]{:S(2)}, u32[]{:S(2)}) collective-permute-start(bf16[192,1024]{1,0:T(8,128)(2,1)} %pad_maximum_fusion), channel_id=1, source_target_pairs={{0,30},{1,31},{2,0},{3,1},{4,2},{5,3},{6,4},{7,5},{8,6},{9,7},{10,... | collective-permute-start | bytes 1179656 | tf_op jit(solution)/shard_map/ppermute | solution.py:78
  14.1 23.6 %collective-permute-start.1 = (bf16[192,1024]{1,0:T(8,128)(2,1)}, bf16[192,1024]{1,0:T(8,128)(2,1)}, u32[]{:S(2)}, u32[]{:S(2)}) collective-permute-start(bf16[192,1024]{1,0:T(8,128)(2,1)} %pad_maximum_fusion), channel_id=1, source_target_pairs={{0,2},{1,3},{2,4},{3,5},{4,6},{5,7},{6,8},{7,9},{8,10},{9,11},{10,... | collective-permute-start | bytes 1179656 | tf_op jit(solution)/shard_map/ppermute | solution.py:77
  20.7 5.8 %copy-start.23 = (f32[2,256]{1,0:T(2,128)S(1)}, f32[2,256]{1,0:T(2,128)}, u32[]{:S(2)}) copy-start(f32[2,256]{1,0:T(2,128)} %param.8) | copy-start | bytes 6148
  20.7 10.7 %copy-start.2 = (bf16[192,256]{1,0:T(8,128)(2,1)S(1)}, bf16[192,256]{1,0:T(8,128)(2,1)}, u32[]{:S(2)}) copy-start(bf16[192,256]{1,0:T(8,128)(2,1)} %param.7) | copy-start | bytes 294916
  24.2 55.1 %collective-permute-start = (bf16[16,192,256]{2,1,0:T(8,128)(2,1)}, bf16[16,192,256]{2,1,0:T(8,128)(2,1)S(1)}, u32[]{:S(2)}, u32[]{:S(2)}) collective-permute-start(bf16[16,192,256]{2,1,0:T(8,128)(2,1)} %get-tuple-element.5), channel_id=1, source_target_pairs={{0,1},{1,0},{2,3},{3,2},{4,5},{5,4},{6,7},{7,6},{8,9},{9,8},{10,11... | collective-permute-start | bytes 4718600 | tf_op jit(solution)/shard_map/ppermute | solution.py:88
  32.6 13.0 %collective-permute-start.4 = (bf16[192,1024]{1,0:T(8,128)(2,1)}, bf16[192,1024]{1,0:T(8,128)(2,1)S(1)}, u32[]{:S(2)}, u32[]{:S(2)}) collective-permute-start(bf16[192,1024]{1,0:T(8,128)(2,1)} %collective-permute-done.2), channel_id=1, source_target_pairs={{0,30},{1,31},{2,0},{3,1},{4,2},{5,3},{6,4},{7,5},{8,6},{9,7},{10,... | collective-permute-start | bytes 1179656 | tf_op jit(solution)/shard_map/ppermute | solution.py:78
  37.7 13.3 %collective-permute-start.3 = (bf16[192,1024]{1,0:T(8,128)(2,1)}, bf16[192,1024]{1,0:T(8,128)(2,1)S(1)}, u32[]{:S(2)}, u32[]{:S(2)}) collective-permute-start(bf16[192,1024]{1,0:T(8,128)(2,1)} %collective-permute-done.1), channel_id=1, source_target_pairs={{0,2},{1,3},{2,4},{3,5},{4,6},{5,7},{6,8},{7,9},{8,10},{9,11},{10,... | collective-permute-start | bytes 1179656 | tf_op jit(solution)/shard_map/ppermute | solution.py:77
  45.6 12.1 %collective-permute-start.6 = (bf16[192,1024]{1,0:T(8,128)(2,1)S(1)}, bf16[192,1024]{1,0:T(8,128)(2,1)S(1)}, u32[]{:S(2)}, u32[]{:S(2)}) collective-permute-start(bf16[192,1024]{1,0:T(8,128)(2,1)S(1)} %collective-permute-done.4), channel_id=1, source_target_pairs={{0,30},{1,31},{2,0},{3,1},{4,2},{5,3},{6,4},{7,5},{8,6},{9,7},{10,... | collective-permute-start | bytes 1179656 | tf_op jit(solution)/shard_map/ppermute | solution.py:78
  51.1 12.2 %collective-permute-start.5 = (bf16[192,1024]{1,0:T(8,128)(2,1)S(1)}, bf16[192,1024]{1,0:T(8,128)(2,1)S(1)}, u32[]{:S(2)}, u32[]{:S(2)}) collective-permute-start(bf16[192,1024]{1,0:T(8,128)(2,1)S(1)} %collective-permute-done.3), channel_id=1, source_target_pairs={{0,2},{1,3},{2,4},{3,5},{4,6},{5,7},{6,8},{7,9},{8,10},{9,11},{10,... | collective-permute-start | bytes 1179656 | tf_op jit(solution)/shard_map/ppermute | solution.py:77
  57.7 13.1 %collective-permute-start.8 = (bf16[192,1024]{1,0:T(8,128)(2,1)S(1)}, bf16[192,1024]{1,0:T(8,128)(2,1)S(1)}, u32[]{:S(2)}, u32[]{:S(2)}) collective-permute-start(bf16[192,1024]{1,0:T(8,128)(2,1)S(1)} %collective-permute-done.6), channel_id=1, source_target_pairs={{0,30},{1,31},{2,0},{3,1},{4,2},{5,3},{6,4},{7,5},{8,6},{9,7},{10,... | collective-permute-start | bytes 1179656 | tf_op jit(solution)/shard_map/ppermute | solution.py:78
  63.3 12.7 %collective-permute-start.7 = (bf16[192,1024]{1,0:T(8,128)(2,1)S(1)}, bf16[192,1024]{1,0:T(8,128)(2,1)S(1)}, u32[]{:S(2)}, u32[]{:S(2)}) collective-permute-start(bf16[192,1024]{1,0:T(8,128)(2,1)S(1)} %collective-permute-done.5), channel_id=1, source_target_pairs={{0,2},{1,3},{2,4},{3,5},{4,6},{5,7},{6,8},{7,9},{8,10},{9,11},{10,... | collective-permute-start | bytes 1179656 | tf_op jit(solution)/shard_map/ppermute | solution.py:77
  65.9 19.2 %collective-permute-start.20 = (bf16[1344,256]{1,0:T(8,128)(2,1)S(1)}, bf16[1344,256]{1,0:T(8,128)(2,1)S(1)}, u32[]{:S(2)}, u32[]{:S(2)}) collective-permute-start(bf16[1344,256]{1,0:T(8,128)(2,1)S(1)} %get-tuple-element.45), channel_id=1, source_target_pairs={{0,1},{1,0},{2,3},{3,2},{4,5},{5,4},{6,7},{7,6},{8,9},{9,8},{10,11... | collective-permute-start | bytes 2064392 | tf_op jit(solution)/shard_map/ppermute | solution.py:107
  70.8 17.9 %collective-permute-start.10 = (bf16[192,1024]{1,0:T(8,128)(2,1)S(1)}, bf16[192,1024]{1,0:T(8,128)(2,1)S(1)}, u32[]{:S(2)}, u32[]{:S(2)}) collective-permute-start(bf16[192,1024]{1,0:T(8,128)(2,1)S(1)} %collective-permute-done.8), channel_id=1, source_target_pairs={{0,30},{1,31},{2,0},{3,1},{4,2},{5,3},{6,4},{7,5},{8,6},{9,7},{10,... | collective-permute-start | bytes 1179656 | tf_op jit(solution)/shard_map/ppermute | solution.py:78
  76.0 17.9 %collective-permute-start.9 = (bf16[192,1024]{1,0:T(8,128)(2,1)S(1)}, bf16[192,1024]{1,0:T(8,128)(2,1)S(1)}, u32[]{:S(2)}, u32[]{:S(2)}) collective-permute-start(bf16[192,1024]{1,0:T(8,128)(2,1)S(1)} %collective-permute-done.7), channel_id=1, source_target_pairs={{0,2},{1,3},{2,4},{3,5},{4,6},{5,7},{6,8},{7,9},{8,10},{9,11},{10,... | collective-permute-start | bytes 1179656 | tf_op jit(solution)/shard_map/ppermute | solution.py:77
  88.8 16.7 %collective-permute-start.12 = (bf16[192,1024]{1,0:T(8,128)(2,1)S(1)}, bf16[192,1024]{1,0:T(8,128)(2,1)S(1)}, u32[]{:S(2)}, u32[]{:S(2)}) collective-permute-start(bf16[192,1024]{1,0:T(8,128)(2,1)S(1)} %collective-permute-done.10), channel_id=1, source_target_pairs={{0,30},{1,31},{2,0},{3,1},{4,2},{5,3},{6,4},{7,5},{8,6},{9,7},{10,... | collective-permute-start | bytes 1179656 | tf_op jit(solution)/shard_map/ppermute | solution.py:78
  93.9 10.9 %collective-permute-start.11 = (bf16[192,1024]{1,0:T(8,128)(2,1)S(1)}, bf16[192,1024]{1,0:T(8,128)(2,1)S(1)}, u32[]{:S(2)}, u32[]{:S(2)}) collective-permute-start(bf16[192,1024]{1,0:T(8,128)(2,1)S(1)} %collective-permute-done.9), channel_id=1, source_target_pairs={{0,2},{1,3},{2,4},{3,5},{4,6},{5,7},{6,8},{7,9},{8,10},{9,11},{10,... | collective-permute-start | bytes 1179656 | tf_op jit(solution)/shard_map/ppermute | solution.py:77
  106.2 44.4 %collective-permute-start.21 = (bf16[1152,256]{1,0:T(8,128)(2,1)}, bf16[1152,256]{1,0:T(8,128)(2,1)}, u32[]{:S(2)}, u32[]{:S(2)}) collective-permute-start(bf16[1152,256]{1,0:T(8,128)(2,1)} %get-tuple-element.39), channel_id=1, source_target_pairs={{0,1},{1,0},{2,3},{3,2},{4,5},{5,4},{6,7},{7,6},{8,9},{9,8},{10,11... | collective-permute-start | bytes 1769480 | tf_op jit(solution)/shard_map/ppermute | solution.py:107
  109.8 11.8 %collective-permute-start.14 = (bf16[192,1024]{1,0:T(8,128)(2,1)S(1)}, bf16[192,1024]{1,0:T(8,128)(2,1)S(1)}, u32[]{:S(2)}, u32[]{:S(2)}) collective-permute-start(bf16[192,1024]{1,0:T(8,128)(2,1)S(1)} %collective-permute-done.12), channel_id=1, source_target_pairs={{0,30},{1,31},{2,0},{3,1},{4,2},{5,3},{6,4},{7,5},{8,6},{9,7},{10,... | collective-permute-start | bytes 1179656 | tf_op jit(solution)/shard_map/ppermute | solution.py:78
  111.7 11.9 %collective-permute-start.13 = (bf16[192,1024]{1,0:T(8,128)(2,1)S(1)}, bf16[192,1024]{1,0:T(8,128)(2,1)S(1)}, u32[]{:S(2)}, u32[]{:S(2)}) collective-permute-start(bf16[192,1024]{1,0:T(8,128)(2,1)S(1)} %collective-permute-done.11), channel_id=1, source_target_pairs={{0,2},{1,3},{2,4},{3,5},{4,6},{5,7},{6,8},{7,9},{8,10},{9,11},{10,... | collective-permute-start | bytes 1179656 | tf_op jit(solution)/shard_map/ppermute | solution.py:77
  121.6 10.8 %collective-permute-start.16 = (bf16[96,1024]{1,0:T(8,128)(2,1)S(1)}, bf16[96,1024]{1,0:T(8,128)(2,1)S(1)}, u32[]{:S(2)}, u32[]{:S(2)}) collective-permute-start(bf16[96,1024]{1,0:T(8,128)(2,1)S(1)} %slice.316), channel_id=1, source_target_pairs={{0,30},{1,31},{2,0},{3,1},{4,2},{5,3},{6,4},{7,5},{8,6},{9,7},{10,... | collective-permute-start | bytes 589832 | tf_op jit(solution)/shard_map/ppermute | solution.py:81
  123.6 8.8 %collective-permute-start.15 = (bf16[96,1024]{1,0:T(8,128)(2,1)S(1)}, bf16[96,1024]{1,0:T(8,128)(2,1)S(1)}, u32[]{:S(2)}, u32[]{:S(2)}) collective-permute-start(bf16[96,1024]{1,0:T(8,128)(2,1)S(1)} %slice.315), channel_id=1, source_target_pairs={{0,2},{1,3},{2,4},{3,5},{4,6},{5,7},{6,8},{7,9},{8,10},{9,11},{10,... | collective-permute-start | bytes 589832 | tf_op jit(solution)/shard_map/ppermute | solution.py:80
  135.8 21.6 %copy-start = (f32[512,768]{1,0:T(8,128)}, f32[512,768]{1,0:T(8,128)S(1)}, u32[]{:S(2)}) copy-start(f32[512,768]{1,0:T(8,128)S(1)} %get-tuple-element.65) | copy-start | bytes 4718596
  135.8 15.9 %copy-start.8 = (bf16[1,192,256]{2,1,0:T(8,128)(2,1)S(1)}, bf16[1,192,256]{2,1,0:T(8,128)(2,1)}, u32[]{:S(2)}) copy-start(bf16[1,192,256]{2,1,0:T(8,128)(2,1)} %get-tuple-element.43) | copy-start | bytes 294916
  137.5 14.9 %copy-start.11 = (bf16[1,192,256]{2,1,0:T(8,128)(2,1)S(1)}, bf16[1,192,256]{2,1,0:T(8,128)(2,1)}, u32[]{:S(2)}) copy-start(bf16[1,192,256]{2,1,0:T(8,128)(2,1)} %get-tuple-element.40) | copy-start | bytes 294916
  138.5 14.7 %copy-start.13 = (bf16[1,192,256]{2,1,0:T(8,128)(2,1)S(1)}, bf16[1,192,256]{2,1,0:T(8,128)(2,1)}, u32[]{:S(2)}) copy-start(bf16[1,192,256]{2,1,0:T(8,128)(2,1)} %get-tuple-element.38) | copy-start | bytes 294916
  139.5 22.1 %collective-permute-start.22 = (bf16[576,256]{1,0:T(8,128)(2,1)S(1)}, bf16[576,256]{1,0:T(8,128)(2,1)S(1)}, u32[]{:S(2)}, u32[]{:S(2)}) collective-permute-start(bf16[576,256]{1,0:T(8,128)(2,1)S(1)} %pad_maximum_fusion.1), channel_id=1, source_target_pairs={{0,1},{1,0},{2,3},{3,2},{4,5},{5,4},{6,7},{7,6},{8,9},{9,8},{10,11... | collective-permute-start | bytes 884744 | tf_op jit(solution)/shard_map/ppermute | solution.py:107
  143.2 51.0 %collective-permute-start.18 = (bf16[256,256]{1,0:T(8,128)(2,1)}, bf16[256,256]{1,0:T(8,128)(2,1)}, u32[]{:S(2)}, u32[]{:S(2)}) collective-permute-start(bf16[256,256]{1,0:T(8,128)(2,1)} %slice.322), channel_id=1, source_target_pairs={{0,1},{1,0},{2,3},{3,2},{4,5},{5,4},{6,7},{7,6},{8,9},{9,8},{10,11... | collective-permute-start | bytes 393224 | tf_op jit(solution)/shard_map/ppermute | solution.py:97
  146.9 10.5 %collective-permute-start.17 = (bf16[256,512]{1,0:T(8,128)(2,1)S(1)}, bf16[256,512]{1,0:T(8,128)(2,1)S(1)}, u32[]{:S(2)}, u32[]{:S(2)}) collective-permute-start(bf16[256,512]{1,0:T(8,128)(2,1)S(1)} %slice.319), channel_id=1, source_target_pairs={{0,1},{1,0},{2,3},{3,2},{4,5},{5,4},{6,7},{7,6},{8,9},{9,8},{10,11... | collective-permute-start | bytes 786440 | tf_op jit(solution)/shard_map/ppermute | solution.py:97
  157.5 6.4 %copy-start.1 = (f32[256,512]{1,0:T(8,128)}, f32[256,512]{1,0:T(8,128)S(1)}, u32[]{:S(2)}) copy-start(f32[256,512]{1,0:T(8,128)S(1)} %slice_add_fusion) | copy-start | bytes 1572868
  157.5 5.6 %copy-start.12 = (bf16[1,192,256]{2,1,0:T(8,128)(2,1)S(1)}, bf16[1,192,256]{2,1,0:T(8,128)(2,1)}, u32[]{:S(2)}) copy-start(bf16[1,192,256]{2,1,0:T(8,128)(2,1)} %get-tuple-element.32) | copy-start | bytes 294916
  157.6 6.3 %copy-start.10 = (bf16[1,192,256]{2,1,0:T(8,128)(2,1)S(1)}, bf16[1,192,256]{2,1,0:T(8,128)(2,1)}, u32[]{:S(2)}) copy-start(bf16[1,192,256]{2,1,0:T(8,128)(2,1)} %get-tuple-element.30) | copy-start | bytes 294916
  157.7 6.9 %copy-start.9 = (bf16[1,192,256]{2,1,0:T(8,128)(2,1)S(1)}, bf16[1,192,256]{2,1,0:T(8,128)(2,1)}, u32[]{:S(2)}) copy-start(bf16[1,192,256]{2,1,0:T(8,128)(2,1)} %get-tuple-element.28) | copy-start | bytes 294916
  157.9 7.9 %copy-start.22 = (f32[2,1]{0,1:T(1,128)S(1)}, f32[2,1]{0,1:T(1,128)}, u32[]{:S(2)}) copy-start(f32[2,1]{0,1:T(1,128)} %copy-done.21) | copy-start | bytes 28
  157.9 8.2 %copy-start.26 = (f32[2]{0:T(128)S(1)}, f32[2]{0:T(128)}, u32[]{:S(2)}) copy-start(f32[2]{0:T(128)} %bitcast_exponential_fusion) | copy-start | bytes 28
  157.9 7.7 %collective-permute-start.19 = (bf16[272,128]{1,0:T(8,128)(2,1)S(1)}, bf16[272,128]{1,0:T(8,128)(2,1)S(1)}, u32[]{:S(2)}, u32[]{:S(2)}) collective-permute-start(bf16[272,128]{1,0:T(8,128)(2,1)S(1)} %fusion.147), channel_id=1, source_target_pairs={{0,1},{1,0},{2,3},{3,2},{4,5},{5,4},{6,7},{7,6},{8,9},{9,8},{10,11... | collective-permute-start | bytes 208904 | tf_op jit(solution)/shard_map/ppermute | solution.py:28
  161.6 11.5 %copy-start.7 = (bf16[1,192,256]{2,1,0:T(8,128)(2,1)S(1)}, bf16[1,192,256]{2,1,0:T(8,128)(2,1)}, u32[]{:S(2)}) copy-start(bf16[1,192,256]{2,1,0:T(8,128)(2,1)} %get-tuple-element.26) | copy-start | bytes 294916
  162.4 11.5 %copy-start.6 = (bf16[1,192,256]{2,1,0:T(8,128)(2,1)S(1)}, bf16[1,192,256]{2,1,0:T(8,128)(2,1)}, u32[]{:S(2)}) copy-start(bf16[1,192,256]{2,1,0:T(8,128)(2,1)} %get-tuple-element.24) | copy-start | bytes 294916
  162.4 11.5 %copy-start.17 = (bf16[1,192,256]{2,1,0:T(8,128)(2,1)S(1)}, bf16[1,192,256]{2,1,0:T(8,128)(2,1)}, u32[]{:S(2)}) copy-start(bf16[1,192,256]{2,1,0:T(8,128)(2,1)} %get-tuple-element.9) | copy-start | bytes 294916
  163.1 11.5 %copy-start.5 = (bf16[1,192,256]{2,1,0:T(8,128)(2,1)S(1)}, bf16[1,192,256]{2,1,0:T(8,128)(2,1)}, u32[]{:S(2)}) copy-start(bf16[1,192,256]{2,1,0:T(8,128)(2,1)} %get-tuple-element.22) | copy-start | bytes 294916
  163.1 11.5 %copy-start.16 = (bf16[1,192,256]{2,1,0:T(8,128)(2,1)S(1)}, bf16[1,192,256]{2,1,0:T(8,128)(2,1)}, u32[]{:S(2)}) copy-start(bf16[1,192,256]{2,1,0:T(8,128)(2,1)} %get-tuple-element.8) | copy-start | bytes 294916
  163.9 11.5 %copy-start.4 = (bf16[1,192,256]{2,1,0:T(8,128)(2,1)S(1)}, bf16[1,192,256]{2,1,0:T(8,128)(2,1)}, u32[]{:S(2)}) copy-start(bf16[1,192,256]{2,1,0:T(8,128)(2,1)} %get-tuple-element.20) | copy-start | bytes 294916
  163.9 11.5 %copy-start.15 = (bf16[1,192,256]{2,1,0:T(8,128)(2,1)S(1)}, bf16[1,192,256]{2,1,0:T(8,128)(2,1)}, u32[]{:S(2)}) copy-start(bf16[1,192,256]{2,1,0:T(8,128)(2,1)} %get-tuple-element.7) | copy-start | bytes 294916
  166.8 19.4 %all-to-all-start = ((bf16[16,24,128]{2,1,0:T(8,128)(2,1)}), bf16[16,24,128]{2,1,0:T(8,128)(2,1)S(1)}, u32[]{:S(2)}, u32[]{:S(2)}) async-start(bf16[16,24,128]{2,1,0:T(8,128)(2,1)} %fusion.146), calls=%async_computation | async-start | bytes 196608 | tf_op jit(solution)/shard_map/all_to_all | solution.py:41
  187.4 16.2 %all-to-all-start.1 = ((bf16[16,16,128]{2,1,0:T(8,128)(2,1)}), bf16[16,16,128]{2,1,0:T(8,128)(2,1)S(1)}, u32[]{:S(2)}, u32[]{:S(2)}) async-start(bf16[16,16,128]{2,1,0:T(8,128)(2,1)} %bitcast.100), calls=%async_computation.1 | async-start | bytes 131072 | tf_op jit(solution)/shard_map/all_to_all | solution.py:50
  193.0 10.6 %copy-start.24 = (f32[256,2]{0,1:T(2,128)S(1)}, f32[256,2]{0,1:T(2,128)}, u32[]{:S(2)}) copy-start(f32[256,2]{0,1:T(2,128)} %get-tuple-element.57) | copy-start | bytes 6148
  194.1 11.5 %copy-start.18 = (pred[256,256]{1,0:T(8,128)(4,1)S(1)}, pred[256,256]{1,0:T(8,128)(4,1)}, u32[]{:S(2)}) copy-start(pred[256,256]{1,0:T(8,128)(4,1)} %iota_compare_fusion) | copy-start | bytes 196612
  194.2 11.5 %copy-start.20 = (f32[1,2,2,128]{3,1,2,0:T(2,128)S(1)}, f32[1,2,2,128]{3,1,2,0:T(2,128)}, u32[]{:S(2)}) copy-start(f32[1,2,2,128]{3,1,2,0:T(2,128)} %copy-done.19) | copy-start | bytes 6148
  211.0 5.6 %collective-permute-start.23 = (bf16[8,256,384]{2,1,0:T(8,128)(2,1)}, bf16[8,256,384]{2,1,0:T(8,128)(2,1)}, u32[]{:S(2)}, u32[]{:S(2)}) collective-permute-start(bf16[8,256,384]{2,1,0:T(8,128)(2,1)} %convolution_convert_fusion.1), channel_id=1, source_target_pairs={{0,32},{32,0},{64,96},{96,64},{128,160},{160,128},{192,224},{224,1... | collective-permute-start | bytes 4718600 | tf_op jit(solution)/shard_map/ppermute | solution.py:144
  (6 other events, 15.7 us)
where the time goes:
time: 248 us; the launch traced here: 246 us
  starting transfers between devices  98.2 us (40%)
  waiting for transfers between devices  49.6 us (20%)
  local copies, waits for them, and re-layouts  30.8 us (12%)
  blocking collectives  26.5 us (11%)
  other arithmetic  21.3 us (9%)
  matrix products  19 us (8%)
    ppermute x7, starting transfers between devices, layer(): behind = lax.ppermute(behind, 'seq', down)  39.8 us
    all_to_all x1, blocking collectives, layer(): lax.all_to_all(keep.astype(jnp.bfloat16), 'dp', 0, 0, axis_index_groups=g...  26.5 us
    ppermute x7, starting transfers between devices, layer(): ahead = lax.ppermute(ahead, 'seq', up)  15.4 us
    ppermute x7, waiting for transfers between devices, layer(): behind = lax.ppermute(behind, 'seq', down)  12.5 us
    ppermute x3, starting transfers between devices, layer(): swapped = lax.ppermute(joined, 'seq', flip)  12.2 us
    unnamed x16, other arithmetic  11.2 us
    another operation x16, local copies, waits for them, and re-layouts, layer(): jnp.stack([pieces[o][:, 3 * width:], other_outs[o], pieces[o][:, 3 * widt...  10.8 us
    dot_general x16, matrix products, times(): lax.dot_general(tok, weight, (((0,), (0,)), ((), ())), preferred_element_...  10.3 us
  transfers between devices with their start and end apart: 26, of which 11 were waited for; matrix products, arithmetic and copies ran while one was open for 23% of the time, Pallas kernels for 0%

commit v1 on v0

v1 whole, which is shorter than its diff:
```python
import jax
import jax.numpy as jnp
from jax import lax
from jax.sharding import PartitionSpec as P


def ring_perm(n, step):
    return [(s, (s + step) % n) for s in range(n)]


def pair_perm(n):
    return [(s, s ^ 1) for s in range(n)]


def exclusive_state(local, log_fall, n):
    heads, hsize, _ = local.shape
    rows = heads * hsize * hsize // (n * 128)
    pieces = local.astype(jnp.bfloat16).reshape(n, rows, 128)
    high = lax.reduce_precision(log_fall, 8, 7)
    middle = lax.reduce_precision(log_fall - high, 8, 7)
    low = lax.reduce_precision(log_fall - high - middle, 8, 7)
    falls = jnp.stack([high, middle, low], axis=1)
    falls = jnp.repeat(falls, n // heads, axis=0).astype(jnp.bfloat16)
    falls = jnp.pad(falls[:, None, :], ((0, 0), (0, rows - 1), (0, 128 - 3)))
    sent = jnp.concatenate([pieces, falls], axis=1)
    got = lax.all_to_all(sent, "seq", 0, 0, tiled=True)
    fall_of = jnp.sum(got[:, rows, :3].astype(jnp.float32), axis=1)
    at = jnp.arange(n)
    between = (at[None, None, :] > at[None, :, None]) & (at[None, None, :] < at[:, None, None])
    total = jnp.sum(jnp.where(between, fall_of[None, None, :], 0.0), axis=2)
    mix = jnp.where(at[None, :] < at[:, None], jnp.exp(total), 0.0)
    slices = got[:, :rows, :].reshape(n, rows * 128).astype(jnp.float32)
    earlier = jnp.dot(mix, slices, precision=lax.Precision.HIGHEST)
    earlier = earlier.astype(jnp.bfloat16).reshape(n, rows, 128)
    back = lax.all_to_all(earlier, "seq", 0, 0, tiled=True)
    return back.reshape(heads, hsize, hsize)


def make_body(n_seq, n_dp):
    n_z = n_seq // 2
    up, down, flip = ring_perm(n_seq, 2), ring_perm(n_seq, -2), pair_perm(n_seq)

    def layer(tokens, qkv_weight, out_weight, log_decay, norm_gain):
        rows, _ = tokens.shape
        width = qkv_weight.shape[2]
        heads = log_decay.shape[0]
        hsize = width // heads
        shard = qkv_weight.shape[0]
        place = lax.axis_index("seq")
        z, half = place // 2, place % 2
        core = lax.axis_index("dp") % 2
        f32 = jnp.float32

        parts = jnp.transpose(qkv_weight, (1, 0, 2))
        own = jnp.concatenate([parts[1], parts[2], parts[0], out_weight], axis=1)
        pieces = {0: own}
        last = n_z // 2
        ahead = behind = own
        for k in range(1, last):
            ahead = lax.ppermute(ahead, "seq", up)
            behind = lax.ppermute(behind, "seq", down)
            pieces[-k], pieces[k] = ahead, behind
        top = lax.ppermute(ahead[: shard // 2], "seq", up)
        bottom = lax.ppermute(behind[shard // 2 :], "seq", down)
        pieces[last] = jnp.concatenate([top, bottom], axis=0)

        by_z = tokens.T.reshape(n_z, 2, shard, rows)
        by_z, _ = lax.optimization_barrier((by_z, pieces[-1]))
        by_z = jnp.concatenate([by_z, by_z], axis=0)
        by_z = lax.dynamic_slice_in_dim(by_z, (z + last) % n_z, n_z, axis=0)
        mine = lax.dynamic_index_in_dim(by_z, half, 1, False)
        theirs = lax.dynamic_index_in_dim(by_z, 1 - half, 1, False)
        theirs = lax.ppermute(theirs, "seq", flip)

        inner, outer = last // 2, last - 2
        groups = [
            list(range(-inner, inner + 1)),
            list(range(-outer, -inner)) + list(range(inner + 1, outer + 1)),
            [1 - last, last - 1, last],
        ]

        def times(toks, weight, group):
            tok = jnp.concatenate([toks[(o + last) % n_z] for o in group], axis=0)
            return lax.dot_general(tok, weight, (((0,), (0,)), ((), ())), preferred_element_type=f32)

        def join(partial, keep):
            sent = lax.ppermute(partial.astype(jnp.bfloat16), "seq", flip)
            return keep + sent.astype(f32)

        columns = 3 * width
        mine_sum = theirs_sum = None
        for group in groups[:2]:
            weight = jnp.concatenate([pieces[o][:, :columns] for o in group], axis=0)
            part = times(mine, weight, group)
            mine_sum = part if mine_sum is None else mine_sum + part
            part = times(theirs, weight, group)
            theirs_sum = part if theirs_sum is None else theirs_sum + part
        final = jnp.concatenate([pieces[o] for o in groups[2]], axis=0)
        kv_cols, q_cols = slice(0, 2 * width), slice(2 * width, columns)
        away = theirs_sum[:, kv_cols] + times(theirs, final[:, kv_cols], groups[2])
        kv_proj = join(away, mine_sum[:, kv_cols] + times(mine, final[:, kv_cols], groups[2]))
        away = theirs_sum[:, q_cols] + times(theirs, final[:, q_cols], groups[2])
        q_proj = join(away, mine_sum[:, q_cols] + times(mine, final[:, q_cols], groups[2]))

        other_outs = {}
        for batch in groups:
            joined = jnp.concatenate([pieces[o][:, 3 * width :] for o in batch], axis=0)
            swapped = lax.ppermute(joined, "seq", flip)
            for i, o in enumerate(batch):
                other_outs[o] = swapped[i * shard : (i + 1) * shard]
        key = jax.nn.silu(kv_proj[:, :width]).astype(jnp.bfloat16).reshape(rows, heads, hsize)
        value = kv_proj[:, width:].astype(jnp.bfloat16).reshape(rows, heads, hsize)
        query = jax.nn.silu(q_proj).astype(jnp.bfloat16).reshape(rows, heads, hsize)
        cum = jnp.cumsum(log_decay, axis=1)
        scaled_key = (key.astype(f32) * jnp.exp(cum[:, -1:] - cum).T[:, :, None]).astype(jnp.bfloat16)
        local = jnp.einsum("thd,the->hde", scaled_key, value, preferred_element_type=f32)
        in_order = list(range(0, last + 1)) + list(range(-last + 1, 0))
        own_outs = {o: pieces[o][:, 3 * width :] for o in in_order}
        (own_outs, other_outs), _ = lax.optimization_barrier(((own_outs, other_outs), local))
        outs = jnp.stack(
            [
                jnp.stack([own_outs[o], other_outs[o], own_outs[o]])
                for o in in_order
            ]
        )
        outs = lax.dynamic_slice_in_dim(outs, half, 2, axis=1)
        outs = jnp.roll(outs, z, axis=0).reshape(n_z // 2, 2, 2 * shard, width)
        out_mine = lax.dynamic_index_in_dim(outs, core, 1, False)
        out_theirs = lax.dynamic_index_in_dim(outs, 1 - core, 1, False)

        earlier_state = exclusive_state(local, cum[:, -1], n_seq)

        later = jnp.arange(rows)[:, None] >= jnp.arange(rows)[None, :]
        scores = jnp.einsum("thd,shd->hts", query, key, preferred_element_type=f32)
        spread = cum[:, :, None] - cum[:, None, :]
        factor = jnp.where(later[None], jnp.exp(jnp.minimum(spread, 0.0)), 0.0)
        weights = (scores * factor).astype(jnp.bfloat16)
        intra = jnp.einsum("hts,shd->thd", weights, value, preferred_element_type=f32)
        intra = lax.optimization_barrier(intra)
        carried = jnp.einsum("thd,hde->the", query, earlier_state, preferred_element_type=f32)
        attn = intra + carried * jnp.exp(cum).T[:, :, None]
        power = jnp.mean(attn * attn, axis=-1, keepdims=True)
        gain = norm_gain.reshape(heads, hsize)
        normed = (attn / jnp.sqrt(power + 1e-05) * gain[None]).astype(jnp.bfloat16).reshape(rows, width)

        wide = jnp.broadcast_to(normed[None], (n_dp // 2, rows, width))
        give = jnp.einsum("itg,idg->itd", wide, out_theirs, preferred_element_type=f32)
        taken = lax.ppermute(give.astype(jnp.bfloat16), "dp", pair_perm(n_dp))
        keep = jnp.einsum("itg,idg->itd", wide, out_mine, preferred_element_type=f32)
        keep = keep.astype(jnp.bfloat16).astype(f32) + taken.astype(f32)
        groups = [[2 * i + c for i in range(n_dp // 2)] for c in range(2)]
        spread_out = lax.all_to_all(keep.astype(jnp.bfloat16), "dp", 0, 0, axis_index_groups=groups, tiled=True)
        return jnp.sum(spread_out.astype(f32), axis=0).astype(jnp.bfloat16)

    return layer


def solution(mesh):
    body = make_body(mesh.shape["seq"], mesh.shape["dp"])
    in_specs = (P("seq", None), P("seq", None, "dp"), P("seq", "dp"), P("dp", "seq"), P("dp"))
    return jax.shard_map(body, mesh=mesh, in_specs=in_specs, out_specs=P("seq", "dp"), check_vma=False)
```

time: 248 us -> 236 us (0.952)
  the two profiles are of different devices: /device:TPU:4 before, /device:TPU:1 now
where the time goes in v1:
time: 236 us; the launch traced here: 235 us
  starting transfers between devices  122 us (52%)
  waiting for transfers between devices  34.6 us (15%)
  blocking collectives  24.2 us (10%)
  other arithmetic  21.3 us (9%)
  local copies, waits for them, and re-layouts  18.8 us (8%)
  matrix products  13.2 us (6%)
    ppermute x7, starting transfers between devices, layer(): behind = lax.ppermute(behind, 'seq', down)  38.7 us
    all_to_all x1, blocking collectives, layer(): lax.all_to_all(keep.astype(jnp.bfloat16), 'dp', 0, 0, axis_index_groups=g...  24.2 us
    ppermute x7, starting transfers between devices, layer(): ahead = lax.ppermute(ahead, 'seq', up)  15.8 us
    all_to_all x1, starting transfers between devices, exclusive_state(): back = lax.all_to_all(earlier, 'seq', 0, 0, tiled=True)  14.1 us
    ppermute x1, starting transfers between devices, layer(): taken = lax.ppermute(give.astype(jnp.bfloat16), 'dp', pair_perm(n_dp))  14 us
    unnamed x17, other arithmetic  11.1 us
    unnamed x62, local copies, waits for them, and re-layouts  11 us
    all_to_all x1, starting transfers between devices, exclusive_state(): got = lax.all_to_all(sent, 'seq', 0, 0, tiled=True)  10.7 us
  transfers between devices with their start and end apart: 25, of which 14 were waited for; matrix products, arithmetic and copies ran while one was open for 17% of the time, Pallas kernels for 0%

profile of v1, /device:TPU:1, one launch (start us, length us, event | category | flops | bytes accessed | tf_op | source)
XLA Modules:
  0.0 234.9 jit_solution(3388400794067774617)
XLA Ops:
  0.0 1.0 slice_bitcast_fusion.18
  1.0 1.7 pad_maximum_fusion.1
  2.7 4.4 %collective-permute-start = (bf16[192,1024]{1,0:T(8,128)(2,1)}, bf16[192,1024]{1,0:T(8,128)(2,1)}, u32[]{:S(2)}, u32[]{:S(2)}) collective-permute-start(bf16[192,1024]{1,0:T(8,128)(2,1)} %pad_maximum_fusion.1), channel_id=1, source_target_pairs={{0,2},{1,3},{2,4},{3,5},{4,6},{5,7},{6,8},{7,9},{8,10},{9,11},{10,... | collective-permute-start | bytes 1179656 | tf_op jit(solution)/shard_map/ppermute | solution.py:60
  7.1 9.5 %collective-permute-start.4 = (bf16[192,1024]{1,0:T(8,128)(2,1)}, bf16[192,1024]{1,0:T(8,128)(2,1)}, u32[]{:S(2)}, u32[]{:S(2)}) collective-permute-start(bf16[192,1024]{1,0:T(8,128)(2,1)} %pad_maximum_fusion.1), channel_id=1, source_target_pairs={{0,30},{1,31},{2,0},{3,1},{4,2},{5,3},{6,4},{7,5},{8,6},{9,7},{10,... | collective-permute-start | bytes 1179656 | tf_op jit(solution)/shard_map/ppermute | solution.py:61
  19.8 3.2 %copy.52 = bf16[256,6144]{0,1:T(8,128)(2,1)S(1)} copy(bf16[256,6144]{1,0:T(8,128)(2,1)} %param.5) | data formatting | bytes 6291456 | tf_op args[0]
  24.8 1.9 collective-permute-start.1
  27.1 4.8 %collective-permute-start.16 = (bf16[16,192,256]{2,1,0:T(8,128)(2,1)S(1)}, bf16[16,192,256]{2,1,0:T(8,128)(2,1)S(1)}, u32[]{:S(2)}, u32[]{:S(2)}) collective-permute-start(bf16[16,192,256]{2,1,0:T(8,128)(2,1)S(1)} %dynamic-slice_bitcast_fusion), channel_id=1, source_target_pairs={{0,1},{1,0},{2,3},{3,2},{4,5},{5,4},{6,7},{7,6},{8,9},{9,8},{10,11... | collective-permute-start | bytes 4718600 | tf_op jit(solution)/shard_map/ppermute | solution.py:73
  31.9 4.6 %collective-permute-start.5 = (bf16[192,1024]{1,0:T(8,128)(2,1)}, bf16[192,1024]{1,0:T(8,128)(2,1)S(1)}, u32[]{:S(2)}, u32[]{:S(2)}) collective-permute-start(bf16[192,1024]{1,0:T(8,128)(2,1)} %collective-permute-done.4), channel_id=1, source_target_pairs={{0,30},{1,31},{2,0},{3,1},{4,2},{5,3},{6,4},{7,5},{8,6},{9,7},{10,... | collective-permute-start | bytes 1179656 | tf_op jit(solution)/shard_map/ppermute | solution.py:61
  36.5 1.3 collective-permute-done.1
  37.8 1.9 collective-permute-start.2
  39.8 3.9 %collective-permute-done.5 = bf16[192,1024]{1,0:T(8,128)(2,1)S(1)} collective-permute-done((bf16[192,1024]{1,0:T(8,128)(2,1)}, bf16[192,1024]{1,0:T(8,128)(2,1)S(1)}, u32[]{:S(2)}, u32[]{:S(2)}) %collective-permute-start.5) | collective-permute-done | bytes 393248 | tf_op jit(solution)/shard_map/ppermute | solution.py:61
  43.7 5.2 %collective-permute-start.6 = (bf16[192,1024]{1,0:T(8,128)(2,1)S(1)}, bf16[192,1024]{1,0:T(8,128)(2,1)S(1)}, u32[]{:S(2)}, u32[]{:S(2)}) collective-permute-start(bf16[192,1024]{1,0:T(8,128)(2,1)S(1)} %collective-permute-done.5), channel_id=1, source_target_pairs={{0,30},{1,31},{2,0},{3,1},{4,2},{5,3},{6,4},{7,5},{8,6},{9,7},{10,... | collective-permute-start | bytes 1179656 | tf_op jit(solution)/shard_map/ppermute | solution.py:61
  49.8 1.9 collective-permute-start.3
  51.8 3.1 %collective-permute-done.6 = bf16[192,1024]{1,0:T(8,128)(2,1)S(1)} collective-permute-done((bf16[192,1024]{1,0:T(8,128)(2,1)S(1)}, bf16[192,1024]{1,0:T(8,128)(2,1)S(1)}, u32[]{:S(2)}, u32[]{:S(2)}) %collective-permute-start.6) | collective-permute-done | bytes 393248 | tf_op jit(solution)/shard_map/ppermute | solution.py:61
  55.0 5.3 %collective-permute-start.7 = (bf16[192,1024]{1,0:T(8,128)(2,1)S(1)}, bf16[192,1024]{1,0:T(8,128)(2,1)S(1)}, u32[]{:S(2)}, u32[]{:S(2)}) collective-permute-start(bf16[192,1024]{1,0:T(8,128)(2,1)S(1)} %collective-permute-done.6), channel_id=1, source_target_pairs={{0,30},{1,31},{2,0},{3,1},{4,2},{5,3},{6,4},{7,5},{8,6},{9,7},{10,... | collective-permute-start | bytes 1179656 | tf_op jit(solution)/shard_map/ppermute | solution.py:61
  61.9 1.5 constant_dynamic-update-slice_fusion.27
  66.2 3.8 %collective-permute-start.21 = (bf16[1728,256]{1,0:T(8,128)(2,1)S(1)}, bf16[1728,256]{1,0:T(8,128)(2,1)S(1)}, u32[]{:S(2)}, u32[]{:S(2)}) collective-permute-start(bf16[1728,256]{1,0:T(8,128)(2,1)S(1)} %get-tuple-element.98), channel_id=1, source_target_pairs={{0,1},{1,0},{2,3},{3,2},{4,5},{5,4},{6,7},{7,6},{8,9},{9,8},{10,11... | collective-permute-start | bytes 2654216 | tf_op jit(solution)/shard_map/ppermute | solution.py:108
  70.0 1.9 collective-permute-start.8
  72.0 4.6 %collective-permute-start.10 = (bf16[192,1024]{1,0:T(8,128)(2,1)S(1)}, bf16[192,1024]{1,0:T(8,128)(2,1)S(1)}, u32[]{:S(2)}, u32[]{:S(2)}) collective-permute-start(bf16[192,1024]{1,0:T(8,128)(2,1)S(1)} %collective-permute-done.7), channel_id=1, source_target_pairs={{0,30},{1,31},{2,0},{3,1},{4,2},{5,3},{6,4},{7,5},{8,6},{9,7},{10,... | collective-permute-start | bytes 1179656 | tf_op jit(solution)/shard_map/ppermute | solution.py:61
  80.1 1.9 collective-permute-start.9
  82.0 4.6 %collective-permute-start.11 = (bf16[192,1024]{1,0:T(8,128)(2,1)S(1)}, bf16[192,1024]{1,0:T(8,128)(2,1)S(1)}, u32[]{:S(2)}, u32[]{:S(2)}) collective-permute-start(bf16[192,1024]{1,0:T(8,128)(2,1)S(1)} %collective-permute-done.10), channel_id=1, source_target_pairs={{0,30},{1,31},{2,0},{3,1},{4,2},{5,3},{6,4},{7,5},{8,6},{9,7},{10,... | collective-permute-start | bytes 1179656 | tf_op jit(solution)/shard_map/ppermute | solution.py:61
  87.7 2.4 %collective-permute-done.9 = bf16[192,1024]{1,0:T(8,128)(2,1)S(1)} collective-permute-done((bf16[192,1024]{1,0:T(8,128)(2,1)S(1)}, bf16[192,1024]{1,0:T(8,128)(2,1)S(1)}, u32[]{:S(2)}, u32[]{:S(2)}) %collective-permute-start.9) | collective-permute-done | bytes 393248 | tf_op jit(solution)/shard_map/ppermute | solution.py:60
  90.1 1.2 collective-permute-done.11
  91.4 3.5 %collective-permute-start.20 = (bf16[768,256]{1,0:T(8,128)(2,1)S(1)}, bf16[768,256]{1,0:T(8,128)(2,1)S(1)}, u32[]{:S(2)}, u32[]{:S(2)}) collective-permute-start(bf16[768,256]{1,0:T(8,128)(2,1)S(1)} %pad_maximum_fusion.2), channel_id=1, source_target_pairs={{0,1},{1,0},{2,3},{3,2},{4,5},{5,4},{6,7},{7,6},{8,9},{9,8},{10,11... | collective-permute-start | bytes 1179656 | tf_op jit(solution)/shard_map/ppermute | solution.py:108
  95.0 1.9 collective-permute-start.12
  96.9 5.0 %collective-permute-start.13 = (bf16[192,1024]{1,0:T(8,128)(2,1)S(1)}, bf16[192,1024]{1,0:T(8,128)(2,1)S(1)}, u32[]{:S(2)}, u32[]{:S(2)}) collective-permute-start(bf16[192,1024]{1,0:T(8,128)(2,1)S(1)} %collective-permute-done.11), channel_id=1, source_target_pairs={{0,30},{1,31},{2,0},{3,1},{4,2},{5,3},{6,4},{7,5},{8,6},{9,7},{10,... | collective-permute-start | bytes 1179656 | tf_op jit(solution)/shard_map/ppermute | solution.py:61
  103.1 2.4 %collective-permute-done.12 = bf16[192,1024]{1,0:T(8,128)(2,1)S(1)} collective-permute-done((bf16[192,1024]{1,0:T(8,128)(2,1)S(1)}, bf16[192,1024]{1,0:T(8,128)(2,1)S(1)}, u32[]{:S(2)}, u32[]{:S(2)}) %collective-permute-start.12) | collective-permute-done | bytes 393248 | tf_op jit(solution)/shard_map/ppermute | solution.py:60
  105.5 1.9 collective-permute-start.14
  107.4 4.6 %collective-permute-start.15 = (bf16[96,1024]{1,0:T(8,128)(2,1)S(1)}, bf16[96,1024]{1,0:T(8,128)(2,1)S(1)}, u32[]{:S(2)}, u32[]{:S(2)}) collective-permute-start(bf16[96,1024]{1,0:T(8,128)(2,1)S(1)} %slice.432), channel_id=1, source_target_pairs={{0,30},{1,31},{2,0},{3,1},{4,2},{5,3},{6,4},{7,5},{8,6},{9,7},{10,... | collective-permute-start | bytes 589832 | tf_op jit(solution)/shard_map/ppermute | solution.py:64
  112.2 2.1 collective-permute-done.14
  114.3 1.7 collective-permute-done.15
  116.7 2.8 %collective-permute-start.17 = (bf16[256,512]{1,0:T(8,128)(2,1)S(1)}, bf16[256,512]{1,0:T(8,128)(2,1)S(1)}, u32[]{:S(2)}, u32[]{:S(2)}) collective-permute-start(bf16[256,512]{1,0:T(8,128)(2,1)S(1)} %fusion.13), channel_id=1, source_target_pairs={{0,1},{1,0},{2,3},{3,2},{4,5},{5,4},{6,7},{7,6},{8,9},{9,8},{10,11... | collective-permute-start | bytes 786440 | tf_op jit(solution)/shard_map/ppermute | solution.py:87
  119.6 4.0 %collective-permute-start.18 = (bf16[256,256]{1,0:T(8,128)(2,1)S(1)}, bf16[256,256]{1,0:T(8,128)(2,1)S(1)}, u32[]{:S(2)}, u32[]{:S(2)}) collective-permute-start(bf16[256,256]{1,0:T(8,128)(2,1)S(1)} %fusion.59), channel_id=1, source_target_pairs={{0,1},{1,0},{2,3},{3,2},{4,5},{5,4},{6,7},{7,6},{8,9},{9,8},{10,11... | collective-permute-start | bytes 393224 | tf_op jit(solution)/shard_map/ppermute | solution.py:87
  124.3 2.8 %collective-permute-start.19 = (bf16[576,256]{1,0:T(8,128)(2,1)}, bf16[576,256]{1,0:T(8,128)(2,1)}, u32[]{:S(2)}, u32[]{:S(2)}) collective-permute-start(bf16[576,256]{1,0:T(8,128)(2,1)} %pad_maximum_fusion.5), channel_id=1, source_target_pairs={{0,1},{1,0},{2,3},{3,2},{4,5},{5,4},{6,7},{7,6},{8,9},{9,8},{10,11... | collective-permute-start | bytes 884744 | tf_op jit(solution)/shard_map/ppermute | solution.py:108
  130.3 10.7 %all-to-all-start = ((bf16[32,16,128]{2,1,0:T(8,128)(2,1)}), bf16[32,16,128]{2,1,0:T(8,128)(2,1)}, u32[]{:S(2)}, u32[]{:S(2)}) async-start(bf16[32,16,128]{2,1,0:T(8,128)(2,1)} %fusion.77), calls=%async_computation | async-start | bytes 262144 | tf_op jit(solution)/shard_map/all_to_all | solution.py:26
  141.1 2.0 fusion.9
  143.1 1.0 fusion.111
  155.8 1.2 fusion.93
  158.9 14.1 %all-to-all-start.1 = ((bf16[32,8,128]{2,1,0:T(8,128)(2,1)}), bf16[32,8,128]{2,1,0:T(8,128)(2,1)S(1)}, u32[]{:S(2)}, u32[]{:S(2)}) async-start(bf16[32,8,128]{2,1,0:T(8,128)(2,1)} %bitcast.111), calls=%async_computation.1 | async-start | bytes 131072 | tf_op jit(solution)/shard_map/all_to_all | solution.py:35
  173.0 2.1 constant_dynamic-slice_fusion
  175.2 1.1 fusion
  176.3 10.6 %all-to-all-done.1 = bf16[32,8,128]{2,1,0:T(8,128)(2,1)S(1)} async-done(((bf16[32,8,128]{2,1,0:T(8,128)(2,1)}), bf16[32,8,128]{2,1,0:T(8,128)(2,1)S(1)}, u32[]{:S(2)}, u32[]{:S(2)}) %all-to-all-start.1) | async-done | bytes 65568 | tf_op jit(solution)/shard_map/all_to_all | solution.py:35
  186.9 1.1 multiply_reduce_fusion
  188.3 1.9 convolution_convert_fusion
  190.2 14.0 %collective-permute-start.22 = (bf16[8,256,384]{2,1,0:T(8,128)(2,1)}, bf16[8,256,384]{2,1,0:T(8,128)(2,1)}, u32[]{:S(2)}, u32[]{:S(2)}) collective-permute-start(bf16[8,256,384]{2,1,0:T(8,128)(2,1)} %convolution_convert_fusion), channel_id=1, source_target_pairs={{0,32},{32,0},{64,96},{96,64},{128,160},{160,128},{192,224},{224,1... | collective-permute-start | bytes 4718600 | tf_op jit(solution)/shard_map/ppermute | solution.py:148
  204.3 3.3 %collective-permute-done.22 = bf16[8,256,384]{2,1,0:T(8,128)(2,1)} collective-permute-done((bf16[8,256,384]{2,1,0:T(8,128)(2,1)}, bf16[8,256,384]{2,1,0:T(8,128)(2,1)}, u32[]{:S(2)}, u32[]{:S(2)}) %collective-permute-start.22) | collective-permute-done | bytes 1572896 | tf_op jit(solution)/shard_map/ppermute | solution.py:148
  207.6 2.1 add_convert_fusion
  209.8 24.2 %all_to_all.15 = bf16[8,256,384]{2,1,0:T(8,128)(2,1)S(1)} all-to-all(bf16[8,256,384]{2,1,0:T(8,128)(2,1)S(1)} %add_convert_fusion), channel_id=1, replica_groups={{0,64,128,192,256,320,384,448},{32,96,160,224,288,352,416,480},{1,65,12..., dimensions={0} | all-to-all | bytes 3145728 | tf_op jit(solution)/shard_map/all_to_all | solution.py:152
  (150 shorter events, 35.9 us)
Async XLA Ops:
  2.7 21.8 %collective-permute-start = (bf16[192,1024]{1,0:T(8,128)(2,1)}, bf16[192,1024]{1,0:T(8,128)(2,1)}, u32[]{:S(2)}, u32[]{:S(2)}) collective-permute-start(bf16[192,1024]{1,0:T(8,128)(2,1)} %pad_maximum_fusion.1), channel_id=1, source_target_pairs={{0,2},{1,3},{2,4},{3,5},{4,6},{5,7},{6,8},{7,9},{8,10},{9,11},{10,... | collective-permute-start | bytes 1179656 | tf_op jit(solution)/shard_map/ppermute | solution.py:60
  7.1 24.8 %collective-permute-start.4 = (bf16[192,1024]{1,0:T(8,128)(2,1)}, bf16[192,1024]{1,0:T(8,128)(2,1)}, u32[]{:S(2)}, u32[]{:S(2)}) collective-permute-start(bf16[192,1024]{1,0:T(8,128)(2,1)} %pad_maximum_fusion.1), channel_id=1, source_target_pairs={{0,30},{1,31},{2,0},{3,1},{4,2},{5,3},{6,4},{7,5},{8,6},{9,7},{10,... | collective-permute-start | bytes 1179656 | tf_op jit(solution)/shard_map/ppermute | solution.py:61
  18.9 0.6 copy-start.9
  24.8 13.0 %collective-permute-start.1 = (bf16[192,1024]{1,0:T(8,128)(2,1)}, bf16[192,1024]{1,0:T(8,128)(2,1)S(1)}, u32[]{:S(2)}, u32[]{:S(2)}) collective-permute-start(bf16[192,1024]{1,0:T(8,128)(2,1)} %collective-permute-done), channel_id=1, source_target_pairs={{0,2},{1,3},{2,4},{3,5},{4,6},{5,7},{6,8},{7,9},{8,10},{9,11},{10,... | collective-permute-start | bytes 1179656 | tf_op jit(solution)/shard_map/ppermute | solution.py:60
  27.0 34.8 %copy-start = (bf16[192,256]{1,0:T(8,128)(2,1)S(1)}, bf16[192,256]{1,0:T(8,128)(2,1)}, u32[]{:S(2)}) copy-start(bf16[192,256]{1,0:T(8,128)(2,1)} %param.7) | copy-start | bytes 294916
  27.1 52.6 %collective-permute-start.16 = (bf16[16,192,256]{2,1,0:T(8,128)(2,1)S(1)}, bf16[16,192,256]{2,1,0:T(8,128)(2,1)S(1)}, u32[]{:S(2)}, u32[]{:S(2)}) collective-permute-start(bf16[16,192,256]{2,1,0:T(8,128)(2,1)S(1)} %dynamic-slice_bitcast_fusion), channel_id=1, source_target_pairs={{0,1},{1,0},{2,3},{3,2},{4,5},{5,4},{6,7},{7,6},{8,9},{9,8},{10,11... | collective-permute-start | bytes 4718600 | tf_op jit(solution)/shard_map/ppermute | solution.py:73
  31.9 11.8 %collective-permute-start.5 = (bf16[192,1024]{1,0:T(8,128)(2,1)}, bf16[192,1024]{1,0:T(8,128)(2,1)S(1)}, u32[]{:S(2)}, u32[]{:S(2)}) collective-permute-start(bf16[192,1024]{1,0:T(8,128)(2,1)} %collective-permute-done.4), channel_id=1, source_target_pairs={{0,30},{1,31},{2,0},{3,1},{4,2},{5,3},{6,4},{7,5},{8,6},{9,7},{10,... | collective-permute-start | bytes 1179656 | tf_op jit(solution)/shard_map/ppermute | solution.py:61
  37.8 12.0 %collective-permute-start.2 = (bf16[192,1024]{1,0:T(8,128)(2,1)S(1)}, bf16[192,1024]{1,0:T(8,128)(2,1)S(1)}, u32[]{:S(2)}, u32[]{:S(2)}) collective-permute-start(bf16[192,1024]{1,0:T(8,128)(2,1)S(1)} %collective-permute-done.1), channel_id=1, source_target_pairs={{0,2},{1,3},{2,4},{3,5},{4,6},{5,7},{6,8},{7,9},{8,10},{9,11},{10,... | collective-permute-start | bytes 1179656 | tf_op jit(solution)/shard_map/ppermute | solution.py:60
  43.7 11.3 %collective-permute-start.6 = (bf16[192,1024]{1,0:T(8,128)(2,1)S(1)}, bf16[192,1024]{1,0:T(8,128)(2,1)S(1)}, u32[]{:S(2)}, u32[]{:S(2)}) collective-permute-start(bf16[192,1024]{1,0:T(8,128)(2,1)S(1)} %collective-permute-done.5), channel_id=1, source_target_pairs={{0,30},{1,31},{2,0},{3,1},{4,2},{5,3},{6,4},{7,5},{8,6},{9,7},{10,... | collective-permute-start | bytes 1179656 | tf_op jit(solution)/shard_map/ppermute | solution.py:61
  49.8 11.1 %collective-permute-start.3 = (bf16[192,1024]{1,0:T(8,128)(2,1)S(1)}, bf16[192,1024]{1,0:T(8,128)(2,1)S(1)}, u32[]{:S(2)}, u32[]{:S(2)}) collective-permute-start(bf16[192,1024]{1,0:T(8,128)(2,1)S(1)} %collective-permute-done.2), channel_id=1, source_target_pairs={{0,2},{1,3},{2,4},{3,5},{4,6},{5,7},{6,8},{7,9},{8,10},{9,11},{10,... | collective-permute-start | bytes 1179656 | tf_op jit(solution)/shard_map/ppermute | solution.py:60
  55.0 10.5 %collective-permute-start.7 = (bf16[192,1024]{1,0:T(8,128)(2,1)S(1)}, bf16[192,1024]{1,0:T(8,128)(2,1)S(1)}, u32[]{:S(2)}, u32[]{:S(2)}) collective-permute-start(bf16[192,1024]{1,0:T(8,128)(2,1)S(1)} %collective-permute-done.6), channel_id=1, source_target_pairs={{0,30},{1,31},{2,0},{3,1},{4,2},{5,3},{6,4},{7,5},{8,6},{9,7},{10,... | collective-permute-start | bytes 1179656 | tf_op jit(solution)/shard_map/ppermute | solution.py:61
  66.2 36.8 %collective-permute-start.21 = (bf16[1728,256]{1,0:T(8,128)(2,1)S(1)}, bf16[1728,256]{1,0:T(8,128)(2,1)S(1)}, u32[]{:S(2)}, u32[]{:S(2)}) collective-permute-start(bf16[1728,256]{1,0:T(8,128)(2,1)S(1)} %get-tuple-element.98), channel_id=1, source_target_pairs={{0,1},{1,0},{2,3},{3,2},{4,5},{5,4},{6,7},{7,6},{8,9},{9,8},{10,11... | collective-permute-start | bytes 2654216 | tf_op jit(solution)/shard_map/ppermute | solution.py:108
  70.0 10.0 %collective-permute-start.8 = (bf16[192,1024]{1,0:T(8,128)(2,1)S(1)}, bf16[192,1024]{1,0:T(8,128)(2,1)S(1)}, u32[]{:S(2)}, u32[]{:S(2)}) collective-permute-start(bf16[192,1024]{1,0:T(8,128)(2,1)S(1)} %collective-permute-done.3), channel_id=1, source_target_pairs={{0,2},{1,3},{2,4},{3,5},{4,6},{5,7},{6,8},{7,9},{8,10},{9,11},{10,... | collective-permute-start | bytes 1179656 | tf_op jit(solution)/shard_map/ppermute | solution.py:60
  72.0 10.1 %collective-permute-start.10 = (bf16[192,1024]{1,0:T(8,128)(2,1)S(1)}, bf16[192,1024]{1,0:T(8,128)(2,1)S(1)}, u32[]{:S(2)}, u32[]{:S(2)}) collective-permute-start(bf16[192,1024]{1,0:T(8,128)(2,1)S(1)} %collective-permute-done.7), channel_id=1, source_target_pairs={{0,30},{1,31},{2,0},{3,1},{4,2},{5,3},{6,4},{7,5},{8,6},{9,7},{10,... | collective-permute-start | bytes 1179656 | tf_op jit(solution)/shard_map/ppermute | solution.py:61
  80.1 10.0 %collective-permute-start.9 = (bf16[192,1024]{1,0:T(8,128)(2,1)S(1)}, bf16[192,1024]{1,0:T(8,128)(2,1)S(1)}, u32[]{:S(2)}, u32[]{:S(2)}) collective-permute-start(bf16[192,1024]{1,0:T(8,128)(2,1)S(1)} %collective-permute-done.8), channel_id=1, source_target_pairs={{0,2},{1,3},{2,4},{3,5},{4,6},{5,7},{6,8},{7,9},{8,10},{9,11},{10,... | collective-permute-start | bytes 1179656 | tf_op jit(solution)/shard_map/ppermute | solution.py:60
  82.0 9.3 %collective-permute-start.11 = (bf16[192,1024]{1,0:T(8,128)(2,1)S(1)}, bf16[192,1024]{1,0:T(8,128)(2,1)S(1)}, u32[]{:S(2)}, u32[]{:S(2)}) collective-permute-start(bf16[192,1024]{1,0:T(8,128)(2,1)S(1)} %collective-permute-done.10), channel_id=1, source_target_pairs={{0,30},{1,31},{2,0},{3,1},{4,2},{5,3},{6,4},{7,5},{8,6},{9,7},{10,... | collective-permute-start | bytes 1179656 | tf_op jit(solution)/shard_map/ppermute | solution.py:61
  91.4 20.7 %collective-permute-start.20 = (bf16[768,256]{1,0:T(8,128)(2,1)S(1)}, bf16[768,256]{1,0:T(8,128)(2,1)S(1)}, u32[]{:S(2)}, u32[]{:S(2)}) collective-permute-start(bf16[768,256]{1,0:T(8,128)(2,1)S(1)} %pad_maximum_fusion.2), channel_id=1, source_target_pairs={{0,1},{1,0},{2,3},{3,2},{4,5},{5,4},{6,7},{7,6},{8,9},{9,8},{10,11... | collective-permute-start | bytes 1179656 | tf_op jit(solution)/shard_map/ppermute | solution.py:108
  95.0 10.5 %collective-permute-start.12 = (bf16[192,1024]{1,0:T(8,128)(2,1)S(1)}, bf16[192,1024]{1,0:T(8,128)(2,1)S(1)}, u32[]{:S(2)}, u32[]{:S(2)}) collective-permute-start(bf16[192,1024]{1,0:T(8,128)(2,1)S(1)} %collective-permute-done.9), channel_id=1, source_target_pairs={{0,2},{1,3},{2,4},{3,5},{4,6},{5,7},{6,8},{7,9},{8,10},{9,11},{10,... | collective-permute-start | bytes 1179656 | tf_op jit(solution)/shard_map/ppermute | solution.py:60
  96.9 10.5 %collective-permute-start.13 = (bf16[192,1024]{1,0:T(8,128)(2,1)S(1)}, bf16[192,1024]{1,0:T(8,128)(2,1)S(1)}, u32[]{:S(2)}, u32[]{:S(2)}) collective-permute-start(bf16[192,1024]{1,0:T(8,128)(2,1)S(1)} %collective-permute-done.11), channel_id=1, source_target_pairs={{0,30},{1,31},{2,0},{3,1},{4,2},{5,3},{6,4},{7,5},{8,6},{9,7},{10,... | collective-permute-start | bytes 1179656 | tf_op jit(solution)/shard_map/ppermute | solution.py:61
  105.5 8.8 %collective-permute-start.14 = (bf16[96,1024]{1,0:T(8,128)(2,1)S(1)}, bf16[96,1024]{1,0:T(8,128)(2,1)S(1)}, u32[]{:S(2)}, u32[]{:S(2)}) collective-permute-start(bf16[96,1024]{1,0:T(8,128)(2,1)S(1)} %slice.431), channel_id=1, source_target_pairs={{0,2},{1,3},{2,4},{3,5},{4,6},{5,7},{6,8},{7,9},{8,10},{9,11},{10,... | collective-permute-start | bytes 589832 | tf_op jit(solution)/shard_map/ppermute | solution.py:63
  107.4 8.6 %collective-permute-start.15 = (bf16[96,1024]{1,0:T(8,128)(2,1)S(1)}, bf16[96,1024]{1,0:T(8,128)(2,1)S(1)}, u32[]{:S(2)}, u32[]{:S(2)}) collective-permute-start(bf16[96,1024]{1,0:T(8,128)(2,1)S(1)} %slice.432), channel_id=1, source_target_pairs={{0,30},{1,31},{2,0},{3,1},{4,2},{5,3},{6,4},{7,5},{8,6},{9,7},{10,... | collective-permute-start | bytes 589832 | tf_op jit(solution)/shard_map/ppermute | solution.py:64
  116.7 11.4 %collective-permute-start.17 = (bf16[256,512]{1,0:T(8,128)(2,1)S(1)}, bf16[256,512]{1,0:T(8,128)(2,1)S(1)}, u32[]{:S(2)}, u32[]{:S(2)}) collective-permute-start(bf16[256,512]{1,0:T(8,128)(2,1)S(1)} %fusion.13), channel_id=1, source_target_pairs={{0,1},{1,0},{2,3},{3,2},{4,5},{5,4},{6,7},{7,6},{8,9},{9,8},{10,11... | collective-permute-start | bytes 786440 | tf_op jit(solution)/shard_map/ppermute | solution.py:87
  119.6 7.5 %collective-permute-start.18 = (bf16[256,256]{1,0:T(8,128)(2,1)S(1)}, bf16[256,256]{1,0:T(8,128)(2,1)S(1)}, u32[]{:S(2)}, u32[]{:S(2)}) collective-permute-start(bf16[256,256]{1,0:T(8,128)(2,1)S(1)} %fusion.59), channel_id=1, source_target_pairs={{0,1},{1,0},{2,3},{3,2},{4,5},{5,4},{6,7},{7,6},{8,9},{9,8},{10,11... | collective-permute-start | bytes 393224 | tf_op jit(solution)/shard_map/ppermute | solution.py:87
  124.3 18.8 %collective-permute-start.19 = (bf16[576,256]{1,0:T(8,128)(2,1)}, bf16[576,256]{1,0:T(8,128)(2,1)}, u32[]{:S(2)}, u32[]{:S(2)}) collective-permute-start(bf16[576,256]{1,0:T(8,128)(2,1)} %pad_maximum_fusion.5), channel_id=1, source_target_pairs={{0,1},{1,0},{2,3},{3,2},{4,5},{5,4},{6,7},{7,6},{8,9},{9,8},{10,11... | collective-permute-start | bytes 884744 | tf_op jit(solution)/shard_map/ppermute | solution.py:108
  128.5 16.3 %copy-start.1 = (bf16[192,256]{1,0:T(8,128)(2,1)S(1)}, bf16[192,256]{1,0:T(8,128)(2,1)}, u32[]{:S(2)}) copy-start(bf16[192,256]{1,0:T(8,128)(2,1)} %get-tuple-element.41) | copy-start | bytes 294916
  128.5 17.0 %copy-start.2 = (bf16[192,256]{1,0:T(8,128)(2,1)S(1)}, bf16[192,256]{1,0:T(8,128)(2,1)}, u32[]{:S(2)}) copy-start(bf16[192,256]{1,0:T(8,128)(2,1)} %get-tuple-element.43) | copy-start | bytes 294916
  128.6 17.7 %copy-start.3 = (bf16[192,256]{1,0:T(8,128)(2,1)S(1)}, bf16[192,256]{1,0:T(8,128)(2,1)}, u32[]{:S(2)}) copy-start(bf16[192,256]{1,0:T(8,128)(2,1)} %get-tuple-element.45) | copy-start | bytes 294916
  128.8 18.3 %copy-start.4 = (bf16[192,256]{1,0:T(8,128)(2,1)S(1)}, bf16[192,256]{1,0:T(8,128)(2,1)}, u32[]{:S(2)}) copy-start(bf16[192,256]{1,0:T(8,128)(2,1)} %get-tuple-element.47) | copy-start | bytes 294916
  130.3 25.5 %all-to-all-start = ((bf16[32,16,128]{2,1,0:T(8,128)(2,1)}), bf16[32,16,128]{2,1,0:T(8,128)(2,1)}, u32[]{:S(2)}, u32[]{:S(2)}) async-start(bf16[32,16,128]{2,1,0:T(8,128)(2,1)} %fusion.77), calls=%async_computation | async-start | bytes 262144 | tf_op jit(solution)/shard_map/all_to_all | solution.py:26
  147.8 9.3 %copy-start.6 = (pred[32,32]{1,0:T(8,128)(4,1)S(1)}, pred[32,32]{1,0:T(8,128)(4,1)}, u32[]{:S(2)}) copy-start(pred[32,32]{1,0:T(8,128)(4,1)} %get-tuple-element.127) | copy-start | bytes 3076
  147.8 9.3 %copy-start.7 = (pred[32,32]{1,0:T(8,128)(4,1)S(1)}, pred[32,32]{1,0:T(8,128)(4,1)}, u32[]{:S(2)}) copy-start(pred[32,32]{1,0:T(8,128)(4,1)} %get-tuple-element.128) | copy-start | bytes 3076
  158.9 28.0 %all-to-all-start.1 = ((bf16[32,8,128]{2,1,0:T(8,128)(2,1)}), bf16[32,8,128]{2,1,0:T(8,128)(2,1)S(1)}, u32[]{:S(2)}, u32[]{:S(2)}) async-start(bf16[32,8,128]{2,1,0:T(8,128)(2,1)} %bitcast.111), calls=%async_computation.1 | async-start | bytes 131072 | tf_op jit(solution)/shard_map/all_to_all | solution.py:35
  175.2 11.8 %copy-start.5 = (f32[256,2,128]{0,2,1:T(8,128)S(1)}, f32[256,2,128]{0,2,1:T(8,128)}, u32[]{:S(2)}) copy-start(f32[256,2,128]{0,2,1:T(8,128)} %fusion.9) | copy-start | bytes 786436
  175.2 11.8 %copy-start.8 = (f32[256,2]{0,1:T(2,128)S(1)}, f32[256,2]{0,1:T(2,128)}, u32[]{:S(2)}) copy-start(f32[256,2]{0,1:T(2,128)} %get-tuple-element.120) | copy-start | bytes 6148
  175.2 12.9 %copy-start.10 = (f32[256]{0:T(256)S(1)}, f32[256]{0:T(256)}, u32[]{:S(2)}) copy-start(f32[256]{0:T(256)} %param.9) | copy-start | bytes 3076
  190.2 17.4 %collective-permute-start.22 = (bf16[8,256,384]{2,1,0:T(8,128)(2,1)}, bf16[8,256,384]{2,1,0:T(8,128)(2,1)}, u32[]{:S(2)}, u32[]{:S(2)}) collective-permute-start(bf16[8,256,384]{2,1,0:T(8,128)(2,1)} %convolution_convert_fusion), channel_id=1, source_target_pairs={{0,32},{32,0},{64,96},{96,64},{128,160},{160,128},{192,224},{224,1... | collective-permute-start | bytes 4718600 | tf_op jit(solution)/shard_map/ppermute | solution.py:148

commit v2 on v1

--- a/solution.py
+++ b/solution.py
@@ -2,6 +2,8 @@
 import jax.numpy as jnp
 from jax import lax
 from jax.sharding import PartitionSpec as P
+from jax.experimental import pallas as pl
+from jax.experimental.pallas import tpu as pltpu
 
 
 def ring_perm(n, step):
@@ -12,7 +14,7 @@
     return [(s, s ^ 1) for s in range(n)]
 
 
-def exclusive_state(local, log_fall, n):
+def exclusive_state(local, log_fall, n, where):
     heads, hsize, _ = local.shape
     rows = heads * hsize * hsize // (n * 128)
     pieces = local.astype(jnp.bfloat16).reshape(n, rows, 128)
@@ -32,8 +34,47 @@
     slices = got[:, :rows, :].reshape(n, rows * 128).astype(jnp.float32)
     earlier = jnp.dot(mix, slices, precision=lax.Precision.HIGHEST)
     earlier = earlier.astype(jnp.bfloat16).reshape(n, rows, 128)
+    earlier, where = lax.optimization_barrier((earlier, where))
     back = lax.all_to_all(earlier, "seq", 0, 0, tiled=True)
-    return back.reshape(heads, hsize, hsize)
+    return back.reshape(heads, hsize, hsize), where
+
+
+def place_outs(where, blocks, n_z, shard, width):
+    def kernel(where_ref, *refs):
+        sources, out, sems = refs[: len(set_of)], refs[len(set_of)], refs[len(set_of) + 1]
+        z, half, core = where_ref[0], where_ref[1], where_ref[2]
+        copies = []
+        for n, (source, row, column, offset, other) in enumerate(items):
+            at = lax.rem(z + (offset + n_z), n_z)
+            chip, part = lax.div(at, 2), lax.rem(at, 2)
+            away = lax.rem(part + core, 2)
+            side = half if other == 0 else 1 - half
+            copies.append(
+                pltpu.make_async_copy(
+                    sources[source].at[pl.ds(row, shard), pl.ds(column, width)],
+                    out.at[away, chip, pl.ds(side * shard, shard), :],
+                    sems.at[n],
+                )
+            )
+        for copy in copies:
+            copy.start()
+        for copy in copies:
+            copy.wait()
+
+    set_of, items = [], []
+    for array, row, column, offset, other in blocks:
+        known = [i for i, a in enumerate(set_of) if a is array]
+        if not known:
+            set_of.append(array)
+        items.append((known[0] if known else len(set_of) - 1, row, column, offset, other))
+    return pl.pallas_call(
+        kernel,
+        out_shape=jax.ShapeDtypeStruct((2, n_z // 2, 2 * shard, width), jnp.bfloat16),
+        in_specs=[pl.BlockSpec(memory_space=pltpu.SMEM)] + [pl.BlockSpec(memory_space=pl.ANY)] * len(set_of),
+        out_specs=pl.BlockSpec(memory_space=pl.ANY),
+        scratch_shapes=[pltpu.SemaphoreType.DMA((len(items),))],
+        name="place_outs",
+    )(where, *set_of)
 
 
 def make_body(n_seq, n_dp):
@@ -80,7 +121,10 @@
         ]
 
         def times(toks, weight, group):
-            tok = jnp.concatenate([toks[(o + last) % n_z] for o in group], axis=0)
+            if group == groups[0]:
+                tok = toks[last - inner : last + inner + 1].reshape(len(group) * shard, rows)
+            else:
+                tok = jnp.concatenate([toks[(o + last) % n_z] for o in group], axis=0)
             return lax.dot_general(tok, weight, (((0,), (0,)), ((), ())), preferred_element_type=f32)
 
         def join(partial, keep):
@@ -102,33 +146,23 @@
         away = theirs_sum[:, q_cols] + times(theirs, final[:, q_cols], groups[2])
         q_proj = join(away, mine_sum[:, q_cols] + times(mine, final[:, q_cols], groups[2]))
 
-        other_outs = {}
+        blocks = []
         for batch in groups:
             joined = jnp.concatenate([pieces[o][:, 3 * width :] for o in batch], axis=0)
             swapped = lax.ppermute(joined, "seq", flip)
-            for i, o in enumerate(batch):
-                other_outs[o] = swapped[i * shard : (i + 1) * shard]
+            blocks += [(swapped, i * shard, 0, o, 1) for i, o in enumerate(batch)]
+            blocks += [(pieces[o], 0, 3 * width, o, 0) for o in batch]
+
         key = jax.nn.silu(kv_proj[:, :width]).astype(jnp.bfloat16).reshape(rows, heads, hsize)
         value = kv_proj[:, width:].astype(jnp.bfloat16).reshape(rows, heads, hsize)
         query = jax.nn.silu(q_proj).astype(jnp.bfloat16).reshape(rows, heads, hsize)
         cum = jnp.cumsum(log_decay, axis=1)
         scaled_key = (key.astype(f32) * jnp.exp(cum[:, -1:] - cum).T[:, :, None]).astype(jnp.bfloat16)
         local = jnp.einsum("thd,the->hde", scaled_key, value, preferred_element_type=f32)
-        in_order = list(range(0, last + 1)) + list(range(-last + 1, 0))
-        own_outs = {o: pieces[o][:, 3 * width :] for o in in_order}
-        (own_outs, other_outs), _ = lax.optimization_barrier(((own_outs, other_outs), local))
-        outs = jnp.stack(
-            [
-                jnp.stack([own_outs[o], other_outs[o], own_outs[o]])
-                for o in in_order
-            ]
-        )
-        outs = lax.dynamic_slice_in_dim(outs, half, 2, axis=1)
-        outs = jnp.roll(outs, z, axis=0).reshape(n_z // 2, 2, 2 * shard, width)
-        out_mine = lax.dynamic_index_in_dim(outs, core, 1, False)
-        out_theirs = lax.dynamic_index_in_dim(outs, 1 - core, 1, False)
-
-        earlier_state = exclusive_state(local, cum[:, -1], n_seq)
+        where = jnp.stack([z, half, core]).astype(jnp.int32)
+        earlier_state, where = exclusive_state(local, cum[:, -1], n_seq, where)
+        outs = place_outs(where, blocks, n_z, shard, width)
+        out_mine, out_theirs = outs[0], outs[1]
 
         later = jnp.arange(rows)[:, None] >= jnp.arange(rows)[None, :]
         scores = jnp.einsum("thd,shd->hts", query, key, preferred_element_type=f32)
@@ -147,7 +181,7 @@
         give = jnp.einsum("itg,idg->itd", wide, out_theirs, preferred_element_type=f32)
         taken = lax.ppermute(give.astype(jnp.bfloat16), "dp", pair_perm(n_dp))
         keep = jnp.einsum("itg,idg->itd", wide, out_mine, preferred_element_type=f32)
-        keep = keep.astype(jnp.bfloat16).astype(f32) + taken.astype(f32)
+        keep = lax.optimization_barrier(keep.astype(jnp.bfloat16)).astype(f32) + taken.astype(f32)
         groups = [[2 * i + c for i in range(n_dp // 2)] for c in range(2)]
         spread_out = lax.all_to_all(keep.astype(jnp.bfloat16), "dp", 0, 0, axis_index_groups=groups, tiled=True)
         return jnp.sum(spread_out.astype(f32), axis=0).astype(jnp.bfloat16)

time: 236 us -> 318 us (1.35)
  the two profiles are of different devices: /device:TPU:1 before, /device:TPU:4 now
where the time goes in v2:
time: 318 us; the launch traced here: 316 us
  starting transfers between devices  113 us (36%)
  Pallas kernels  97.4 us (31%)
  waiting for transfers between devices  39.3 us (12%)
  blocking collectives  26.2 us (8%)
  local copies, waits for them, and re-layouts  19.5 us (6%)
  matrix products  12.4 us (4%)
  other arithmetic  7.26 us (2%)
    pallas_call x1, Pallas kernels, place_outs(): pl.pallas_call(kernel, out_shape=jax.ShapeDtypeStruct((2, n_z // 2, 2 * s...  97.4 us
    ppermute x7, starting transfers between devices, layer(): behind = lax.ppermute(behind, 'seq', down)  41.1 us
    all_to_all x1, blocking collectives, layer(): lax.all_to_all(keep.astype(jnp.bfloat16), 'dp', 0, 0, axis_index_groups=g...  26.2 us
    ppermute x7, waiting for transfers between devices, layer(): ahead = lax.ppermute(ahead, 'seq', up)  21.2 us
    unnamed x118, local copies, waits for them, and re-layouts  15.7 us
    ppermute x7, starting transfers between devices, layer(): ahead = lax.ppermute(ahead, 'seq', up)  15.3 us
    all_to_all x1, starting transfers between devices, exclusive_state(): back = lax.all_to_all(earlier, 'seq', 0, 0, tiled=True)  14.6 us
    all_to_all x1, starting transfers between devices, exclusive_state(): got = lax.all_to_all(sent, 'seq', 0, 0, tiled=True)  12.5 us
  transfers between devices with their start and end apart: 25, of which 14 were waited for; matrix products, arithmetic and copies ran while one was open for 8% of the time, Pallas kernels for 31%

profile of v2, /device:TPU:4, one launch (start us, length us, event | category | flops | bytes accessed | tf_op | source)
XLA Modules:
  0.0 316.4 jit_solution(9034700262285408262)
XLA Ops:
  0.0 1.0 slice_bitcast_fusion.13
  1.0 1.0 pad_maximum_fusion.1.refs_5_
  2.1 3.8 %collective-permute-start = (bf16[192,1024]{1,0:T(8,128)(2,1)S(1)}, bf16[192,1024]{1,0:T(8,128)(2,1)S(1)}, u32[]{:S(2)}, u32[]{:S(2)}) collective-permute-start(bf16[192,1024]{1,0:T(8,128)(2,1)S(1)} %pad_maximum_fusion.1.refs_5_), channel_id=1, source_target_pairs={{0,2},{1,3},{2,4},{3,5},{4,6},{5,7},{6,8},{7,9},{8,10},{9,11},{10,... | collective-permute-start | bytes 1179656 | tf_op jit(solution)/shard_map/ppermute | solution.py:101
  6.0 9.5 %collective-permute-start.4 = (bf16[192,1024]{1,0:T(8,128)(2,1)S(1)}, bf16[192,1024]{1,0:T(8,128)(2,1)}, u32[]{:S(2)}, u32[]{:S(2)}) collective-permute-start(bf16[192,1024]{1,0:T(8,128)(2,1)S(1)} %pad_maximum_fusion.1.refs_5_), channel_id=1, source_target_pairs={{0,30},{1,31},{2,0},{3,1},{4,2},{5,3},{6,4},{7,5},{8,6},{9,7},{10,... | collective-permute-start | bytes 1179656 | tf_op jit(solution)/shard_map/ppermute | solution.py:102
  18.5 4.1 %collective-permute-done.refs_4_ = bf16[192,1024]{1,0:T(8,128)(2,1)S(1)} collective-permute-done((bf16[192,1024]{1,0:T(8,128)(2,1)S(1)}, bf16[192,1024]{1,0:T(8,128)(2,1)S(1)}, u32[]{:S(2)}, u32[]{:S(2)}) %collective-permute-start) | collective-permute-done | bytes 393248 | tf_op jit(solution)/shard_map/ppermute | solution.py:101
  22.6 1.9 collective-permute-start.1
  25.9 5.1 %collective-permute-start.5 = (bf16[192,1024]{1,0:T(8,128)(2,1)}, bf16[192,1024]{1,0:T(8,128)(2,1)}, u32[]{:S(2)}, u32[]{:S(2)}) collective-permute-start(bf16[192,1024]{1,0:T(8,128)(2,1)} %collective-permute-done.4.refs_6_), channel_id=1, source_target_pairs={{0,30},{1,31},{2,0},{3,1},{4,2},{5,3},{6,4},{7,5},{8,6},{9,7},{10,... | collective-permute-start | bytes 1179656 | tf_op jit(solution)/shard_map/ppermute | solution.py:102
  31.0 5.1 %collective-permute-done.1.refs_3_ = bf16[192,1024]{1,0:T(8,128)(2,1)} collective-permute-done((bf16[192,1024]{1,0:T(8,128)(2,1)S(1)}, bf16[192,1024]{1,0:T(8,128)(2,1)}, u32[]{:S(2)}, u32[]{:S(2)}) %collective-permute-start.1) | collective-permute-done | bytes 393248 | tf_op jit(solution)/shard_map/ppermute | solution.py:101
  36.1 1.9 collective-permute-start.2
  38.9 3.2 %copy.44 = bf16[256,6144]{0,1:T(8,128)(2,1)S(1)} copy(bf16[256,6144]{1,0:T(8,128)(2,1)} %param.5) | data formatting | bytes 6291456 | tf_op args[0]
  42.6 5.1 %collective-permute-start.6 = (bf16[192,1024]{1,0:T(8,128)(2,1)}, bf16[192,1024]{1,0:T(8,128)(2,1)S(1)}, u32[]{:S(2)}, u32[]{:S(2)}) collective-permute-start(bf16[192,1024]{1,0:T(8,128)(2,1)} %collective-permute-done.5.refs_7_), channel_id=1, source_target_pairs={{0,30},{1,31},{2,0},{3,1},{4,2},{5,3},{6,4},{7,5},{8,6},{9,7},{10,... | collective-permute-start | bytes 1179656 | tf_op jit(solution)/shard_map/ppermute | solution.py:102
  47.7 1.2 collective-permute-done.2.refs_2_
  48.9 1.9 collective-permute-start.3
  51.0 2.5 collective-permute-start.16
  54.7 5.5 %collective-permute-start.7 = (bf16[192,1024]{1,0:T(8,128)(2,1)S(1)}, bf16[192,1024]{1,0:T(8,128)(2,1)S(1)}, u32[]{:S(2)}, u32[]{:S(2)}) collective-permute-start(bf16[192,1024]{1,0:T(8,128)(2,1)S(1)} %collective-permute-done.6.refs_8_), channel_id=1, source_target_pairs={{0,30},{1,31},{2,0},{3,1},{4,2},{5,3},{6,4},{7,5},{8,6},{9,7},{10,... | collective-permute-start | bytes 1179656 | tf_op jit(solution)/shard_map/ppermute | solution.py:102
  60.8 1.0 slice_dynamic-update-slice_fusion.14
  62.8 1.9 collective-permute-start.8
  67.8 5.1 %collective-permute-start.10 = (bf16[192,1024]{1,0:T(8,128)(2,1)S(1)}, bf16[192,1024]{1,0:T(8,128)(2,1)S(1)}, u32[]{:S(2)}, u32[]{:S(2)}) collective-permute-start(bf16[192,1024]{1,0:T(8,128)(2,1)S(1)} %collective-permute-done.7.refs_9_), channel_id=1, source_target_pairs={{0,30},{1,31},{2,0},{3,1},{4,2},{5,3},{6,4},{7,5},{8,6},{9,7},{10,... | collective-permute-start | bytes 1179656 | tf_op jit(solution)/shard_map/ppermute | solution.py:102
  76.8 1.5 collective-permute-done.10.refs_13_
  78.2 5.6 %collective-permute-start.11 = (bf16[192,1024]{1,0:T(8,128)(2,1)S(1)}, bf16[192,1024]{1,0:T(8,128)(2,1)S(1)}, u32[]{:S(2)}, u32[]{:S(2)}) collective-permute-start(bf16[192,1024]{1,0:T(8,128)(2,1)S(1)} %collective-permute-done.10.refs_13_), channel_id=1, source_target_pairs={{0,30},{1,31},{2,0},{3,1},{4,2},{5,3},{6,4},{7,5},{8,6},{9,7},{10,... | collective-permute-start | bytes 1179656 | tf_op jit(solution)/shard_map/ppermute | solution.py:102
  83.9 1.9 collective-permute-start.9
  85.8 2.5 collective-permute-done.16
  89.4 5.7 %collective-permute-done.9.refs_11_ = bf16[192,1024]{1,0:T(8,128)(2,1)S(1)} collective-permute-done((bf16[192,1024]{1,0:T(8,128)(2,1)S(1)}, bf16[192,1024]{1,0:T(8,128)(2,1)S(1)}, u32[]{:S(2)}, u32[]{:S(2)}) %collective-permute-start.9) | collective-permute-done | bytes 393248 | tf_op jit(solution)/shard_map/ppermute | solution.py:101
  95.1 1.9 collective-permute-start.12
  97.0 5.1 %collective-permute-start.13 = (bf16[192,1024]{1,0:T(8,128)(2,1)S(1)}, bf16[192,1024]{1,0:T(8,128)(2,1)S(1)}, u32[]{:S(2)}, u32[]{:S(2)}) collective-permute-start(bf16[192,1024]{1,0:T(8,128)(2,1)S(1)} %collective-permute-done.11.refs_14_), channel_id=1, source_target_pairs={{0,30},{1,31},{2,0},{3,1},{4,2},{5,3},{6,4},{7,5},{8,6},{9,7},{10,... | collective-permute-start | bytes 1179656 | tf_op jit(solution)/shard_map/ppermute | solution.py:102
  102.9 4.5 %collective-permute-done.12.refs_16_ = bf16[192,1024]{1,0:T(8,128)(2,1)S(1)} collective-permute-done((bf16[192,1024]{1,0:T(8,128)(2,1)S(1)}, bf16[192,1024]{1,0:T(8,128)(2,1)S(1)}, u32[]{:S(2)}, u32[]{:S(2)}) %collective-permute-start.12) | collective-permute-done | bytes 393248 | tf_op jit(solution)/shard_map/ppermute | solution.py:101
  107.4 1.9 collective-permute-start.14
  109.4 5.4 %collective-permute-start.15 = (bf16[96,1024]{1,0:T(8,128)(2,1)S(1)}, bf16[96,1024]{1,0:T(8,128)(2,1)S(1)}, u32[]{:S(2)}, u32[]{:S(2)}) collective-permute-start(bf16[96,1024]{1,0:T(8,128)(2,1)S(1)} %slice.289), channel_id=1, source_target_pairs={{0,30},{1,31},{2,0},{3,1},{4,2},{5,3},{6,4},{7,5},{8,6},{9,7},{10,... | collective-permute-start | bytes 589832 | tf_op jit(solution)/shard_map/ppermute | solution.py:105
  114.8 1.4 collective-permute-done.14
  116.2 1.7 collective-permute-done.15
  118.4 2.9 collective-permute-start.17
  121.8 6.4 %collective-permute-done.17 = bf16[256,512]{1,0:T(8,128)(2,1)S(1)} collective-permute-done((bf16[256,512]{1,0:T(8,128)(2,1)S(1)}, bf16[256,512]{1,0:T(8,128)(2,1)S(1)}, u32[]{:S(2)}, u32[]{:S(2)}) %collective-permute-start.17) | collective-permute-done | bytes 262176 | tf_op jit(solution)/shard_map/ppermute | solution.py:131
  129.6 1.1 convolution_convert_fusion.3
  131.4 12.5 %all-to-all-start = ((bf16[32,16,128]{2,1,0:T(8,128)(2,1)}), bf16[32,16,128]{2,1,0:T(8,128)(2,1)S(1)}, u32[]{:S(2)}, u32[]{:S(2)}) async-start(bf16[32,16,128]{2,1,0:T(8,128)(2,1)} %fusion.54), calls=%async_computation | async-start | bytes 262144 | tf_op jit(solution)/shard_map/all_to_all | solution.py:28
  144.6 2.1 collective-permute-start.19
  146.9 5.2 %collective-permute-start.20 = (bf16[768,256]{1,0:T(8,128)(2,1)S(1)}, bf16[768,256]{1,0:T(8,128)(2,1)S(1)}, u32[]{:S(2)}, u32[]{:S(2)}) collective-permute-start(bf16[768,256]{1,0:T(8,128)(2,1)S(1)} %pad_maximum_fusion.2), channel_id=1, source_target_pairs={{0,1},{1,0},{2,3},{3,2},{4,5},{5,4},{6,7},{7,6},{8,9},{9,8},{10,11... | collective-permute-start | bytes 1179656 | tf_op jit(solution)/shard_map/ppermute | solution.py:152
  152.2 1.4 fusion.36
  153.7 2.3 collective-permute-start.21
  155.9 5.2 %collective-permute-start.18 = (bf16[256,256]{1,0:T(8,128)(2,1)S(1)}, bf16[256,256]{1,0:T(8,128)(2,1)S(1)}, u32[]{:S(2)}, u32[]{:S(2)}) collective-permute-start(bf16[256,256]{1,0:T(8,128)(2,1)S(1)} %fusion.36), channel_id=1, source_target_pairs={{0,1},{1,0},{2,3},{3,2},{4,5},{5,4},{6,7},{7,6},{8,9},{9,8},{10,11... | collective-permute-start | bytes 393224 | tf_op jit(solution)/shard_map/ppermute | solution.py:131
  162.6 14.6 %all-to-all-start.1 = ((bf16[32,8,128]{2,1,0:T(8,128)(2,1)}), bf16[32,8,128]{2,1,0:T(8,128)(2,1)S(1)}, u32[]{:S(2)}, u32[]{:S(2)}) async-start(bf16[32,8,128]{2,1,0:T(8,128)(2,1)} %bitcast.49), calls=%async_computation.1 | async-start | bytes 131072 | tf_op jit(solution)/shard_map/all_to_all | solution.py:38
  177.2 1.1 collective-permute-done.18
  178.3 1.5 fusion.51
  181.7 97.4 %place_outs.1 = bf16[2,8,384,256]{3,2,1,0:T(8,128)(2,1)} custom-call(s32[3]{0:T(128)} %pad_add_fusion.where_ref, bf16[1728,256]{1,0:T(8,128)(2,1)} %collective-permute-done.19.refs_0_, bf16[192,1024]{1,0:T(8,128)(2,1)} %copy-done.7, bf16[192,1024]{1,0:T(8,128)(2,1)} %collective-permute-done.2.refs_2_, bf16[192,1024]{1,0:T(8,128)(2,1)} %collective-permute-done.1.refs_3_, ...), custom_call_target="tpu_custom_call" | custom-call | tf_op jit(solution)/shard_map/place_outs/pallas_call | solution.py:70
  279.8 1.3 multiply_reduce_fusion
  281.4 2.1 convolution_convert_fusion
  283.5 1.9 collective-permute-start.22
  286.1 2.6 collective-permute-done.22
  289.2 26.2 %all_to_all.15 = bf16[8,256,384]{2,1,0:T(8,128)(2,1)S(1)} all-to-all(bf16[8,256,384]{2,1,0:T(8,128)(2,1)S(1)} %add_convert_fusion), channel_id=1, replica_groups={{0,64,128,192,256,320,384,448},{32,96,160,224,288,352,416,480},{1,65,12..., dimensions={0} | all-to-all | bytes 3145728 | tf_op jit(solution)/shard_map/all_to_all | solution.py:186
  (188 shorter events, 27.1 us)
Async XLA Ops:
  2.1 40.0 %copy-start.3 = (bf16[192,1024]{1,0:T(8,128)(2,1)}, bf16[192,1024]{1,0:T(8,128)(2,1)S(1)}, u32[]{:S(2)}) copy-start(bf16[192,1024]{1,0:T(8,128)(2,1)S(1)} %pad_maximum_fusion.1.refs_5_) | copy-start | bytes 1179652
  2.1 20.5 %collective-permute-start = (bf16[192,1024]{1,0:T(8,128)(2,1)S(1)}, bf16[192,1024]{1,0:T(8,128)(2,1)S(1)}, u32[]{:S(2)}, u32[]{:S(2)}) collective-permute-start(bf16[192,1024]{1,0:T(8,128)(2,1)S(1)} %pad_maximum_fusion.1.refs_5_), channel_id=1, source_target_pairs={{0,2},{1,3},{2,4},{3,5},{4,6},{5,7},{6,8},{7,9},{8,10},{9,11},{10,... | collective-permute-start | bytes 1179656 | tf_op jit(solution)/shard_map/ppermute | solution.py:101
  6.0 19.9 %collective-permute-start.4 = (bf16[192,1024]{1,0:T(8,128)(2,1)S(1)}, bf16[192,1024]{1,0:T(8,128)(2,1)}, u32[]{:S(2)}, u32[]{:S(2)}) collective-permute-start(bf16[192,1024]{1,0:T(8,128)(2,1)S(1)} %pad_maximum_fusion.1.refs_5_), channel_id=1, source_target_pairs={{0,30},{1,31},{2,0},{3,1},{4,2},{5,3},{6,4},{7,5},{8,6},{9,7},{10,... | collective-permute-start | bytes 1179656 | tf_op jit(solution)/shard_map/ppermute | solution.py:102
  22.6 16.2 %copy-start.4 = (bf16[192,1024]{1,0:T(8,128)(2,1)}, bf16[192,1024]{1,0:T(8,128)(2,1)S(1)}, u32[]{:S(2)}) copy-start(bf16[192,1024]{1,0:T(8,128)(2,1)S(1)} %collective-permute-done.refs_4_) | copy-start | bytes 1179652
  22.6 13.5 %collective-permute-start.1 = (bf16[192,1024]{1,0:T(8,128)(2,1)S(1)}, bf16[192,1024]{1,0:T(8,128)(2,1)}, u32[]{:S(2)}, u32[]{:S(2)}) collective-permute-start(bf16[192,1024]{1,0:T(8,128)(2,1)S(1)} %collective-permute-done.refs_4_), channel_id=1, source_target_pairs={{0,2},{1,3},{2,4},{3,5},{4,6},{5,7},{6,8},{7,9},{8,10},{9,11},{10,... | collective-permute-start | bytes 1179656 | tf_op jit(solution)/shard_map/ppermute | solution.py:101
  25.9 16.7 %collective-permute-start.5 = (bf16[192,1024]{1,0:T(8,128)(2,1)}, bf16[192,1024]{1,0:T(8,128)(2,1)}, u32[]{:S(2)}, u32[]{:S(2)}) collective-permute-start(bf16[192,1024]{1,0:T(8,128)(2,1)} %collective-permute-done.4.refs_6_), channel_id=1, source_target_pairs={{0,30},{1,31},{2,0},{3,1},{4,2},{5,3},{6,4},{7,5},{8,6},{9,7},{10,... | collective-permute-start | bytes 1179656 | tf_op jit(solution)/shard_map/ppermute | solution.py:102
  36.1 12.8 %collective-permute-start.2 = (bf16[192,1024]{1,0:T(8,128)(2,1)}, bf16[192,1024]{1,0:T(8,128)(2,1)}, u32[]{:S(2)}, u32[]{:S(2)}) collective-permute-start(bf16[192,1024]{1,0:T(8,128)(2,1)} %collective-permute-done.1.refs_3_), channel_id=1, source_target_pairs={{0,2},{1,3},{2,4},{3,5},{4,6},{5,7},{6,8},{7,9},{8,10},{9,11},{10,... | collective-permute-start | bytes 1179656 | tf_op jit(solution)/shard_map/ppermute | solution.py:101
  42.6 12.1 %collective-permute-start.6 = (bf16[192,1024]{1,0:T(8,128)(2,1)}, bf16[192,1024]{1,0:T(8,128)(2,1)S(1)}, u32[]{:S(2)}, u32[]{:S(2)}) collective-permute-start(bf16[192,1024]{1,0:T(8,128)(2,1)} %collective-permute-done.5.refs_7_), channel_id=1, source_target_pairs={{0,30},{1,31},{2,0},{3,1},{4,2},{5,3},{6,4},{7,5},{8,6},{9,7},{10,... | collective-permute-start | bytes 1179656 | tf_op jit(solution)/shard_map/ppermute | solution.py:102
  48.9 11.9 %collective-permute-start.3 = (bf16[192,1024]{1,0:T(8,128)(2,1)}, bf16[192,1024]{1,0:T(8,128)(2,1)S(1)}, u32[]{:S(2)}, u32[]{:S(2)}) collective-permute-start(bf16[192,1024]{1,0:T(8,128)(2,1)} %collective-permute-done.2.refs_2_), channel_id=1, source_target_pairs={{0,2},{1,3},{2,4},{3,5},{4,6},{5,7},{6,8},{7,9},{8,10},{9,11},{10,... | collective-permute-start | bytes 1179656 | tf_op jit(solution)/shard_map/ppermute | solution.py:101
  51.0 37.4 %collective-permute-start.16 = (bf16[16,192,256]{2,1,0:T(8,128)(2,1)S(1)}, bf16[16,192,256]{2,1,0:T(8,128)(2,1)S(1)}, u32[]{:S(2)}, u32[]{:S(2)}) collective-permute-start(bf16[16,192,256]{2,1,0:T(8,128)(2,1)S(1)} %dynamic-slice_bitcast_fusion), channel_id=1, source_target_pairs={{0,1},{1,0},{2,3},{3,2},{4,5},{5,4},{6,7},{7,6},{8,9},{9,8},{10,11... | collective-permute-start | bytes 4718600 | tf_op jit(solution)/shard_map/ppermute | solution.py:114
  53.6 74.6 %copy-start.28 = (bf16[192,256]{1,0:T(8,128)(2,1)}, bf16[192,256]{1,0:T(8,128)(2,1)S(1)}, u32[]{:S(2)}) copy-start(bf16[192,256]{1,0:T(8,128)(2,1)S(1)} %get-tuple-element.12) | copy-start | bytes 294916
  53.6 74.6 %copy-start.29 = (bf16[192,256]{1,0:T(8,128)(2,1)}, bf16[192,256]{1,0:T(8,128)(2,1)S(1)}, u32[]{:S(2)}) copy-start(bf16[192,256]{1,0:T(8,128)(2,1)S(1)} %get-tuple-element.17) | copy-start | bytes 294916
  54.7 31.1 %copy-start.6 = (bf16[192,1024]{1,0:T(8,128)(2,1)}, bf16[192,1024]{1,0:T(8,128)(2,1)S(1)}, u32[]{:S(2)}) copy-start(bf16[192,1024]{1,0:T(8,128)(2,1)S(1)} %collective-permute-done.6.refs_8_) | copy-start | bytes 1179652
  54.7 13.2 %collective-permute-start.7 = (bf16[192,1024]{1,0:T(8,128)(2,1)S(1)}, bf16[192,1024]{1,0:T(8,128)(2,1)S(1)}, u32[]{:S(2)}, u32[]{:S(2)}) collective-permute-start(bf16[192,1024]{1,0:T(8,128)(2,1)S(1)} %collective-permute-done.6.refs_8_), channel_id=1, source_target_pairs={{0,30},{1,31},{2,0},{3,1},{4,2},{5,3},{6,4},{7,5},{8,6},{9,7},{10,... | collective-permute-start | bytes 1179656 | tf_op jit(solution)/shard_map/ppermute | solution.py:102
  62.8 21.0 %collective-permute-start.8 = (bf16[192,1024]{1,0:T(8,128)(2,1)S(1)}, bf16[192,1024]{1,0:T(8,128)(2,1)S(1)}, u32[]{:S(2)}, u32[]{:S(2)}) collective-permute-start(bf16[192,1024]{1,0:T(8,128)(2,1)S(1)} %collective-permute-done.3.refs_1_), channel_id=1, source_target_pairs={{0,2},{1,3},{2,4},{3,5},{4,6},{5,7},{6,8},{7,9},{8,10},{9,11},{10,... | collective-permute-start | bytes 1179656 | tf_op jit(solution)/shard_map/ppermute | solution.py:101
  67.8 76.1 %copy-start.8 = (bf16[192,1024]{1,0:T(8,128)(2,1)}, bf16[192,1024]{1,0:T(8,128)(2,1)S(1)}, u32[]{:S(2)}) copy-start(bf16[192,1024]{1,0:T(8,128)(2,1)S(1)} %collective-permute-done.7.refs_9_) | copy-start | bytes 1179652
  67.8 10.4 %collective-permute-start.10 = (bf16[192,1024]{1,0:T(8,128)(2,1)S(1)}, bf16[192,1024]{1,0:T(8,128)(2,1)S(1)}, u32[]{:S(2)}, u32[]{:S(2)}) collective-permute-start(bf16[192,1024]{1,0:T(8,128)(2,1)S(1)} %collective-permute-done.7.refs_9_), channel_id=1, source_target_pairs={{0,30},{1,31},{2,0},{3,1},{4,2},{5,3},{6,4},{7,5},{8,6},{9,7},{10,... | collective-permute-start | bytes 1179656 | tf_op jit(solution)/shard_map/ppermute | solution.py:102
  78.2 68.5 %copy-start.10 = (bf16[192,1024]{1,0:T(8,128)(2,1)}, bf16[192,1024]{1,0:T(8,128)(2,1)S(1)}, u32[]{:S(2)}) copy-start(bf16[192,1024]{1,0:T(8,128)(2,1)S(1)} %collective-permute-done.10.refs_13_) | copy-start | bytes 1179652
  78.2 18.8 %collective-permute-start.11 = (bf16[192,1024]{1,0:T(8,128)(2,1)S(1)}, bf16[192,1024]{1,0:T(8,128)(2,1)S(1)}, u32[]{:S(2)}, u32[]{:S(2)}) collective-permute-start(bf16[192,1024]{1,0:T(8,128)(2,1)S(1)} %collective-permute-done.10.refs_13_), channel_id=1, source_target_pairs={{0,30},{1,31},{2,0},{3,1},{4,2},{5,3},{6,4},{7,5},{8,6},{9,7},{10,... | collective-permute-start | bytes 1179656 | tf_op jit(solution)/shard_map/ppermute | solution.py:102
  83.9 62.9 %copy-start.9 = (bf16[192,1024]{1,0:T(8,128)(2,1)}, bf16[192,1024]{1,0:T(8,128)(2,1)S(1)}, u32[]{:S(2)}) copy-start(bf16[192,1024]{1,0:T(8,128)(2,1)S(1)} %collective-permute-done.8.refs_12_) | copy-start | bytes 1179652
  83.9 11.2 %collective-permute-start.9 = (bf16[192,1024]{1,0:T(8,128)(2,1)S(1)}, bf16[192,1024]{1,0:T(8,128)(2,1)S(1)}, u32[]{:S(2)}, u32[]{:S(2)}) collective-permute-start(bf16[192,1024]{1,0:T(8,128)(2,1)S(1)} %collective-permute-done.8.refs_12_), channel_id=1, source_target_pairs={{0,2},{1,3},{2,4},{3,5},{4,6},{5,7},{6,8},{7,9},{8,10},{9,11},{10,... | collective-permute-start | bytes 1179656 | tf_op jit(solution)/shard_map/ppermute | solution.py:101
  95.1 51.8 %copy-start.12 = (bf16[192,1024]{1,0:T(8,128)(2,1)}, bf16[192,1024]{1,0:T(8,128)(2,1)S(1)}, u32[]{:S(2)}) copy-start(bf16[192,1024]{1,0:T(8,128)(2,1)S(1)} %collective-permute-done.9.refs_11_) | copy-start | bytes 1179652
  95.1 12.3 %collective-permute-start.12 = (bf16[192,1024]{1,0:T(8,128)(2,1)S(1)}, bf16[192,1024]{1,0:T(8,128)(2,1)S(1)}, u32[]{:S(2)}, u32[]{:S(2)}) collective-permute-start(bf16[192,1024]{1,0:T(8,128)(2,1)S(1)} %collective-permute-done.9.refs_11_), channel_id=1, source_target_pairs={{0,2},{1,3},{2,4},{3,5},{4,6},{5,7},{6,8},{7,9},{8,10},{9,11},{10,... | collective-permute-start | bytes 1179656 | tf_op jit(solution)/shard_map/ppermute | solution.py:101
  97.0 49.8 %copy-start.11 = (bf16[192,1024]{1,0:T(8,128)(2,1)}, bf16[192,1024]{1,0:T(8,128)(2,1)S(1)}, u32[]{:S(2)}) copy-start(bf16[192,1024]{1,0:T(8,128)(2,1)S(1)} %collective-permute-done.11.refs_14_) | copy-start | bytes 1179652
  97.0 12.3 %collective-permute-start.13 = (bf16[192,1024]{1,0:T(8,128)(2,1)S(1)}, bf16[192,1024]{1,0:T(8,128)(2,1)S(1)}, u32[]{:S(2)}, u32[]{:S(2)}) collective-permute-start(bf16[192,1024]{1,0:T(8,128)(2,1)S(1)} %collective-permute-done.11.refs_14_), channel_id=1, source_target_pairs={{0,30},{1,31},{2,0},{3,1},{4,2},{5,3},{6,4},{7,5},{8,6},{9,7},{10,... | collective-permute-start | bytes 1179656 | tf_op jit(solution)/shard_map/ppermute | solution.py:102
  102.2 15.8 %copy-start.30 = (bf16[192,256]{1,0:T(8,128)(2,1)}, bf16[192,256]{1,0:T(8,128)(2,1)S(1)}, u32[]{:S(2)}) copy-start(bf16[192,256]{1,0:T(8,128)(2,1)S(1)} %get-tuple-element.18) | copy-start | bytes 294916
  102.2 15.8 %copy-start.32 = (bf16[192,256]{1,0:T(8,128)(2,1)}, bf16[192,256]{1,0:T(8,128)(2,1)S(1)}, u32[]{:S(2)}) copy-start(bf16[192,256]{1,0:T(8,128)(2,1)S(1)} %get-tuple-element.19) | copy-start | bytes 294916
  107.4 44.7 %copy-start.1 = (bf16[192,1024]{1,0:T(8,128)(2,1)}, bf16[192,1024]{1,0:T(8,128)(2,1)S(1)}, u32[]{:S(2)}) copy-start(bf16[192,1024]{1,0:T(8,128)(2,1)S(1)} %collective-permute-done.12.refs_16_) | copy-start | bytes 1179652
  107.4 8.8 %collective-permute-start.14 = (bf16[96,1024]{1,0:T(8,128)(2,1)S(1)}, bf16[96,1024]{1,0:T(8,128)(2,1)S(1)}, u32[]{:S(2)}, u32[]{:S(2)}) collective-permute-start(bf16[96,1024]{1,0:T(8,128)(2,1)S(1)} %slice.288), channel_id=1, source_target_pairs={{0,2},{1,3},{2,4},{3,5},{4,6},{5,7},{6,8},{7,9},{8,10},{9,11},{10,... | collective-permute-start | bytes 589832 | tf_op jit(solution)/shard_map/ppermute | solution.py:104
  109.4 42.8 %copy-start.2 = (bf16[192,1024]{1,0:T(8,128)(2,1)}, bf16[192,1024]{1,0:T(8,128)(2,1)S(1)}, u32[]{:S(2)}) copy-start(bf16[192,1024]{1,0:T(8,128)(2,1)S(1)} %collective-permute-done.13.refs_17_) | copy-start | bytes 1179652
  109.4 8.5 %collective-permute-start.15 = (bf16[96,1024]{1,0:T(8,128)(2,1)S(1)}, bf16[96,1024]{1,0:T(8,128)(2,1)S(1)}, u32[]{:S(2)}, u32[]{:S(2)}) collective-permute-start(bf16[96,1024]{1,0:T(8,128)(2,1)S(1)} %slice.289), channel_id=1, source_target_pairs={{0,30},{1,31},{2,0},{3,1},{4,2},{5,3},{6,4},{7,5},{8,6},{9,7},{10,... | collective-permute-start | bytes 589832 | tf_op jit(solution)/shard_map/ppermute | solution.py:105
  118.0 34.2 %copy-start.13 = (bf16[192,1024]{1,0:T(8,128)(2,1)}, bf16[192,1024]{1,0:T(8,128)(2,1)S(1)}, u32[]{:S(2)}) copy-start(bf16[192,1024]{1,0:T(8,128)(2,1)S(1)} %get-tuple-element.28.refs_18_) | copy-start | bytes 1179652
  118.4 9.8 %collective-permute-start.17 = (bf16[256,512]{1,0:T(8,128)(2,1)S(1)}, bf16[256,512]{1,0:T(8,128)(2,1)S(1)}, u32[]{:S(2)}, u32[]{:S(2)}) collective-permute-start(bf16[256,512]{1,0:T(8,128)(2,1)S(1)} %fusion.6), channel_id=1, source_target_pairs={{0,1},{1,0},{2,3},{3,2},{4,5},{5,4},{6,7},{7,6},{8,9},{9,8},{10,11... | collective-permute-start | bytes 786440 | tf_op jit(solution)/shard_map/ppermute | solution.py:131
  131.4 30.1 %copy-start.37 = (pred[32,32]{1,0:T(8,128)(4,1)S(1)}, pred[32,32]{1,0:T(8,128)(4,1)}, u32[]{:S(2)}) copy-start(pred[32,32]{1,0:T(8,128)(4,1)} %get-tuple-element.39) | copy-start | bytes 3076
  131.4 30.1 %copy-start.38 = (pred[32,32]{1,0:T(8,128)(4,1)S(1)}, pred[32,32]{1,0:T(8,128)(4,1)}, u32[]{:S(2)}) copy-start(pred[32,32]{1,0:T(8,128)(4,1)} %get-tuple-element.40) | copy-start | bytes 3076
  131.4 29.7 %all-to-all-start = ((bf16[32,16,128]{2,1,0:T(8,128)(2,1)}), bf16[32,16,128]{2,1,0:T(8,128)(2,1)S(1)}, u32[]{:S(2)}, u32[]{:S(2)}) async-start(bf16[32,16,128]{2,1,0:T(8,128)(2,1)} %fusion.54), calls=%async_computation | async-start | bytes 262144 | tf_op jit(solution)/shard_map/all_to_all | solution.py:28
  144.6 35.7 %collective-permute-start.19 = (bf16[1728,256]{1,0:T(8,128)(2,1)}, bf16[1728,256]{1,0:T(8,128)(2,1)}, u32[]{:S(2)}, u32[]{:S(2)}) collective-permute-start(bf16[1728,256]{1,0:T(8,128)(2,1)} %slice_dynamic-update-slice_fusion.8), channel_id=1, source_target_pairs={{0,1},{1,0},{2,3},{3,2},{4,5},{5,4},{6,7},{7,6},{8,9},{9,8},{10,11... | collective-permute-start | bytes 2654216 | tf_op jit(solution)/shard_map/ppermute | solution.py:152
  146.9 33.4 %collective-permute-start.20 = (bf16[768,256]{1,0:T(8,128)(2,1)S(1)}, bf16[768,256]{1,0:T(8,128)(2,1)S(1)}, u32[]{:S(2)}, u32[]{:S(2)}) collective-permute-start(bf16[768,256]{1,0:T(8,128)(2,1)S(1)} %pad_maximum_fusion.2), channel_id=1, source_target_pairs={{0,1},{1,0},{2,3},{3,2},{4,5},{5,4},{6,7},{7,6},{8,9},{9,8},{10,11... | collective-permute-start | bytes 1179656 | tf_op jit(solution)/shard_map/ppermute | solution.py:152
  153.6 26.2 %copy-start.21 = (f32[256,512]{1,0:T(8,128)S(1)}, f32[256,512]{1,0:T(8,128)}, u32[]{:S(2)}) copy-start(f32[256,512]{1,0:T(8,128)} %copy-done.20) | copy-start | bytes 1572868
  153.6 26.2 %copy-start.36 = (pred[256,256]{1,0:T(8,128)(4,1)S(1)}, pred[256,256]{1,0:T(8,128)(4,1)}, u32[]{:S(2)}) copy-start(pred[256,256]{1,0:T(8,128)(4,1)} %iota_compare_fusion.1) | copy-start | bytes 196612
  153.6 26.2 %copy-start.43 = (f32[1,2,2,128]{3,1,2,0:T(2,128)S(1)}, f32[1,2,2,128]{3,1,2,0:T(2,128)}, u32[]{:S(2)}) copy-start(f32[1,2,2,128]{3,1,2,0:T(2,128)} %copy-done.42) | copy-start | bytes 6148
  153.7 26.6 %collective-permute-start.21 = (bf16[576,256]{1,0:T(8,128)(2,1)S(1)}, bf16[576,256]{1,0:T(8,128)(2,1)S(1)}, u32[]{:S(2)}, u32[]{:S(2)}) collective-permute-start(bf16[576,256]{1,0:T(8,128)(2,1)S(1)} %pad_maximum_fusion.5), channel_id=1, source_target_pairs={{0,1},{1,0},{2,3},{3,2},{4,5},{5,4},{6,7},{7,6},{8,9},{9,8},{10,11... | collective-permute-start | bytes 884744 | tf_op jit(solution)/shard_map/ppermute | solution.py:152
  155.9 22.3 %collective-permute-start.18 = (bf16[256,256]{1,0:T(8,128)(2,1)S(1)}, bf16[256,256]{1,0:T(8,128)(2,1)S(1)}, u32[]{:S(2)}, u32[]{:S(2)}) collective-permute-start(bf16[256,256]{1,0:T(8,128)(2,1)S(1)} %fusion.36), channel_id=1, source_target_pairs={{0,1},{1,0},{2,3},{3,2},{4,5},{5,4},{6,7},{7,6},{8,9},{9,8},{10,11... | collective-permute-start | bytes 393224 | tf_op jit(solution)/shard_map/ppermute | solution.py:131
  162.6 116.5 %all-to-all-start.1 = ((bf16[32,8,128]{2,1,0:T(8,128)(2,1)}), bf16[32,8,128]{2,1,0:T(8,128)(2,1)S(1)}, u32[]{:S(2)}, u32[]{:S(2)}) async-start(bf16[32,8,128]{2,1,0:T(8,128)(2,1)} %bitcast.49), calls=%async_computation.1 | async-start | bytes 131072 | tf_op jit(solution)/shard_map/all_to_all | solution.py:38
  179.8 99.3 %copy-start.27 = (bf16[32,2,8,128]{3,2,1,0:T(8,128)(2,1)}, bf16[32,2,8,128]{3,2,1,0:T(8,128)(2,1)S(1)}, u32[]{:S(2)}) copy-start(bf16[32,2,8,128]{3,2,1,0:T(8,128)(2,1)S(1)} %fusion.51) | copy-start | bytes 393220
  180.2 99.6 %copy-start.40 = (f32[256,2]{0,1:T(2,128)S(1)}, f32[256,2]{0,1:T(2,128)}, u32[]{:S(2)}) copy-start(f32[256,2]{0,1:T(2,128)} %get-tuple-element.32) | copy-start | bytes 6148
  180.2 100.9 %copy-start.44 = (f32[256]{0:T(256)S(1)}, f32[256]{0:T(256)}, u32[]{:S(2)}) copy-start(f32[256]{0:T(256)} %param.9) | copy-start | bytes 3076
  283.5 5.3 %collective-permute-start.22 = (bf16[8,256,384]{2,1,0:T(8,128)(2,1)S(1)}, bf16[8,256,384]{2,1,0:T(8,128)(2,1)S(1)}, u32[]{:S(2)}, u32[]{:S(2)}) collective-permute-start(bf16[8,256,384]{2,1,0:T(8,128)(2,1)S(1)} %convolution_convert_fusion), channel_id=1, source_target_pairs={{0,32},{32,0},{64,96},{96,64},{128,160},{160,128},{192,224},{224,1... | collective-permute-start | bytes 4718600 | tf_op jit(solution)/shard_map/ppermute | solution.py:182
  (24 other events, 181.6 us)

commit v3 on v1

--- a/solution.py
+++ b/solution.py
@@ -2,6 +2,8 @@
 import jax.numpy as jnp
 from jax import lax
 from jax.sharding import PartitionSpec as P
+from jax.experimental import pallas as pl
+from jax.experimental.pallas import tpu as pltpu
 
 
 def ring_perm(n, step):
@@ -12,7 +14,7 @@
     return [(s, s ^ 1) for s in range(n)]
 
 
-def exclusive_state(local, log_fall, n):
+def exclusive_state(local, log_fall, n, where):
     heads, hsize, _ = local.shape
     rows = heads * hsize * hsize // (n * 128)
     pieces = local.astype(jnp.bfloat16).reshape(n, rows, 128)
@@ -32,8 +34,71 @@
     slices = got[:, :rows, :].reshape(n, rows * 128).astype(jnp.float32)
     earlier = jnp.dot(mix, slices, precision=lax.Precision.HIGHEST)
     earlier = earlier.astype(jnp.bfloat16).reshape(n, rows, 128)
+    earlier, where = lax.optimization_barrier((earlier, where))
     back = lax.all_to_all(earlier, "seq", 0, 0, tiled=True)
-    return back.reshape(heads, hsize, hsize)
+    return back.reshape(heads, hsize, hsize), where
+
+
+def whole(shape):
+    return pl.BlockSpec(shape, lambda i: (0,) * len(shape), pipeline_mode=pl.Buffered(1))
+
+
+def place_outs(where, own, own_at, swapped, swapped_at, n_z, shard, width):
+    def kernel(where_ref, *refs):
+        out = refs[-1]
+        z, half, core = where_ref[0], where_ref[1], where_ref[2]
+
+        def place(block, offset, side):
+            at = lax.rem(z + (offset + n_z), n_z)
+            away = lax.rem(lax.rem(at, 2) + core, 2)
+            rows = pl.ds(pl.multiple_of(side * shard, shard), shard)
+            out[away, lax.div(at, 2), rows, :] = block
+
+        for ref, offset in zip(refs, own_at):
+            place(ref[...], offset, half)
+        for ref, offsets in zip(refs[len(own) :], swapped_at):
+            for n, offset in enumerate(offsets):
+                place(ref[n * shard : (n + 1) * shard, :], offset, 1 - half)
+
+    shape = (2, n_z // 2, 2 * shard, width)
+    return pl.pallas_call(
+        kernel,
+        out_shape=jax.ShapeDtypeStruct(shape, jnp.bfloat16),
+        grid=(1,),
+        in_specs=[pl.BlockSpec(memory_space=pltpu.SMEM)]
+        + [pl.BlockSpec((shard, width), lambda i: (0, 3), pipeline_mode=pl.Buffered(1))] * len(own)
+        + [whole(a.shape) for a in swapped],
+        out_specs=whole(shape),
+        compiler_params=pltpu.CompilerParams(vmem_limit_bytes=24 << 20),
+        name="place_outs",
+    )(where, *own, *swapped)
+
+
+def project(mine, theirs, sums, pieces, places, width):
+    def kernel(mine_ref, theirs_ref, *refs):
+        weights, outs = refs[len(sums) : len(sums) + len(pieces)], refs[-2:]
+        for n, (tok, out) in enumerate(zip((mine_ref, theirs_ref), outs)):
+            total = refs[n][...] if sums else None
+            for weight, place in zip(weights, places):
+                part = lax.dot_general(
+                    tok[place], weight[...], (((0,), (0,)), ((), ())), preferred_element_type=jnp.float32
+                )
+                total = part if total is None else total + part
+            out[...] = total
+
+    shard = pieces[0].shape[0]
+    shape = (mine.shape[2], 3 * width)
+    return pl.pallas_call(
+        kernel,
+        out_shape=[jax.ShapeDtypeStruct(shape, jnp.float32)] * 2,
+        grid=(1,),
+        in_specs=[whole(mine.shape)] * 2
+        + [whole(shape)] * len(sums)
+        + [pl.BlockSpec((shard, 3 * width), lambda i: (0, 0), pipeline_mode=pl.Buffered(1))] * len(pieces),
+        out_specs=[whole(shape)] * 2,
+        compiler_params=pltpu.CompilerParams(vmem_limit_bytes=32 << 20),
+        name="project",
+    )(mine, theirs, *sums, *pieces)
 
 
 def make_body(n_seq, n_dp):
@@ -88,13 +153,11 @@
             return keep + sent.astype(f32)
 
         columns = 3 * width
-        mine_sum = theirs_sum = None
+        sums = ()
         for group in groups[:2]:
-            weight = jnp.concatenate([pieces[o][:, :columns] for o in group], axis=0)
-            part = times(mine, weight, group)
-            mine_sum = part if mine_sum is None else mine_sum + part
-            part = times(theirs, weight, group)
-            theirs_sum = part if theirs_sum is None else theirs_sum + part
+            places = [(o + last) % n_z for o in group]
+            sums = project(mine, theirs, sums, [pieces[o] for o in group], places, width)
+        mine_sum, theirs_sum = sums
         final = jnp.concatenate([pieces[o] for o in groups[2]], axis=0)
         kv_cols, q_cols = slice(0, 2 * width), slice(2 * width, columns)
         away = theirs_sum[:, kv_cols] + times(theirs, final[:, kv_cols], groups[2])
@@ -102,33 +165,24 @@
         away = theirs_sum[:, q_cols] + times(theirs, final[:, q_cols], groups[2])
         q_proj = join(away, mine_sum[:, q_cols] + times(mine, final[:, q_cols], groups[2]))
 
-        other_outs = {}
-        for batch in groups:
+        swaps = []
+        batches = (groups[0], groups[1] + groups[2])
+        for batch in batches:
             joined = jnp.concatenate([pieces[o][:, 3 * width :] for o in batch], axis=0)
-            swapped = lax.ppermute(joined, "seq", flip)
-            for i, o in enumerate(batch):
-                other_outs[o] = swapped[i * shard : (i + 1) * shard]
+            swaps.append(lax.ppermute(joined, "seq", flip))
+
         key = jax.nn.silu(kv_proj[:, :width]).astype(jnp.bfloat16).reshape(rows, heads, hsize)
         value = kv_proj[:, width:].astype(jnp.bfloat16).reshape(rows, heads, hsize)
         query = jax.nn.silu(q_proj).astype(jnp.bfloat16).reshape(rows, heads, hsize)
         cum = jnp.cumsum(log_decay, axis=1)
         scaled_key = (key.astype(f32) * jnp.exp(cum[:, -1:] - cum).T[:, :, None]).astype(jnp.bfloat16)
         local = jnp.einsum("thd,the->hde", scaled_key, value, preferred_element_type=f32)
-        in_order = list(range(0, last + 1)) + list(range(-last + 1, 0))
-        own_outs = {o: pieces[o][:, 3 * width :] for o in in_order}
-        (own_outs, other_outs), _ = lax.optimization_barrier(((own_outs, other_outs), local))
-        outs = jnp.stack(
-            [
-                jnp.stack([own_outs[o], other_outs[o], own_outs[o]])
-                for o in in_order
-            ]
-        )
-        outs = lax.dynamic_slice_in_dim(outs, half, 2, axis=1)
-        outs = jnp.roll(outs, z, axis=0).reshape(n_z // 2, 2, 2 * shard, width)
-        out_mine = lax.dynamic_index_in_dim(outs, core, 1, False)
-        out_theirs = lax.dynamic_index_in_dim(outs, 1 - core, 1, False)
-
-        earlier_state = exclusive_state(local, cum[:, -1], n_seq)
+        where = jnp.stack([z, half, core]).astype(jnp.int32)
+        earlier_state, where = exclusive_state(local, cum[:, -1], n_seq, where)
+        own_at = list(pieces)
+        own = [pieces[o] for o in own_at]
+        outs = place_outs(where, own, own_at, swaps, batches, n_z, shard, width)
+        out_mine, out_theirs = outs[0], outs[1]
 
         later = jnp.arange(rows)[:, None] >= jnp.arange(rows)[None, :]
         scores = jnp.einsum("thd,shd->hts", query, key, preferred_element_type=f32)
@@ -147,7 +201,7 @@
         give = jnp.einsum("itg,idg->itd", wide, out_theirs, preferred_element_type=f32)
         taken = lax.ppermute(give.astype(jnp.bfloat16), "dp", pair_perm(n_dp))
         keep = jnp.einsum("itg,idg->itd", wide, out_mine, preferred_element_type=f32)
-        keep = keep.astype(jnp.bfloat16).astype(f32) + taken.astype(f32)
+        keep = lax.optimization_barrier(keep.astype(jnp.bfloat16)).astype(f32) + taken.astype(f32)
         groups = [[2 * i + c for i in range(n_dp // 2)] for c in range(2)]
         spread_out = lax.all_to_all(keep.astype(jnp.bfloat16), "dp", 0, 0, axis_index_groups=groups, tiled=True)
         return jnp.sum(spread_out.astype(f32), axis=0).astype(jnp.bfloat16)

time: 236 us -> 235 us (level)
  the two profiles are of different devices: /device:TPU:1 before, /device:TPU:4 now
where the time goes in v3:
time: 235 us; the launch traced here: 233 us
  starting transfers between devices  105 us (45%)
  waiting for transfers between devices  42.1 us (18%)
  local copies, waits for them, and re-layouts  38.9 us (17%)
  blocking collectives  26.5 us (11%)
  matrix products  9.28 us (4%)
  other arithmetic  5.55 us (2%)
  Pallas kernels  4.85 us (2%)
    ppermute x7, starting transfers between devices, layer(): behind = lax.ppermute(behind, 'seq', down)  40.7 us
    unnamed x107, local copies, waits for them, and re-layouts  34.5 us
    all_to_all x1, blocking collectives, layer(): lax.all_to_all(keep.astype(jnp.bfloat16), 'dp', 0, 0, axis_index_groups=g...  26.5 us
    ppermute x7, starting transfers between devices, layer(): ahead = lax.ppermute(ahead, 'seq', up)  15.3 us
    ppermute x7, waiting for transfers between devices, layer(): ahead = lax.ppermute(ahead, 'seq', up)  14.2 us
    ppermute x1, waiting for transfers between devices, layer(): theirs = lax.ppermute(theirs, 'seq', flip)  13.3 us
    all_to_all x1, starting transfers between devices, exclusive_state(): got = lax.all_to_all(sent, 'seq', 0, 0, tiled=True)  12.4 us
    all_to_all x1, starting transfers between devices, exclusive_state(): back = lax.all_to_all(earlier, 'seq', 0, 0, tiled=True)  11.5 us
  transfers between devices with their start and end apart: 24, of which 11 were waited for; matrix products, arithmetic and copies ran while one was open for 13% of the time, Pallas kernels for 2%

profile of v3, /device:TPU:4, one launch (start us, length us, event | category | flops | bytes accessed | tf_op | source)
XLA Modules:
  0.0 232.8 jit_solution(3821905081686143335)
XLA Ops:
  0.0 1.0 slice_bitcast_fusion.9
  2.0 3.8 %collective-permute-start = (bf16[192,1024]{1,0:T(8,128)(2,1)S(1)}, bf16[192,1024]{1,0:T(8,128)(2,1)S(1)}, u32[]{:S(2)}, u32[]{:S(2)}) collective-permute-start(bf16[192,1024]{1,0:T(8,128)(2,1)S(1)} %pad_maximum_fusion.refs_4_.refs_0_), channel_id=1, source_target_pairs={{0,2},{1,3},{2,4},{3,5},{4,6},{5,7},{6,8},{7,9},{8,10},{9,11},{10,... | collective-permute-start | bytes 1179656 | tf_op jit(solution)/shard_map/ppermute | solution.py:125
  5.8 9.5 %collective-permute-start.5 = (bf16[192,1024]{1,0:T(8,128)(2,1)S(1)}, bf16[192,1024]{1,0:T(8,128)(2,1)S(1)}, u32[]{:S(2)}, u32[]{:S(2)}) collective-permute-start(bf16[192,1024]{1,0:T(8,128)(2,1)S(1)} %pad_maximum_fusion.refs_4_.refs_0_), channel_id=1, source_target_pairs={{0,30},{1,31},{2,0},{3,1},{4,2},{5,3},{6,4},{7,5},{8,6},{9,7},{10,... | collective-permute-start | bytes 1179656 | tf_op jit(solution)/shard_map/ppermute | solution.py:126
  17.7 4.7 %collective-permute-done.refs_3_.refs_1_ = bf16[192,1024]{1,0:T(8,128)(2,1)S(1)} collective-permute-done((bf16[192,1024]{1,0:T(8,128)(2,1)S(1)}, bf16[192,1024]{1,0:T(8,128)(2,1)S(1)}, u32[]{:S(2)}, u32[]{:S(2)}) %collective-permute-start) | collective-permute-done | bytes 393248 | tf_op jit(solution)/shard_map/ppermute | solution.py:125
  22.5 1.9 collective-permute-start.2
  25.0 5.1 %collective-permute-start.6 = (bf16[192,1024]{1,0:T(8,128)(2,1)S(1)}, bf16[192,1024]{1,0:T(8,128)(2,1)S(1)}, u32[]{:S(2)}, u32[]{:S(2)}) collective-permute-start(bf16[192,1024]{1,0:T(8,128)(2,1)S(1)} %collective-permute-done.5.refs_5_.refs_2_), channel_id=1, source_target_pairs={{0,30},{1,31},{2,0},{3,1},{4,2},{5,3},{6,4},{7,5},{8,6},{9,7},{10,... | collective-permute-start | bytes 1179656 | tf_op jit(solution)/shard_map/ppermute | solution.py:126
  30.3 5.6 %collective-permute-done.2.refs_2_.refs_3_ = bf16[192,1024]{1,0:T(8,128)(2,1)S(1)} collective-permute-done((bf16[192,1024]{1,0:T(8,128)(2,1)S(1)}, bf16[192,1024]{1,0:T(8,128)(2,1)S(1)}, u32[]{:S(2)}, u32[]{:S(2)}) %collective-permute-start.2) | collective-permute-done | bytes 393248 | tf_op jit(solution)/shard_map/ppermute | solution.py:125
  35.8 1.9 collective-permute-start.3
  37.8 5.5 %collective-permute-start.7 = (bf16[192,1024]{1,0:T(8,128)(2,1)S(1)}, bf16[192,1024]{1,0:T(8,128)(2,1)S(1)}, u32[]{:S(2)}, u32[]{:S(2)}) collective-permute-start(bf16[192,1024]{1,0:T(8,128)(2,1)S(1)} %collective-permute-done.6.refs_6_.refs_4_), channel_id=1, source_target_pairs={{0,30},{1,31},{2,0},{3,1},{4,2},{5,3},{6,4},{7,5},{8,6},{9,7},{10,... | collective-permute-start | bytes 1179656 | tf_op jit(solution)/shard_map/ppermute | solution.py:126
  43.3 4.7 %copy.40 = bf16[256,6144]{0,1:T(8,128)(2,1)} copy(bf16[256,6144]{1,0:T(8,128)(2,1)} %param.5) | data formatting | bytes 6291456 | tf_op args[0]
  48.3 2.4 %constant_dynamic-update-slice_fusion.1 = bf16[32,2,192,256]{3,2,1,0:T(8,128)(2,1)S(1)} fusion(bf16[16,2,192,256]{3,2,1,0:T(8,128)(2,1)} %bitcast.95), kind=kLoop, calls=%fused_computation.90 | loop fusion | bytes 6291456
  50.7 1.9 collective-permute-start.4
  53.0 5.3 %collective-permute-start.8 = (bf16[192,1024]{1,0:T(8,128)(2,1)S(1)}, bf16[192,1024]{1,0:T(8,128)(2,1)S(1)}, u32[]{:S(2)}, u32[]{:S(2)}) collective-permute-start(bf16[192,1024]{1,0:T(8,128)(2,1)S(1)} %collective-permute-done.7.refs_7_.refs_6_), channel_id=1, source_target_pairs={{0,30},{1,31},{2,0},{3,1},{4,2},{5,3},{6,4},{7,5},{8,6},{9,7},{10,... | collective-permute-start | bytes 1179656 | tf_op jit(solution)/shard_map/ppermute | solution.py:126
  58.6 2.4 %collective-permute-start.1 = (bf16[16,192,256]{2,1,0:T(8,128)(2,1)S(1)}, bf16[16,192,256]{2,1,0:T(8,128)(2,1)S(1)}, u32[]{:S(2)}, u32[]{:S(2)}) collective-permute-start(bf16[16,192,256]{2,1,0:T(8,128)(2,1)S(1)} %get-tuple-element.22), channel_id=1, source_target_pairs={{0,1},{1,0},{2,3},{3,2},{4,5},{5,4},{6,7},{7,6},{8,9},{9,8},{10,11... | collective-permute-start | bytes 4718600 | tf_op jit(solution)/shard_map/ppermute | solution.py:138
  61.1 1.6 collective-permute-done.4.refs_0_.refs_7_
  62.7 1.9 collective-permute-start.9
  65.2 5.1 %collective-permute-start.11 = (bf16[192,1024]{1,0:T(8,128)(2,1)S(1)}, bf16[192,1024]{1,0:T(8,128)(2,1)S(1)}, u32[]{:S(2)}, u32[]{:S(2)}) collective-permute-start(bf16[192,1024]{1,0:T(8,128)(2,1)S(1)} %collective-permute-done.8.refs_8_), channel_id=1, source_target_pairs={{0,30},{1,31},{2,0},{3,1},{4,2},{5,3},{6,4},{7,5},{8,6},{9,7},{10,... | collective-permute-start | bytes 1179656 | tf_op jit(solution)/shard_map/ppermute | solution.py:126
  74.9 1.9 collective-permute-start.10
  77.4 3.4 %collective-permute-start.19 = (bf16[1728,256]{1,0:T(8,128)(2,1)}, bf16[1728,256]{1,0:T(8,128)(2,1)}, u32[]{:S(2)}, u32[]{:S(2)}) collective-permute-start(bf16[1728,256]{1,0:T(8,128)(2,1)} %slice_dynamic-update-slice_fusion.7), channel_id=1, source_target_pairs={{0,1},{1,0},{2,3},{3,2},{4,5},{5,4},{6,7},{7,6},{8,9},{9,8},{10,11... | collective-permute-start | bytes 2654216 | tf_op jit(solution)/shard_map/ppermute | solution.py:172
  80.9 5.1 %collective-permute-start.12 = (bf16[192,1024]{1,0:T(8,128)(2,1)S(1)}, bf16[192,1024]{1,0:T(8,128)(2,1)S(1)}, u32[]{:S(2)}, u32[]{:S(2)}) collective-permute-start(bf16[192,1024]{1,0:T(8,128)(2,1)S(1)} %collective-permute-done.11.refs_4_.refs_10_), channel_id=1, source_target_pairs={{0,30},{1,31},{2,0},{3,1},{4,2},{5,3},{6,4},{7,5},{8,6},{9,7},{10,... | collective-permute-start | bytes 1179656 | tf_op jit(solution)/shard_map/ppermute | solution.py:126
  86.0 13.3 %collective-permute-done.1.theirs_ref = bf16[16,192,256]{2,1,0:T(8,128)(2,1)S(1)} collective-permute-done((bf16[16,192,256]{2,1,0:T(8,128)(2,1)S(1)}, bf16[16,192,256]{2,1,0:T(8,128)(2,1)S(1)}, u32[]{:S(2)}, u32[]{:S(2)}) %collective-permute-start.1) | collective-permute-done | bytes 1572896 | tf_op jit(solution)/shard_map/ppermute | solution.py:138
  99.3 2.1 project.2
  101.4 1.9 collective-permute-start.13
  104.0 5.1 %collective-permute-start.14 = (bf16[192,1024]{1,0:T(8,128)(2,1)S(1)}, bf16[192,1024]{1,0:T(8,128)(2,1)S(1)}, u32[]{:S(2)}, u32[]{:S(2)}) collective-permute-start(bf16[192,1024]{1,0:T(8,128)(2,1)S(1)} %collective-permute-done.12.refs_5_.refs_12_), channel_id=1, source_target_pairs={{0,30},{1,31},{2,0},{3,1},{4,2},{5,3},{6,4},{7,5},{8,6},{9,7},{10,... | collective-permute-start | bytes 1179656 | tf_op jit(solution)/shard_map/ppermute | solution.py:126
  109.8 1.0 project.3
  112.2 2.3 collective-permute-done.13.refs_13_
  114.4 1.9 collective-permute-start.15
  116.5 5.6 %collective-permute-start.16 = (bf16[96,1024]{1,0:T(8,128)(2,1)S(1)}, bf16[96,1024]{1,0:T(8,128)(2,1)S(1)}, u32[]{:S(2)}, u32[]{:S(2)}) collective-permute-start(bf16[96,1024]{1,0:T(8,128)(2,1)S(1)} %slice.181), channel_id=1, source_target_pairs={{0,30},{1,31},{2,0},{3,1},{4,2},{5,3},{6,4},{7,5},{8,6},{9,7},{10,... | collective-permute-start | bytes 589832 | tf_op jit(solution)/shard_map/ppermute | solution.py:129
  123.3 2.1 collective-permute-done.16
  125.8 2.4 %collective-permute-start.17 = (bf16[256,512]{1,0:T(8,128)(2,1)S(1)}, bf16[256,512]{1,0:T(8,128)(2,1)S(1)}, u32[]{:S(2)}, u32[]{:S(2)}) collective-permute-start(bf16[256,512]{1,0:T(8,128)(2,1)S(1)} %add_convert_fusion.1), channel_id=1, source_target_pairs={{0,1},{1,0},{2,3},{3,2},{4,5},{5,4},{6,7},{7,6},{8,9},{9,8},{10,11... | collective-permute-start | bytes 786440 | tf_op jit(solution)/shard_map/ppermute | solution.py:152
  129.3 6.3 %collective-permute-done.17 = bf16[256,512]{1,0:T(8,128)(2,1)S(1)} collective-permute-done((bf16[256,512]{1,0:T(8,128)(2,1)S(1)}, bf16[256,512]{1,0:T(8,128)(2,1)S(1)}, u32[]{:S(2)}, u32[]{:S(2)}) %collective-permute-start.17) | collective-permute-done | bytes 262176 | tf_op jit(solution)/shard_map/ppermute | solution.py:152
  136.7 12.4 %all-to-all-start = ((bf16[32,16,128]{2,1,0:T(8,128)(2,1)}), bf16[32,16,128]{2,1,0:T(8,128)(2,1)S(1)}, u32[]{:S(2)}, u32[]{:S(2)}) async-start(bf16[32,16,128]{2,1,0:T(8,128)(2,1)} %fusion.29), calls=%async_computation | async-start | bytes 262144 | tf_op jit(solution)/shard_map/all_to_all | solution.py:28
  149.1 2.0 add_convert_fusion.2
  151.1 2.1 collective-permute-start.18
  153.3 1.4 fusion.25
  155.3 5.2 %collective-permute-start.20 = (bf16[1344,256]{1,0:T(8,128)(2,1)}, bf16[1344,256]{1,0:T(8,128)(2,1)S(1)}, u32[]{:S(2)}, u32[]{:S(2)}) collective-permute-start(bf16[1344,256]{1,0:T(8,128)(2,1)} %slice_dynamic-update-slice_fusion), channel_id=1, source_target_pairs={{0,1},{1,0},{2,3},{3,2},{4,5},{5,4},{6,7},{7,6},{8,9},{9,8},{10,11... | collective-permute-start | bytes 2064392 | tf_op jit(solution)/shard_map/ppermute | solution.py:172
  160.5 3.2 %all-to-all-done = bf16[32,16,128]{2,1,0:T(8,128)(2,1)S(1)} async-done(((bf16[32,16,128]{2,1,0:T(8,128)(2,1)}), bf16[32,16,128]{2,1,0:T(8,128)(2,1)S(1)}, u32[]{:S(2)}, u32[]{:S(2)}) %all-to-all-start) | async-done | bytes 131104 | tf_op jit(solution)/shard_map/all_to_all | solution.py:28
  165.1 11.5 %all-to-all-start.1 = ((bf16[32,8,128]{2,1,0:T(8,128)(2,1)}), bf16[32,8,128]{2,1,0:T(8,128)(2,1)}, u32[]{:S(2)}, u32[]{:S(2)}) async-start(bf16[32,8,128]{2,1,0:T(8,128)(2,1)} %bitcast.40), calls=%async_computation.1 | async-start | bytes 131072 | tf_op jit(solution)/shard_map/all_to_all | solution.py:38
  176.7 2.0 fusion.2
  180.6 1.0 copy-done.3
  184.6 1.0 copy-done.11
  189.5 1.0 copy-done.21
  194.5 1.1 copy-done.31
  195.6 1.8 place_outs.1
  197.4 1.3 multiply_reduce_fusion
  199.7 1.9 collective-permute-start.21
  202.3 2.6 %collective-permute-done.21 = bf16[8,256,384]{2,1,0:T(8,128)(2,1)S(1)} collective-permute-done((bf16[8,256,384]{2,1,0:T(8,128)(2,1)S(1)}, bf16[8,256,384]{2,1,0:T(8,128)(2,1)S(1)}, u32[]{:S(2)}, u32[]{:S(2)}) %collective-permute-start.21) | collective-permute-done | bytes 1572896 | tf_op jit(solution)/shard_map/ppermute | solution.py:202
  205.4 26.5 %all_to_all.15 = bf16[8,256,384]{2,1,0:T(8,128)(2,1)S(1)} all-to-all(bf16[8,256,384]{2,1,0:T(8,128)(2,1)S(1)} %add_convert_fusion), channel_id=1, replica_groups={{0,64,128,192,256,320,384,448},{32,96,160,224,288,352,416,480},{1,65,12..., dimensions={0} | all-to-all | bytes 3145728 | tf_op jit(solution)/shard_map/all_to_all | solution.py:206
  (159 shorter events, 35.4 us)
Async XLA Ops:
  2.0 20.5 %collective-permute-start = (bf16[192,1024]{1,0:T(8,128)(2,1)S(1)}, bf16[192,1024]{1,0:T(8,128)(2,1)S(1)}, u32[]{:S(2)}, u32[]{:S(2)}) collective-permute-start(bf16[192,1024]{1,0:T(8,128)(2,1)S(1)} %pad_maximum_fusion.refs_4_.refs_0_), channel_id=1, source_target_pairs={{0,2},{1,3},{2,4},{3,5},{4,6},{5,7},{6,8},{7,9},{8,10},{9,11},{10,... | collective-permute-start | bytes 1179656 | tf_op jit(solution)/shard_map/ppermute | solution.py:125
  5.8 19.2 %collective-permute-start.5 = (bf16[192,1024]{1,0:T(8,128)(2,1)S(1)}, bf16[192,1024]{1,0:T(8,128)(2,1)S(1)}, u32[]{:S(2)}, u32[]{:S(2)}) collective-permute-start(bf16[192,1024]{1,0:T(8,128)(2,1)S(1)} %pad_maximum_fusion.refs_4_.refs_0_), channel_id=1, source_target_pairs={{0,30},{1,31},{2,0},{3,1},{4,2},{5,3},{6,4},{7,5},{8,6},{9,7},{10,... | collective-permute-start | bytes 1179656 | tf_op jit(solution)/shard_map/ppermute | solution.py:126
  22.5 76.8 %copy-start.4 = (bf16[192,1024]{1,0:T(8,128)(2,1)}, bf16[192,1024]{1,0:T(8,128)(2,1)S(1)}, u32[]{:S(2)}) copy-start(bf16[192,1024]{1,0:T(8,128)(2,1)S(1)} %collective-permute-done.refs_3_.refs_1_) | copy-start | bytes 1179652
  22.5 13.4 %collective-permute-start.2 = (bf16[192,1024]{1,0:T(8,128)(2,1)S(1)}, bf16[192,1024]{1,0:T(8,128)(2,1)S(1)}, u32[]{:S(2)}, u32[]{:S(2)}) collective-permute-start(bf16[192,1024]{1,0:T(8,128)(2,1)S(1)} %collective-permute-done.refs_3_.refs_1_), channel_id=1, source_target_pairs={{0,2},{1,3},{2,4},{3,5},{4,6},{5,7},{6,8},{7,9},{8,10},{9,11},{10,... | collective-permute-start | bytes 1179656 | tf_op jit(solution)/shard_map/ppermute | solution.py:125
  25.0 74.2 %copy-start.6 = (bf16[192,1024]{1,0:T(8,128)(2,1)}, bf16[192,1024]{1,0:T(8,128)(2,1)S(1)}, u32[]{:S(2)}) copy-start(bf16[192,1024]{1,0:T(8,128)(2,1)S(1)} %collective-permute-done.5.refs_5_.refs_2_) | copy-start | bytes 1179652
  25.0 12.7 %collective-permute-start.6 = (bf16[192,1024]{1,0:T(8,128)(2,1)S(1)}, bf16[192,1024]{1,0:T(8,128)(2,1)S(1)}, u32[]{:S(2)}, u32[]{:S(2)}) collective-permute-start(bf16[192,1024]{1,0:T(8,128)(2,1)S(1)} %collective-permute-done.5.refs_5_.refs_2_), channel_id=1, source_target_pairs={{0,30},{1,31},{2,0},{3,1},{4,2},{5,3},{6,4},{7,5},{8,6},{9,7},{10,... | collective-permute-start | bytes 1179656 | tf_op jit(solution)/shard_map/ppermute | solution.py:126
  35.8 63.4 %copy-start.8 = (bf16[192,1024]{1,0:T(8,128)(2,1)}, bf16[192,1024]{1,0:T(8,128)(2,1)S(1)}, u32[]{:S(2)}) copy-start(bf16[192,1024]{1,0:T(8,128)(2,1)S(1)} %collective-permute-done.2.refs_2_.refs_3_) | copy-start | bytes 1179652
  35.8 14.8 %collective-permute-start.3 = (bf16[192,1024]{1,0:T(8,128)(2,1)S(1)}, bf16[192,1024]{1,0:T(8,128)(2,1)S(1)}, u32[]{:S(2)}, u32[]{:S(2)}) collective-permute-start(bf16[192,1024]{1,0:T(8,128)(2,1)S(1)} %collective-permute-done.2.refs_2_.refs_3_), channel_id=1, source_target_pairs={{0,2},{1,3},{2,4},{3,5},{4,6},{5,7},{6,8},{7,9},{8,10},{9,11},{10,... | collective-permute-start | bytes 1179656 | tf_op jit(solution)/shard_map/ppermute | solution.py:125
  37.8 61.5 %copy-start.10 = (bf16[192,1024]{1,0:T(8,128)(2,1)}, bf16[192,1024]{1,0:T(8,128)(2,1)S(1)}, u32[]{:S(2)}) copy-start(bf16[192,1024]{1,0:T(8,128)(2,1)S(1)} %collective-permute-done.6.refs_6_.refs_4_) | copy-start | bytes 1179652
  37.8 15.2 %collective-permute-start.7 = (bf16[192,1024]{1,0:T(8,128)(2,1)S(1)}, bf16[192,1024]{1,0:T(8,128)(2,1)S(1)}, u32[]{:S(2)}, u32[]{:S(2)}) collective-permute-start(bf16[192,1024]{1,0:T(8,128)(2,1)S(1)} %collective-permute-done.6.refs_6_.refs_4_), channel_id=1, source_target_pairs={{0,30},{1,31},{2,0},{3,1},{4,2},{5,3},{6,4},{7,5},{8,6},{9,7},{10,... | collective-permute-start | bytes 1179656 | tf_op jit(solution)/shard_map/ppermute | solution.py:126
  48.3 4.3 %copy-start.32 = (bf16[256,6144]{0,1:T(8,128)(2,1)S(1)}, bf16[256,6144]{0,1:T(8,128)(2,1)}, u32[]{:S(2)}) copy-start(bf16[256,6144]{0,1:T(8,128)(2,1)} %copy.40) | copy-start | bytes 9437188
  50.7 48.6 %copy-start.12 = (bf16[192,1024]{1,0:T(8,128)(2,1)}, bf16[192,1024]{1,0:T(8,128)(2,1)S(1)}, u32[]{:S(2)}) copy-start(bf16[192,1024]{1,0:T(8,128)(2,1)S(1)} %collective-permute-done.3.refs_1_.refs_5_) | copy-start | bytes 1179652
  50.7 12.0 %collective-permute-start.4 = (bf16[192,1024]{1,0:T(8,128)(2,1)S(1)}, bf16[192,1024]{1,0:T(8,128)(2,1)S(1)}, u32[]{:S(2)}, u32[]{:S(2)}) collective-permute-start(bf16[192,1024]{1,0:T(8,128)(2,1)S(1)} %collective-permute-done.3.refs_1_.refs_5_), channel_id=1, source_target_pairs={{0,2},{1,3},{2,4},{3,5},{4,6},{5,7},{6,8},{7,9},{8,10},{9,11},{10,... | collective-permute-start | bytes 1179656 | tf_op jit(solution)/shard_map/ppermute | solution.py:125
  53.0 19.3 %copy-start.34 = (bf16[192,256]{1,0:T(8,128)(2,1)S(1)}, bf16[192,256]{1,0:T(8,128)(2,1)}, u32[]{:S(2)}) copy-start(bf16[192,256]{1,0:T(8,128)(2,1)} %param.7) | copy-start | bytes 294916
  53.0 46.3 %copy-start.14 = (bf16[192,1024]{1,0:T(8,128)(2,1)}, bf16[192,1024]{1,0:T(8,128)(2,1)S(1)}, u32[]{:S(2)}) copy-start(bf16[192,1024]{1,0:T(8,128)(2,1)S(1)} %collective-permute-done.7.refs_7_.refs_6_) | copy-start | bytes 1179652
  53.0 12.2 %collective-permute-start.8 = (bf16[192,1024]{1,0:T(8,128)(2,1)S(1)}, bf16[192,1024]{1,0:T(8,128)(2,1)S(1)}, u32[]{:S(2)}, u32[]{:S(2)}) collective-permute-start(bf16[192,1024]{1,0:T(8,128)(2,1)S(1)} %collective-permute-done.7.refs_7_.refs_6_), channel_id=1, source_target_pairs={{0,30},{1,31},{2,0},{3,1},{4,2},{5,3},{6,4},{7,5},{8,6},{9,7},{10,... | collective-permute-start | bytes 1179656 | tf_op jit(solution)/shard_map/ppermute | solution.py:126
  58.6 40.7 %collective-permute-start.1 = (bf16[16,192,256]{2,1,0:T(8,128)(2,1)S(1)}, bf16[16,192,256]{2,1,0:T(8,128)(2,1)S(1)}, u32[]{:S(2)}, u32[]{:S(2)}) collective-permute-start(bf16[16,192,256]{2,1,0:T(8,128)(2,1)S(1)} %get-tuple-element.22), channel_id=1, source_target_pairs={{0,1},{1,0},{2,3},{3,2},{4,5},{5,4},{6,7},{7,6},{8,9},{9,8},{10,11... | collective-permute-start | bytes 4718600 | tf_op jit(solution)/shard_map/ppermute | solution.py:138
  61.1 67.8 %copy-start.36 = (bf16[192,256]{1,0:T(8,128)(2,1)}, bf16[192,256]{1,0:T(8,128)(2,1)S(1)}, u32[]{:S(2)}) copy-start(bf16[192,256]{1,0:T(8,128)(2,1)S(1)} %get-tuple-element.19) | copy-start | bytes 294916
  61.1 67.8 %copy-start.37 = (bf16[192,256]{1,0:T(8,128)(2,1)}, bf16[192,256]{1,0:T(8,128)(2,1)S(1)}, u32[]{:S(2)}) copy-start(bf16[192,256]{1,0:T(8,128)(2,1)S(1)} %get-tuple-element.20) | copy-start | bytes 294916
  61.1 67.8 %copy-start.38 = (bf16[192,256]{1,0:T(8,128)(2,1)}, bf16[192,256]{1,0:T(8,128)(2,1)S(1)}, u32[]{:S(2)}) copy-start(bf16[192,256]{1,0:T(8,128)(2,1)S(1)} %get-tuple-element.21) | copy-start | bytes 294916
  62.6 38.7 %copy-start.16 = (bf16[192,1024]{1,0:T(8,128)(2,1)}, bf16[192,1024]{1,0:T(8,128)(2,1)S(1)}, u32[]{:S(2)}) copy-start(bf16[192,1024]{1,0:T(8,128)(2,1)S(1)} %collective-permute-done.4.refs_0_.refs_7_) | copy-start | bytes 1179652
  62.7 12.2 %collective-permute-start.9 = (bf16[192,1024]{1,0:T(8,128)(2,1)S(1)}, bf16[192,1024]{1,0:T(8,128)(2,1)S(1)}, u32[]{:S(2)}, u32[]{:S(2)}) collective-permute-start(bf16[192,1024]{1,0:T(8,128)(2,1)S(1)} %collective-permute-done.4.refs_0_.refs_7_), channel_id=1, source_target_pairs={{0,2},{1,3},{2,4},{3,5},{4,6},{5,7},{6,8},{7,9},{8,10},{9,11},{10,... | collective-permute-start | bytes 1179656 | tf_op jit(solution)/shard_map/ppermute | solution.py:125
  65.2 36.2 %copy-start.18 = (bf16[192,1024]{1,0:T(8,128)(2,1)}, bf16[192,1024]{1,0:T(8,128)(2,1)S(1)}, u32[]{:S(2)}) copy-start(bf16[192,1024]{1,0:T(8,128)(2,1)S(1)} %collective-permute-done.8.refs_8_) | copy-start | bytes 1179652
  65.2 15.6 %collective-permute-start.11 = (bf16[192,1024]{1,0:T(8,128)(2,1)S(1)}, bf16[192,1024]{1,0:T(8,128)(2,1)S(1)}, u32[]{:S(2)}, u32[]{:S(2)}) collective-permute-start(bf16[192,1024]{1,0:T(8,128)(2,1)S(1)} %collective-permute-done.8.refs_8_), channel_id=1, source_target_pairs={{0,30},{1,31},{2,0},{3,1},{4,2},{5,3},{6,4},{7,5},{8,6},{9,7},{10,... | collective-permute-start | bytes 1179656 | tf_op jit(solution)/shard_map/ppermute | solution.py:126
  74.9 34.9 %copy-start.20 = (bf16[192,1024]{1,0:T(8,128)(2,1)}, bf16[192,1024]{1,0:T(8,128)(2,1)S(1)}, u32[]{:S(2)}) copy-start(bf16[192,1024]{1,0:T(8,128)(2,1)S(1)} %collective-permute-done.9.refs_3_.refs_9_) | copy-start | bytes 1179652
  74.9 26.6 %collective-permute-start.10 = (bf16[192,1024]{1,0:T(8,128)(2,1)S(1)}, bf16[192,1024]{1,0:T(8,128)(2,1)S(1)}, u32[]{:S(2)}, u32[]{:S(2)}) collective-permute-start(bf16[192,1024]{1,0:T(8,128)(2,1)S(1)} %collective-permute-done.9.refs_3_.refs_9_), channel_id=1, source_target_pairs={{0,2},{1,3},{2,4},{3,5},{4,6},{5,7},{6,8},{7,9},{8,10},{9,11},{10,... | collective-permute-start | bytes 1179656 | tf_op jit(solution)/shard_map/ppermute | solution.py:125
  77.4 101.3 %collective-permute-start.19 = (bf16[1728,256]{1,0:T(8,128)(2,1)}, bf16[1728,256]{1,0:T(8,128)(2,1)}, u32[]{:S(2)}, u32[]{:S(2)}) collective-permute-start(bf16[1728,256]{1,0:T(8,128)(2,1)} %slice_dynamic-update-slice_fusion.7), channel_id=1, source_target_pairs={{0,1},{1,0},{2,3},{3,2},{4,5},{5,4},{6,7},{7,6},{8,9},{9,8},{10,11... | collective-permute-start | bytes 2654216 | tf_op jit(solution)/shard_map/ppermute | solution.py:172
  80.9 30.0 %copy-start.22 = (bf16[192,1024]{1,0:T(8,128)(2,1)}, bf16[192,1024]{1,0:T(8,128)(2,1)S(1)}, u32[]{:S(2)}) copy-start(bf16[192,1024]{1,0:T(8,128)(2,1)S(1)} %collective-permute-done.11.refs_4_.refs_10_) | copy-start | bytes 1179652
  80.9 23.2 %collective-permute-start.12 = (bf16[192,1024]{1,0:T(8,128)(2,1)S(1)}, bf16[192,1024]{1,0:T(8,128)(2,1)S(1)}, u32[]{:S(2)}, u32[]{:S(2)}) collective-permute-start(bf16[192,1024]{1,0:T(8,128)(2,1)S(1)} %collective-permute-done.11.refs_4_.refs_10_), channel_id=1, source_target_pairs={{0,30},{1,31},{2,0},{3,1},{4,2},{5,3},{6,4},{7,5},{8,6},{9,7},{10,... | collective-permute-start | bytes 1179656 | tf_op jit(solution)/shard_map/ppermute | solution.py:126
  101.4 24.0 %copy-start.39 = (bf16[192,256]{1,0:T(8,128)(2,1)}, bf16[192,256]{1,0:T(8,128)(2,1)S(1)}, u32[]{:S(2)}) copy-start(bf16[192,256]{1,0:T(8,128)(2,1)S(1)} %get-tuple-element.26) | copy-start | bytes 294916
  101.4 9.4 %copy-start.24 = (bf16[192,1024]{1,0:T(8,128)(2,1)}, bf16[192,1024]{1,0:T(8,128)(2,1)S(1)}, u32[]{:S(2)}) copy-start(bf16[192,1024]{1,0:T(8,128)(2,1)S(1)} %collective-permute-done.10.refs_2_.refs_11_) | copy-start | bytes 1179652
  101.4 13.0 %collective-permute-start.13 = (bf16[192,1024]{1,0:T(8,128)(2,1)S(1)}, bf16[192,1024]{1,0:T(8,128)(2,1)S(1)}, u32[]{:S(2)}, u32[]{:S(2)}) collective-permute-start(bf16[192,1024]{1,0:T(8,128)(2,1)S(1)} %collective-permute-done.10.refs_2_.refs_11_), channel_id=1, source_target_pairs={{0,2},{1,3},{2,4},{3,5},{4,6},{5,7},{6,8},{7,9},{8,10},{9,11},{10,... | collective-permute-start | bytes 1179656 | tf_op jit(solution)/shard_map/ppermute | solution.py:125
  104.0 7.5 %copy-start.26 = (bf16[192,1024]{1,0:T(8,128)(2,1)}, bf16[192,1024]{1,0:T(8,128)(2,1)S(1)}, u32[]{:S(2)}) copy-start(bf16[192,1024]{1,0:T(8,128)(2,1)S(1)} %collective-permute-done.12.refs_5_.refs_12_) | copy-start | bytes 1179652
  104.0 12.5 %collective-permute-start.14 = (bf16[192,1024]{1,0:T(8,128)(2,1)S(1)}, bf16[192,1024]{1,0:T(8,128)(2,1)S(1)}, u32[]{:S(2)}, u32[]{:S(2)}) collective-permute-start(bf16[192,1024]{1,0:T(8,128)(2,1)S(1)} %collective-permute-done.12.refs_5_.refs_12_), channel_id=1, source_target_pairs={{0,30},{1,31},{2,0},{3,1},{4,2},{5,3},{6,4},{7,5},{8,6},{9,7},{10,... | collective-permute-start | bytes 1179656 | tf_op jit(solution)/shard_map/ppermute | solution.py:126
  114.4 8.8 %copy-start = (bf16[192,1024]{1,0:T(8,128)(2,1)}, bf16[192,1024]{1,0:T(8,128)(2,1)S(1)}, u32[]{:S(2)}) copy-start(bf16[192,1024]{1,0:T(8,128)(2,1)S(1)} %collective-permute-done.13.refs_13_) | copy-start | bytes 1179652
  114.4 8.8 %collective-permute-start.15 = (bf16[96,1024]{1,0:T(8,128)(2,1)S(1)}, bf16[96,1024]{1,0:T(8,128)(2,1)S(1)}, u32[]{:S(2)}, u32[]{:S(2)}) collective-permute-start(bf16[96,1024]{1,0:T(8,128)(2,1)S(1)} %slice.180), channel_id=1, source_target_pairs={{0,2},{1,3},{2,4},{3,5},{4,6},{5,7},{6,8},{7,9},{8,10},{9,11},{10,... | collective-permute-start | bytes 589832 | tf_op jit(solution)/shard_map/ppermute | solution.py:128
  116.5 11.7 %copy-start.2 = (bf16[192,1024]{1,0:T(8,128)(2,1)}, bf16[192,1024]{1,0:T(8,128)(2,1)S(1)}, u32[]{:S(2)}) copy-start(bf16[192,1024]{1,0:T(8,128)(2,1)S(1)} %collective-permute-done.14.refs_14_) | copy-start | bytes 1179652
  116.5 8.8 %collective-permute-start.16 = (bf16[96,1024]{1,0:T(8,128)(2,1)S(1)}, bf16[96,1024]{1,0:T(8,128)(2,1)S(1)}, u32[]{:S(2)}, u32[]{:S(2)}) collective-permute-start(bf16[96,1024]{1,0:T(8,128)(2,1)S(1)} %slice.181), channel_id=1, source_target_pairs={{0,30},{1,31},{2,0},{3,1},{4,2},{5,3},{6,4},{7,5},{8,6},{9,7},{10,... | collective-permute-start | bytes 589832 | tf_op jit(solution)/shard_map/ppermute | solution.py:129
  125.4 3.9 %copy-start.35 = (bf16[576,1024]{1,0:T(8,128)(2,1)}, bf16[576,1024]{1,0:T(8,128)(2,1)S(1)}, u32[]{:S(2)}) copy-start(bf16[576,1024]{1,0:T(8,128)(2,1)S(1)} %get-tuple-element.31) | copy-start | bytes 3538948
  125.4 29.3 %copy-start.28 = (bf16[192,1024]{1,0:T(8,128)(2,1)}, bf16[192,1024]{1,0:T(8,128)(2,1)S(1)}, u32[]{:S(2)}) copy-start(bf16[192,1024]{1,0:T(8,128)(2,1)S(1)} %get-tuple-element.30.refs_15_) | copy-start | bytes 1179652
  125.8 9.8 %collective-permute-start.17 = (bf16[256,512]{1,0:T(8,128)(2,1)S(1)}, bf16[256,512]{1,0:T(8,128)(2,1)S(1)}, u32[]{:S(2)}, u32[]{:S(2)}) collective-permute-start(bf16[256,512]{1,0:T(8,128)(2,1)S(1)} %add_convert_fusion.1), channel_id=1, source_target_pairs={{0,1},{1,0},{2,3},{3,2},{4,5},{5,4},{6,7},{7,6},{8,9},{9,8},{10,11... | collective-permute-start | bytes 786440 | tf_op jit(solution)/shard_map/ppermute | solution.py:152
  136.7 27.0 %all-to-all-start = ((bf16[32,16,128]{2,1,0:T(8,128)(2,1)}), bf16[32,16,128]{2,1,0:T(8,128)(2,1)S(1)}, u32[]{:S(2)}, u32[]{:S(2)}) async-start(bf16[32,16,128]{2,1,0:T(8,128)(2,1)} %fusion.29), calls=%async_computation | async-start | bytes 262144 | tf_op jit(solution)/shard_map/all_to_all | solution.py:28
  151.1 25.5 %collective-permute-start.18 = (bf16[256,256]{1,0:T(8,128)(2,1)}, bf16[256,256]{1,0:T(8,128)(2,1)S(1)}, u32[]{:S(2)}, u32[]{:S(2)}) collective-permute-start(bf16[256,256]{1,0:T(8,128)(2,1)} %add_convert_fusion.2), channel_id=1, source_target_pairs={{0,1},{1,0},{2,3},{3,2},{4,5},{5,4},{6,7},{7,6},{8,9},{9,8},{10,11... | collective-permute-start | bytes 393224 | tf_op jit(solution)/shard_map/ppermute | solution.py:152
  155.3 23.4 %collective-permute-start.20 = (bf16[1344,256]{1,0:T(8,128)(2,1)}, bf16[1344,256]{1,0:T(8,128)(2,1)S(1)}, u32[]{:S(2)}, u32[]{:S(2)}) collective-permute-start(bf16[1344,256]{1,0:T(8,128)(2,1)} %slice_dynamic-update-slice_fusion), channel_id=1, source_target_pairs={{0,1},{1,0},{2,3},{3,2},{4,5},{5,4},{6,7},{7,6},{8,9},{9,8},{10,11... | collective-permute-start | bytes 2064392 | tf_op jit(solution)/shard_map/ppermute | solution.py:172
  165.1 32.3 %all-to-all-start.1 = ((bf16[32,8,128]{2,1,0:T(8,128)(2,1)}), bf16[32,8,128]{2,1,0:T(8,128)(2,1)}, u32[]{:S(2)}, u32[]{:S(2)}) async-start(bf16[32,8,128]{2,1,0:T(8,128)(2,1)} %bitcast.40), calls=%async_computation.1 | async-start | bytes 131072 | tf_op jit(solution)/shard_map/all_to_all | solution.py:38
  176.7 2.0 copy-start.33
  176.7 22.0 %copy-start.41 = (f32[256]{0:T(256)S(1)}, f32[256]{0:T(256)}, u32[]{:S(2)}) copy-start(f32[256]{0:T(256)} %param.9) | copy-start | bytes 3076
  199.7 5.3 %collective-permute-start.21 = (bf16[8,256,384]{2,1,0:T(8,128)(2,1)S(1)}, bf16[8,256,384]{2,1,0:T(8,128)(2,1)S(1)}, u32[]{:S(2)}, u32[]{:S(2)}) collective-permute-start(bf16[8,256,384]{2,1,0:T(8,128)(2,1)S(1)} %convolution_convert_fusion), channel_id=1, source_target_pairs={{0,32},{32,0},{64,96},{96,64},{128,160},{160,128},{192,224},{224,1... | collective-permute-start | bytes 4718600 | tf_op jit(solution)/shard_map/ppermute | solution.py:202
  (18 other events, 17.4 us)

commit v4 on v3

--- a/solution.py
+++ b/solution.py
@@ -43,7 +43,7 @@
     return pl.BlockSpec(shape, lambda i: (0,) * len(shape), pipeline_mode=pl.Buffered(1))
 
 
-def place_outs(where, own, own_at, swapped, swapped_at, n_z, shard, width):
+def place_outs(where, own, swapped, batches, n_z, shard, width):
     def kernel(where_ref, *refs):
         out = refs[-1]
         z, half, core = where_ref[0], where_ref[1], where_ref[2]
@@ -54,11 +54,11 @@
             rows = pl.ds(pl.multiple_of(side * shard, shard), shard)
             out[away, lax.div(at, 2), rows, :] = block
 
-        for ref, offset in zip(refs, own_at):
-            place(ref[...], offset, half)
-        for ref, offsets in zip(refs[len(own) :], swapped_at):
+        for i, offsets in enumerate(batches):
             for n, offset in enumerate(offsets):
-                place(ref[n * shard : (n + 1) * shard, :], offset, 1 - half)
+                rows = slice(n * shard, (n + 1) * shard)
+                place(refs[i][rows, :], offset, half)
+                place(refs[len(own) + i][rows, :], offset, 1 - half)
 
     shape = (2, n_z // 2, 2 * shard, width)
     return pl.pallas_call(
@@ -66,12 +66,29 @@
         out_shape=jax.ShapeDtypeStruct(shape, jnp.bfloat16),
         grid=(1,),
         in_specs=[pl.BlockSpec(memory_space=pltpu.SMEM)]
-        + [pl.BlockSpec((shard, width), lambda i: (0, 3), pipeline_mode=pl.Buffered(1))] * len(own)
-        + [whole(a.shape) for a in swapped],
+        + [whole(a.shape) for a in (*own, *swapped)],
         out_specs=whole(shape),
         compiler_params=pltpu.CompilerParams(vmem_limit_bytes=24 << 20),
         name="place_outs",
     )(where, *own, *swapped)
+
+
+def pack_outs(pieces, width):
+    def kernel(*refs):
+        for n, ref in enumerate(refs[:-1]):
+            refs[-1][n * shard : (n + 1) * shard, :] = ref[...]
+
+    shard = pieces[0].shape[0]
+    shape = (len(pieces) * shard, width)
+    return pl.pallas_call(
+        kernel,
+        out_shape=jax.ShapeDtypeStruct(shape, jnp.bfloat16),
+        grid=(1,),
+        in_specs=[pl.BlockSpec((shard, width), lambda i: (0, 3), pipeline_mode=pl.Buffered(1))] * len(pieces),
+        out_specs=whole(shape),
+        compiler_params=pltpu.CompilerParams(vmem_limit_bytes=12 << 20),
+        name="pack_outs",
+    )(*pieces)
 
 
 def project(mine, theirs, sums, pieces, places, width):
@@ -153,10 +170,9 @@
             return keep + sent.astype(f32)
 
         columns = 3 * width
-        sums = ()
-        for group in groups[:2]:
-            places = [(o + last) % n_z for o in group]
-            sums = project(mine, theirs, sums, [pieces[o] for o in group], places, width)
+        known = groups[0] + groups[1]
+        places = [(o + last) % n_z for o in known]
+        sums = project(mine, theirs, (), [pieces[o] for o in known], places, width)
         mine_sum, theirs_sum = sums
         final = jnp.concatenate([pieces[o] for o in groups[2]], axis=0)
         kv_cols, q_cols = slice(0, 2 * width), slice(2 * width, columns)
@@ -165,11 +181,16 @@
         away = theirs_sum[:, q_cols] + times(theirs, final[:, q_cols], groups[2])
         q_proj = join(away, mine_sum[:, q_cols] + times(mine, final[:, q_cols], groups[2]))
 
-        swaps = []
-        batches = (groups[0], groups[1] + groups[2])
-        for batch in batches:
-            joined = jnp.concatenate([pieces[o][:, 3 * width :] for o in batch], axis=0)
-            swaps.append(lax.ppermute(joined, "seq", flip))
+        swaps, packs = [], []
+        first, second = last // 2 - 1, last // 2 + 1
+        batches = (
+            list(range(-first, first + 1)),
+            list(range(-second, -first)) + list(range(first + 1, second + 1)),
+            list(range(1 - last, -second)) + list(range(second + 1, last + 1)),
+        )
+        for n, batch in enumerate(batches):
+            packs.append(pack_outs([pieces[o] for o in batch], width))
+            swaps.append(lax.ppermute(packs[n], "seq", flip))
 
         key = jax.nn.silu(kv_proj[:, :width]).astype(jnp.bfloat16).reshape(rows, heads, hsize)
         value = kv_proj[:, width:].astype(jnp.bfloat16).reshape(rows, heads, hsize)
@@ -179,9 +200,7 @@
         local = jnp.einsum("thd,the->hde", scaled_key, value, preferred_element_type=f32)
         where = jnp.stack([z, half, core]).astype(jnp.int32)
         earlier_state, where = exclusive_state(local, cum[:, -1], n_seq, where)
-        own_at = list(pieces)
-        own = [pieces[o] for o in own_at]
-        outs = place_outs(where, own, own_at, swaps, batches, n_z, shard, width)
+        outs = place_outs(where, packs, swaps, batches, n_z, shard, width)
         out_mine, out_theirs = outs[0], outs[1]
 
         later = jnp.arange(rows)[:, None] >= jnp.arange(rows)[None, :]

time: 235 us -> 232 us (0.987)
  the two profiles are of different devices: /device:TPU:4 before, /device:TPU:1 now
where the time goes in v4:
time: 232 us; the launch traced here: 230 us
  starting transfers between devices  116 us (50%)
  local copies, waits for them, and re-layouts  35.3 us (15%)
  waiting for transfers between devices  25.8 us (11%)
  blocking collectives  24.1 us (10%)
  other arithmetic  11 us (5%)
  matrix products  9.85 us (4%)
  Pallas kernels  7.16 us (3%)
    ppermute x7, starting transfers between devices, layer(): behind = lax.ppermute(behind, 'seq', down)  37.4 us
    unnamed x111, local copies, waits for them, and re-layouts  26.3 us
    all_to_all x1, blocking collectives, layer(): lax.all_to_all(keep.astype(jnp.bfloat16), 'dp', 0, 0, axis_index_groups=g...  24.1 us
    ppermute x7, starting transfers between devices, layer(): ahead = lax.ppermute(ahead, 'seq', up)  15.8 us
    ppermute x1, starting transfers between devices, layer(): taken = lax.ppermute(give.astype(jnp.bfloat16), 'dp', pair_perm(n_dp))  13 us
    ppermute x7, waiting for transfers between devices, layer(): ahead = lax.ppermute(ahead, 'seq', up)  12.4 us
    all_to_all x1, starting transfers between devices, exclusive_state(): got = lax.all_to_all(sent, 'seq', 0, 0, tiled=True)  11.4 us
    all_to_all x1, starting transfers between devices, exclusive_state(): back = lax.all_to_all(earlier, 'seq', 0, 0, tiled=True)  11 us
  transfers between devices with their start and end apart: 25, of which 9 were waited for; matrix products, arithmetic and copies ran while one was open for 14% of the time, Pallas kernels for 3%

profile of v4, /device:TPU:1, one launch (start us, length us, event | category | flops | bytes accessed | tf_op | source)
XLA Modules:
  0.0 229.9 jit_solution(10896441828183639774)
XLA Ops:
  2.0 4.4 %collective-permute-start = (bf16[192,1024]{1,0:T(8,128)(2,1)S(1)}, bf16[192,1024]{1,0:T(8,128)(2,1)S(1)}, u32[]{:S(2)}, u32[]{:S(2)}) collective-permute-start(bf16[192,1024]{1,0:T(8,128)(2,1)S(1)} %pad_maximum_fusion.refs_4_.refs_3_), channel_id=1, source_target_pairs={{0,2},{1,3},{2,4},{3,5},{4,6},{5,7},{6,8},{7,9},{8,10},{9,11},{10,... | collective-permute-start | bytes 1179656 | tf_op jit(solution)/shard_map/ppermute | solution.py:142
  6.3 9.5 %collective-permute-start.5 = (bf16[192,1024]{1,0:T(8,128)(2,1)S(1)}, bf16[192,1024]{1,0:T(8,128)(2,1)S(1)}, u32[]{:S(2)}, u32[]{:S(2)}) collective-permute-start(bf16[192,1024]{1,0:T(8,128)(2,1)S(1)} %pad_maximum_fusion.refs_4_.refs_3_), channel_id=1, source_target_pairs={{0,30},{1,31},{2,0},{3,1},{4,2},{5,3},{6,4},{7,5},{8,6},{9,7},{10,... | collective-permute-start | bytes 1179656 | tf_op jit(solution)/shard_map/ppermute | solution.py:143
  15.8 6.9 %collective-permute-done.refs_3_.refs_2_ = bf16[192,1024]{1,0:T(8,128)(2,1)S(1)} collective-permute-done((bf16[192,1024]{1,0:T(8,128)(2,1)S(1)}, bf16[192,1024]{1,0:T(8,128)(2,1)S(1)}, u32[]{:S(2)}, u32[]{:S(2)}) %collective-permute-start) | collective-permute-done | bytes 393248 | tf_op jit(solution)/shard_map/ppermute | solution.py:142
  22.7 1.9 collective-permute-start.2
  24.6 4.6 %collective-permute-start.6 = (bf16[192,1024]{1,0:T(8,128)(2,1)S(1)}, bf16[192,1024]{1,0:T(8,128)(2,1)S(1)}, u32[]{:S(2)}, u32[]{:S(2)}) collective-permute-start(bf16[192,1024]{1,0:T(8,128)(2,1)S(1)} %collective-permute-done.5.refs_5_.refs_4_), channel_id=1, source_target_pairs={{0,30},{1,31},{2,0},{3,1},{4,2},{5,3},{6,4},{7,5},{8,6},{9,7},{10,... | collective-permute-start | bytes 1179656 | tf_op jit(solution)/shard_map/ppermute | solution.py:143
  29.3 4.7 %copy.40 = bf16[256,6144]{0,1:T(8,128)(2,1)} copy(bf16[256,6144]{1,0:T(8,128)(2,1)} %param.5) | data formatting | bytes 6291456 | tf_op args[0]
  34.0 2.4 %constant_dynamic-update-slice_fusion.1 = bf16[32,2,192,256]{3,2,1,0:T(8,128)(2,1)S(1)} fusion(bf16[16,2,192,256]{3,2,1,0:T(8,128)(2,1)} %bitcast.95), kind=kLoop, calls=%fused_computation.82 | loop fusion | bytes 6291456
  36.4 1.9 collective-permute-start.3
  38.3 4.6 %collective-permute-start.7 = (bf16[192,1024]{1,0:T(8,128)(2,1)S(1)}, bf16[192,1024]{1,0:T(8,128)(2,1)S(1)}, u32[]{:S(2)}, u32[]{:S(2)}) collective-permute-start(bf16[192,1024]{1,0:T(8,128)(2,1)S(1)} %collective-permute-done.6.refs_6_.refs_5_), channel_id=1, source_target_pairs={{0,30},{1,31},{2,0},{3,1},{4,2},{5,3},{6,4},{7,5},{8,6},{9,7},{10,... | collective-permute-start | bytes 1179656 | tf_op jit(solution)/shard_map/ppermute | solution.py:143
  43.3 1.7 dynamic-slice_bitcast_fusion
  45.0 1.5 copy-done.27
  46.5 4.6 %collective-permute-start.1 = (bf16[16,192,256]{2,1,0:T(8,128)(2,1)}, bf16[16,192,256]{2,1,0:T(8,128)(2,1)}, u32[]{:S(2)}, u32[]{:S(2)}) collective-permute-start(bf16[16,192,256]{2,1,0:T(8,128)(2,1)} %get-tuple-element.18), channel_id=1, source_target_pairs={{0,1},{1,0},{2,3},{3,2},{4,5},{5,4},{6,7},{7,6},{8,9},{9,8},{10,11... | collective-permute-start | bytes 4718600 | tf_op jit(solution)/shard_map/ppermute | solution.py:155
  51.1 1.9 collective-permute-start.4
  53.8 4.6 %collective-permute-start.8 = (bf16[192,1024]{1,0:T(8,128)(2,1)S(1)}, bf16[192,1024]{1,0:T(8,128)(2,1)S(1)}, u32[]{:S(2)}, u32[]{:S(2)}) collective-permute-start(bf16[192,1024]{1,0:T(8,128)(2,1)S(1)} %collective-permute-done.7.refs_7_.refs_6_), channel_id=1, source_target_pairs={{0,30},{1,31},{2,0},{3,1},{4,2},{5,3},{6,4},{7,5},{8,6},{9,7},{10,... | collective-permute-start | bytes 1179656 | tf_op jit(solution)/shard_map/ppermute | solution.py:143
  60.1 2.2 collective-permute-done.4.refs_0_.refs_1_
  62.4 1.9 collective-permute-start.9
  65.0 4.6 %collective-permute-start.11 = (bf16[192,1024]{1,0:T(8,128)(2,1)S(1)}, bf16[192,1024]{1,0:T(8,128)(2,1)}, u32[]{:S(2)}, u32[]{:S(2)}) collective-permute-start(bf16[192,1024]{1,0:T(8,128)(2,1)S(1)} %collective-permute-done.8.refs_8_.refs_2_), channel_id=1, source_target_pairs={{0,30},{1,31},{2,0},{3,1},{4,2},{5,3},{6,4},{7,5},{8,6},{9,7},{10,... | collective-permute-start | bytes 1179656 | tf_op jit(solution)/shard_map/ppermute | solution.py:143
  71.0 1.8 collective-permute-done.9.refs_10_.refs_0_
  72.8 1.9 collective-permute-start.10
  74.8 5.0 %collective-permute-start.12 = (bf16[192,1024]{1,0:T(8,128)(2,1)}, bf16[192,1024]{1,0:T(8,128)(2,1)S(1)}, u32[]{:S(2)}, u32[]{:S(2)}) collective-permute-start(bf16[192,1024]{1,0:T(8,128)(2,1)} %collective-permute-done.11.refs_11_.refs_3_), channel_id=1, source_target_pairs={{0,30},{1,31},{2,0},{3,1},{4,2},{5,3},{6,4},{7,5},{8,6},{9,7},{10,... | collective-permute-start | bytes 1179656 | tf_op jit(solution)/shard_map/ppermute | solution.py:143
  80.4 1.3 exponential_bitcast_fusion
  81.7 1.5 collective-permute-done.10.refs_9_.refs_1_
  83.2 1.9 collective-permute-start.13
  85.1 4.6 %collective-permute-start.14 = (bf16[192,1024]{1,0:T(8,128)(2,1)S(1)}, bf16[192,1024]{1,0:T(8,128)(2,1)S(1)}, u32[]{:S(2)}, u32[]{:S(2)}) collective-permute-start(bf16[192,1024]{1,0:T(8,128)(2,1)S(1)} %collective-permute-done.12.refs_12_.refs_2_), channel_id=1, source_target_pairs={{0,30},{1,31},{2,0},{3,1},{4,2},{5,3},{6,4},{7,5},{8,6},{9,7},{10,... | collective-permute-start | bytes 1179656 | tf_op jit(solution)/shard_map/ppermute | solution.py:143
  89.8 1.3 broadcast_in_dim.33
  91.1 1.4 convert_element_type.83
  92.5 1.4 copy.55
  103.6 4.6 %project.1 = (f32[256,768]{1,0:T(8,128)S(1)}, f32[256,768]{1,0:T(8,128)S(1)}) custom-call(bf16[16,192,256]{2,1,0:T(8,128)(2,1)S(1)} %get-tuple-element.19.mine_ref, bf16[16,192,256]{2,1,0:T(8,128)(2,1)} %collective-permute-done.1.theirs_ref, bf16[192,1024]{1,0:T(8,128)(2,1)S(1)} %copy-done.17, bf16[192,1024]{1,0:T(8,128)(2,1)S(1)} %copy-done.13, ...), custom_call_target="tpu_custom_call" | custom-call | tf_op jit(solution)/shard_map/project/pallas_call | solution.py:108
  108.2 1.9 collective-permute-start.15
  110.2 4.6 %collective-permute-start.16 = (bf16[96,1024]{1,0:T(8,128)(2,1)S(1)}, bf16[96,1024]{1,0:T(8,128)(2,1)S(1)}, u32[]{:S(2)}, u32[]{:S(2)}) collective-permute-start(bf16[96,1024]{1,0:T(8,128)(2,1)S(1)} %slice.121), channel_id=1, source_target_pairs={{0,30},{1,31},{2,0},{3,1},{4,2},{5,3},{6,4},{7,5},{8,6},{9,7},{10,... | collective-permute-start | bytes 589832 | tf_op jit(solution)/shard_map/ppermute | solution.py:146
  115.9 1.5 collective-permute-done.16
  117.8 2.0 collective-permute-start.17
  121.1 4.7 %collective-permute-start.19 = (bf16[1344,256]{1,0:T(8,128)(2,1)S(1)}, bf16[1344,256]{1,0:T(8,128)(2,1)}, u32[]{:S(2)}, u32[]{:S(2)}) collective-permute-start(bf16[1344,256]{1,0:T(8,128)(2,1)S(1)} %pack_outs.3.refs_0_), channel_id=1, source_target_pairs={{0,1},{1,0},{2,3},{3,2},{4,5},{5,4},{6,7},{7,6},{8,9},{9,8},{10,11... | collective-permute-start | bytes 2064392 | tf_op jit(solution)/shard_map/ppermute | solution.py:193
  126.8 2.0 collective-permute-start.20
  130.5 1.4 fusion.29
  131.9 11.4 %all-to-all-start = ((bf16[32,16,128]{2,1,0:T(8,128)(2,1)}), bf16[32,16,128]{2,1,0:T(8,128)(2,1)}, u32[]{:S(2)}, u32[]{:S(2)}) async-start(bf16[32,16,128]{2,1,0:T(8,128)(2,1)} %fusion.29), calls=%async_computation | async-start | bytes 262144 | tf_op jit(solution)/shard_map/all_to_all | solution.py:28
  143.3 2.1 add_convert_fusion.2
  145.5 4.7 %collective-permute-start.18 = (bf16[256,256]{1,0:T(8,128)(2,1)}, bf16[256,256]{1,0:T(8,128)(2,1)}, u32[]{:S(2)}, u32[]{:S(2)}) collective-permute-start(bf16[256,256]{1,0:T(8,128)(2,1)} %add_convert_fusion.2), channel_id=1, source_target_pairs={{0,1},{1,0},{2,3},{3,2},{4,5},{5,4},{6,7},{7,6},{8,9},{9,8},{10,11... | collective-permute-start | bytes 393224 | tf_op jit(solution)/shard_map/ppermute | solution.py:169
  151.3 2.3 %collective-permute-start.21 = (bf16[960,256]{1,0:T(8,128)(2,1)S(1)}, bf16[960,256]{1,0:T(8,128)(2,1)S(1)}, u32[]{:S(2)}, u32[]{:S(2)}) collective-permute-start(bf16[960,256]{1,0:T(8,128)(2,1)S(1)} %pack_outs.5.refs_2_), channel_id=1, source_target_pairs={{0,1},{1,0},{2,3},{3,2},{4,5},{5,4},{6,7},{7,6},{8,9},{9,8},{10,11... | collective-permute-start | bytes 1474568 | tf_op jit(solution)/shard_map/ppermute | solution.py:193
  155.0 3.1 %all-to-all-done = bf16[32,16,128]{2,1,0:T(8,128)(2,1)} async-done(((bf16[32,16,128]{2,1,0:T(8,128)(2,1)}), bf16[32,16,128]{2,1,0:T(8,128)(2,1)}, u32[]{:S(2)}, u32[]{:S(2)}) %all-to-all-start) | async-done | bytes 131104 | tf_op jit(solution)/shard_map/all_to_all | solution.py:28
  161.2 11.0 %all-to-all-start.1 = ((bf16[32,8,128]{2,1,0:T(8,128)(2,1)}), bf16[32,8,128]{2,1,0:T(8,128)(2,1)}, u32[]{:S(2)}, u32[]{:S(2)}) async-start(bf16[32,8,128]{2,1,0:T(8,128)(2,1)} %bitcast.40), calls=%async_computation.1 | async-start | bytes 131072 | tf_op jit(solution)/shard_map/all_to_all | solution.py:38
  173.4 2.0 fusion.2
  179.4 1.4 place_outs.1
  180.8 5.4 %all-to-all-done.1 = bf16[32,8,128]{2,1,0:T(8,128)(2,1)} async-done(((bf16[32,8,128]{2,1,0:T(8,128)(2,1)}), bf16[32,8,128]{2,1,0:T(8,128)(2,1)}, u32[]{:S(2)}, u32[]{:S(2)}) %all-to-all-start.1) | async-done | bytes 65568 | tf_op jit(solution)/shard_map/all_to_all | solution.py:38
  186.3 1.3 multiply_reduce_fusion
  188.5 13.0 %collective-permute-start.22 = (bf16[8,256,384]{2,1,0:T(8,128)(2,1)S(1)}, bf16[8,256,384]{2,1,0:T(8,128)(2,1)S(1)}, u32[]{:S(2)}, u32[]{:S(2)}) collective-permute-start(bf16[8,256,384]{2,1,0:T(8,128)(2,1)S(1)} %convolution_convert_fusion), channel_id=1, source_target_pairs={{0,32},{32,0},{64,96},{96,64},{128,160},{160,128},{192,224},{224,1... | collective-permute-start | bytes 4718600 | tf_op jit(solution)/shard_map/ppermute | solution.py:221
  202.2 2.3 collective-permute-done.22
  204.9 24.1 %all_to_all.15 = bf16[8,256,384]{2,1,0:T(8,128)(2,1)S(1)} all-to-all(bf16[8,256,384]{2,1,0:T(8,128)(2,1)S(1)} %add_convert_fusion), channel_id=1, replica_groups={{0,64,128,192,256,320,384,448},{32,96,160,224,288,352,416,480},{1,65,12..., dimensions={0} | all-to-all | bytes 3145728 | tf_op jit(solution)/shard_map/all_to_all | solution.py:225
  (166 shorter events, 36.0 us)
Async XLA Ops:
  2.0 20.8 %collective-permute-start = (bf16[192,1024]{1,0:T(8,128)(2,1)S(1)}, bf16[192,1024]{1,0:T(8,128)(2,1)S(1)}, u32[]{:S(2)}, u32[]{:S(2)}) collective-permute-start(bf16[192,1024]{1,0:T(8,128)(2,1)S(1)} %pad_maximum_fusion.refs_4_.refs_3_), channel_id=1, source_target_pairs={{0,2},{1,3},{2,4},{3,5},{4,6},{5,7},{6,8},{7,9},{8,10},{9,11},{10,... | collective-permute-start | bytes 1179656 | tf_op jit(solution)/shard_map/ppermute | solution.py:142
  6.3 18.3 %collective-permute-start.5 = (bf16[192,1024]{1,0:T(8,128)(2,1)S(1)}, bf16[192,1024]{1,0:T(8,128)(2,1)S(1)}, u32[]{:S(2)}, u32[]{:S(2)}) collective-permute-start(bf16[192,1024]{1,0:T(8,128)(2,1)S(1)} %pad_maximum_fusion.refs_4_.refs_3_), channel_id=1, source_target_pairs={{0,30},{1,31},{2,0},{3,1},{4,2},{5,3},{6,4},{7,5},{8,6},{9,7},{10,... | collective-permute-start | bytes 1179656 | tf_op jit(solution)/shard_map/ppermute | solution.py:143
  22.7 11.2 %copy-start.4 = (bf16[192,1024]{1,0:T(8,128)(2,1)}, bf16[192,1024]{1,0:T(8,128)(2,1)S(1)}, u32[]{:S(2)}) copy-start(bf16[192,1024]{1,0:T(8,128)(2,1)S(1)} %collective-permute-done.refs_3_.refs_2_) | copy-start | bytes 1179652
  22.7 13.6 %collective-permute-start.2 = (bf16[192,1024]{1,0:T(8,128)(2,1)S(1)}, bf16[192,1024]{1,0:T(8,128)(2,1)S(1)}, u32[]{:S(2)}, u32[]{:S(2)}) collective-permute-start(bf16[192,1024]{1,0:T(8,128)(2,1)S(1)} %collective-permute-done.refs_3_.refs_2_), channel_id=1, source_target_pairs={{0,2},{1,3},{2,4},{3,5},{4,6},{5,7},{6,8},{7,9},{8,10},{9,11},{10,... | collective-permute-start | bytes 1179656 | tf_op jit(solution)/shard_map/ppermute | solution.py:142
  24.6 9.3 %copy-start.6 = (bf16[192,1024]{1,0:T(8,128)(2,1)}, bf16[192,1024]{1,0:T(8,128)(2,1)S(1)}, u32[]{:S(2)}) copy-start(bf16[192,1024]{1,0:T(8,128)(2,1)S(1)} %collective-permute-done.5.refs_5_.refs_4_) | copy-start | bytes 1179652
  24.6 13.6 %collective-permute-start.6 = (bf16[192,1024]{1,0:T(8,128)(2,1)S(1)}, bf16[192,1024]{1,0:T(8,128)(2,1)S(1)}, u32[]{:S(2)}, u32[]{:S(2)}) collective-permute-start(bf16[192,1024]{1,0:T(8,128)(2,1)S(1)} %collective-permute-done.5.refs_5_.refs_4_), channel_id=1, source_target_pairs={{0,30},{1,31},{2,0},{3,1},{4,2},{5,3},{6,4},{7,5},{8,6},{9,7},{10,... | collective-permute-start | bytes 1179656 | tf_op jit(solution)/shard_map/ppermute | solution.py:143
  34.0 8.9 %copy-start.26 = (bf16[256,6144]{0,1:T(8,128)(2,1)S(1)}, bf16[256,6144]{0,1:T(8,128)(2,1)}, u32[]{:S(2)}) copy-start(bf16[256,6144]{0,1:T(8,128)(2,1)} %copy.40) | copy-start | bytes 9437188
  36.4 14.8 %collective-permute-start.3 = (bf16[192,1024]{1,0:T(8,128)(2,1)S(1)}, bf16[192,1024]{1,0:T(8,128)(2,1)S(1)}, u32[]{:S(2)}, u32[]{:S(2)}) collective-permute-start(bf16[192,1024]{1,0:T(8,128)(2,1)S(1)} %collective-permute-done.2.refs_2_.refs_1_), channel_id=1, source_target_pairs={{0,2},{1,3},{2,4},{3,5},{4,6},{5,7},{6,8},{7,9},{8,10},{9,11},{10,... | collective-permute-start | bytes 1179656 | tf_op jit(solution)/shard_map/ppermute | solution.py:142
  38.3 15.5 %collective-permute-start.7 = (bf16[192,1024]{1,0:T(8,128)(2,1)S(1)}, bf16[192,1024]{1,0:T(8,128)(2,1)S(1)}, u32[]{:S(2)}, u32[]{:S(2)}) collective-permute-start(bf16[192,1024]{1,0:T(8,128)(2,1)S(1)} %collective-permute-done.6.refs_6_.refs_5_), channel_id=1, source_target_pairs={{0,30},{1,31},{2,0},{3,1},{4,2},{5,3},{6,4},{7,5},{8,6},{9,7},{10,... | collective-permute-start | bytes 1179656 | tf_op jit(solution)/shard_map/ppermute | solution.py:143
  43.3 15.9 %copy-start.48 = (f32[2,256]{1,0:T(2,128)S(1)}, f32[2,256]{1,0:T(2,128)}, u32[]{:S(2)}) copy-start(f32[2,256]{1,0:T(2,128)} %param.8) | copy-start | bytes 6148
  46.5 48.0 %collective-permute-start.1 = (bf16[16,192,256]{2,1,0:T(8,128)(2,1)}, bf16[16,192,256]{2,1,0:T(8,128)(2,1)}, u32[]{:S(2)}, u32[]{:S(2)}) collective-permute-start(bf16[16,192,256]{2,1,0:T(8,128)(2,1)} %get-tuple-element.18), channel_id=1, source_target_pairs={{0,1},{1,0},{2,3},{3,2},{4,5},{5,4},{6,7},{7,6},{8,9},{9,8},{10,11... | collective-permute-start | bytes 4718600 | tf_op jit(solution)/shard_map/ppermute | solution.py:155
  51.1 11.2 %collective-permute-start.4 = (bf16[192,1024]{1,0:T(8,128)(2,1)S(1)}, bf16[192,1024]{1,0:T(8,128)(2,1)S(1)}, u32[]{:S(2)}, u32[]{:S(2)}) collective-permute-start(bf16[192,1024]{1,0:T(8,128)(2,1)S(1)} %collective-permute-done.3.refs_1_.refs_0_), channel_id=1, source_target_pairs={{0,2},{1,3},{2,4},{3,5},{4,6},{5,7},{6,8},{7,9},{8,10},{9,11},{10,... | collective-permute-start | bytes 1179656 | tf_op jit(solution)/shard_map/ppermute | solution.py:142
  53.8 11.2 %collective-permute-start.8 = (bf16[192,1024]{1,0:T(8,128)(2,1)S(1)}, bf16[192,1024]{1,0:T(8,128)(2,1)S(1)}, u32[]{:S(2)}, u32[]{:S(2)}) collective-permute-start(bf16[192,1024]{1,0:T(8,128)(2,1)S(1)} %collective-permute-done.7.refs_7_.refs_6_), channel_id=1, source_target_pairs={{0,30},{1,31},{2,0},{3,1},{4,2},{5,3},{6,4},{7,5},{8,6},{9,7},{10,... | collective-permute-start | bytes 1179656 | tf_op jit(solution)/shard_map/ppermute | solution.py:143
  62.4 10.5 %collective-permute-start.9 = (bf16[192,1024]{1,0:T(8,128)(2,1)S(1)}, bf16[192,1024]{1,0:T(8,128)(2,1)}, u32[]{:S(2)}, u32[]{:S(2)}) collective-permute-start(bf16[192,1024]{1,0:T(8,128)(2,1)S(1)} %collective-permute-done.4.refs_0_.refs_1_), channel_id=1, source_target_pairs={{0,2},{1,3},{2,4},{3,5},{4,6},{5,7},{6,8},{7,9},{8,10},{9,11},{10,... | collective-permute-start | bytes 1179656 | tf_op jit(solution)/shard_map/ppermute | solution.py:142
  65.0 9.7 %collective-permute-start.11 = (bf16[192,1024]{1,0:T(8,128)(2,1)S(1)}, bf16[192,1024]{1,0:T(8,128)(2,1)}, u32[]{:S(2)}, u32[]{:S(2)}) collective-permute-start(bf16[192,1024]{1,0:T(8,128)(2,1)S(1)} %collective-permute-done.8.refs_8_.refs_2_), channel_id=1, source_target_pairs={{0,30},{1,31},{2,0},{3,1},{4,2},{5,3},{6,4},{7,5},{8,6},{9,7},{10,... | collective-permute-start | bytes 1179656 | tf_op jit(solution)/shard_map/ppermute | solution.py:143
  70.6 9.8 %copy-start.49 = (f32[2,1]{0,1:T(1,128)}, f32[2,1]{0,1:T(1,128)S(1)}, u32[]{:S(2)}) copy-start(f32[2,1]{0,1:T(1,128)S(1)} %copy.54) | copy-start | bytes 28
  72.8 10.3 %collective-permute-start.10 = (bf16[192,1024]{1,0:T(8,128)(2,1)}, bf16[192,1024]{1,0:T(8,128)(2,1)S(1)}, u32[]{:S(2)}, u32[]{:S(2)}) collective-permute-start(bf16[192,1024]{1,0:T(8,128)(2,1)} %collective-permute-done.9.refs_10_.refs_0_), channel_id=1, source_target_pairs={{0,2},{1,3},{2,4},{3,5},{4,6},{5,7},{6,8},{7,9},{8,10},{9,11},{10,... | collective-permute-start | bytes 1179656 | tf_op jit(solution)/shard_map/ppermute | solution.py:142
  74.8 10.3 %collective-permute-start.12 = (bf16[192,1024]{1,0:T(8,128)(2,1)}, bf16[192,1024]{1,0:T(8,128)(2,1)S(1)}, u32[]{:S(2)}, u32[]{:S(2)}) collective-permute-start(bf16[192,1024]{1,0:T(8,128)(2,1)} %collective-permute-done.11.refs_11_.refs_3_), channel_id=1, source_target_pairs={{0,30},{1,31},{2,0},{3,1},{4,2},{5,3},{6,4},{7,5},{8,6},{9,7},{10,... | collective-permute-start | bytes 1179656 | tf_op jit(solution)/shard_map/ppermute | solution.py:143
  83.2 25.0 %collective-permute-start.13 = (bf16[192,1024]{1,0:T(8,128)(2,1)S(1)}, bf16[192,1024]{1,0:T(8,128)(2,1)S(1)}, u32[]{:S(2)}, u32[]{:S(2)}) collective-permute-start(bf16[192,1024]{1,0:T(8,128)(2,1)S(1)} %collective-permute-done.10.refs_9_.refs_1_), channel_id=1, source_target_pairs={{0,2},{1,3},{2,4},{3,5},{4,6},{5,7},{6,8},{7,9},{8,10},{9,11},{10,... | collective-permute-start | bytes 1179656 | tf_op jit(solution)/shard_map/ppermute | solution.py:142
  85.1 25.1 %collective-permute-start.14 = (bf16[192,1024]{1,0:T(8,128)(2,1)S(1)}, bf16[192,1024]{1,0:T(8,128)(2,1)S(1)}, u32[]{:S(2)}, u32[]{:S(2)}) collective-permute-start(bf16[192,1024]{1,0:T(8,128)(2,1)S(1)} %collective-permute-done.12.refs_12_.refs_2_), channel_id=1, source_target_pairs={{0,30},{1,31},{2,0},{3,1},{4,2},{5,3},{6,4},{7,5},{8,6},{9,7},{10,... | collective-permute-start | bytes 1179656 | tf_op jit(solution)/shard_map/ppermute | solution.py:143
  95.5 21.9 %copy-start.36 = (bf16[192,256]{1,0:T(8,128)(2,1)}, bf16[192,256]{1,0:T(8,128)(2,1)S(1)}, u32[]{:S(2)}) copy-start(bf16[192,256]{1,0:T(8,128)(2,1)S(1)} %get-tuple-element.20) | copy-start | bytes 294916
  95.5 21.9 %copy-start.38 = (bf16[192,256]{1,0:T(8,128)(2,1)}, bf16[192,256]{1,0:T(8,128)(2,1)S(1)}, u32[]{:S(2)}) copy-start(bf16[192,256]{1,0:T(8,128)(2,1)S(1)} %get-tuple-element.21) | copy-start | bytes 294916
  95.5 21.9 %copy-start.39 = (bf16[192,256]{1,0:T(8,128)(2,1)}, bf16[192,256]{1,0:T(8,128)(2,1)S(1)}, u32[]{:S(2)}) copy-start(bf16[192,256]{1,0:T(8,128)(2,1)S(1)} %get-tuple-element.22) | copy-start | bytes 294916
  108.2 9.2 %copy-start.25 = (f32[256,768]{1,0:T(8,128)}, f32[256,768]{1,0:T(8,128)S(1)}, u32[]{:S(2)}) copy-start(f32[256,768]{1,0:T(8,128)S(1)} %get-tuple-element.12) | copy-start | bytes 2359300
  108.2 21.1 %copy-start.22 = (f32[256,768]{1,0:T(8,128)}, f32[256,768]{1,0:T(8,128)S(1)}, u32[]{:S(2)}) copy-start(f32[256,768]{1,0:T(8,128)S(1)} %get-tuple-element.11) | copy-start | bytes 2359300
  108.2 7.6 %collective-permute-start.15 = (bf16[96,1024]{1,0:T(8,128)(2,1)S(1)}, bf16[96,1024]{1,0:T(8,128)(2,1)S(1)}, u32[]{:S(2)}, u32[]{:S(2)}) collective-permute-start(bf16[96,1024]{1,0:T(8,128)(2,1)S(1)} %slice.120), channel_id=1, source_target_pairs={{0,2},{1,3},{2,4},{3,5},{4,6},{5,7},{6,8},{7,9},{8,10},{9,11},{10,... | collective-permute-start | bytes 589832 | tf_op jit(solution)/shard_map/ppermute | solution.py:145
  110.2 7.2 %collective-permute-start.16 = (bf16[96,1024]{1,0:T(8,128)(2,1)S(1)}, bf16[96,1024]{1,0:T(8,128)(2,1)S(1)}, u32[]{:S(2)}, u32[]{:S(2)}) collective-permute-start(bf16[96,1024]{1,0:T(8,128)(2,1)S(1)} %slice.121), channel_id=1, source_target_pairs={{0,30},{1,31},{2,0},{3,1},{4,2},{5,3},{6,4},{7,5},{8,6},{9,7},{10,... | collective-permute-start | bytes 589832 | tf_op jit(solution)/shard_map/ppermute | solution.py:146
  115.9 13.4 %copy-start.30 = (bf16[96,1024]{1,0:T(8,128)(2,1)}, bf16[96,1024]{1,0:T(8,128)(2,1)S(1)}, u32[]{:S(2)}) copy-start(bf16[96,1024]{1,0:T(8,128)(2,1)S(1)} %collective-permute-done.15) | copy-start | bytes 589828
  117.4 11.9 %copy-start.31 = (bf16[96,1024]{1,0:T(8,128)(2,1)}, bf16[96,1024]{1,0:T(8,128)(2,1)S(1)}, u32[]{:S(2)}) copy-start(bf16[96,1024]{1,0:T(8,128)(2,1)S(1)} %collective-permute-done.16) | copy-start | bytes 589828
  117.4 11.5 %copy-start.35 = (bf16[576,1024]{1,0:T(8,128)(2,1)}, bf16[576,1024]{1,0:T(8,128)(2,1)S(1)}, u32[]{:S(2)}) copy-start(bf16[576,1024]{1,0:T(8,128)(2,1)S(1)} %constant_dynamic-update-slice_fusion.2) | copy-start | bytes 3538948
  117.8 11.5 %collective-permute-start.17 = (bf16[256,512]{1,0:T(8,128)(2,1)S(1)}, bf16[256,512]{1,0:T(8,128)(2,1)S(1)}, u32[]{:S(2)}, u32[]{:S(2)}) collective-permute-start(bf16[256,512]{1,0:T(8,128)(2,1)S(1)} %add_convert_fusion.1), channel_id=1, source_target_pairs={{0,1},{1,0},{2,3},{3,2},{4,5},{5,4},{6,7},{7,6},{8,9},{9,8},{10,11... | collective-permute-start | bytes 786440 | tf_op jit(solution)/shard_map/ppermute | solution.py:169
  121.1 54.3 %collective-permute-start.19 = (bf16[1344,256]{1,0:T(8,128)(2,1)S(1)}, bf16[1344,256]{1,0:T(8,128)(2,1)}, u32[]{:S(2)}, u32[]{:S(2)}) collective-permute-start(bf16[1344,256]{1,0:T(8,128)(2,1)S(1)} %pack_outs.3.refs_0_), channel_id=1, source_target_pairs={{0,1},{1,0},{2,3},{3,2},{4,5},{5,4},{6,7},{7,6},{8,9},{9,8},{10,11... | collective-permute-start | bytes 2064392 | tf_op jit(solution)/shard_map/ppermute | solution.py:193
  126.8 48.6 %collective-permute-start.20 = (bf16[768,256]{1,0:T(8,128)(2,1)S(1)}, bf16[768,256]{1,0:T(8,128)(2,1)}, u32[]{:S(2)}, u32[]{:S(2)}) collective-permute-start(bf16[768,256]{1,0:T(8,128)(2,1)S(1)} %pack_outs.4.refs_1_), channel_id=1, source_target_pairs={{0,1},{1,0},{2,3},{3,2},{4,5},{5,4},{6,7},{7,6},{8,9},{9,8},{10,11... | collective-permute-start | bytes 1179656 | tf_op jit(solution)/shard_map/ppermute | solution.py:193
  129.3 14.0 %copy-start.37 = (bf16[192,256]{1,0:T(8,128)(2,1)S(1)}, bf16[192,256]{1,0:T(8,128)(2,1)}, u32[]{:S(2)}) copy-start(bf16[192,256]{1,0:T(8,128)(2,1)} %copy-done.36) | copy-start | bytes 294916
  129.5 16.0 %copy-start.28 = (f32[256,512]{1,0:T(8,128)}, f32[256,512]{1,0:T(8,128)S(1)}, u32[]{:S(2)}) copy-start(f32[256,512]{1,0:T(8,128)S(1)} %convert_add_fusion) | copy-start | bytes 1572868
  129.7 15.8 %copy-start.32 = (bf16[256,256]{0,1:T(8,128)(2,1)}, bf16[256,256]{0,1:T(8,128)(2,1)S(1)}, u32[]{:S(2)}) copy-start(bf16[256,256]{0,1:T(8,128)(2,1)S(1)} %copy.56) | copy-start | bytes 393220
  131.9 26.3 %all-to-all-start = ((bf16[32,16,128]{2,1,0:T(8,128)(2,1)}), bf16[32,16,128]{2,1,0:T(8,128)(2,1)}, u32[]{:S(2)}, u32[]{:S(2)}) async-start(bf16[32,16,128]{2,1,0:T(8,128)(2,1)} %fusion.29), calls=%async_computation | async-start | bytes 262144 | tf_op jit(solution)/shard_map/all_to_all | solution.py:28
  145.4 8.3 %copy-start.43 = (bf16[192,256]{1,0:T(8,128)(2,1)S(1)}, bf16[192,256]{1,0:T(8,128)(2,1)}, u32[]{:S(2)}) copy-start(bf16[192,256]{1,0:T(8,128)(2,1)} %copy-done.42) | copy-start | bytes 294916
  145.5 26.7 %collective-permute-start.18 = (bf16[256,256]{1,0:T(8,128)(2,1)}, bf16[256,256]{1,0:T(8,128)(2,1)}, u32[]{:S(2)}, u32[]{:S(2)}) collective-permute-start(bf16[256,256]{1,0:T(8,128)(2,1)} %add_convert_fusion.2), channel_id=1, source_target_pairs={{0,1},{1,0},{2,3},{3,2},{4,5},{5,4},{6,7},{7,6},{8,9},{9,8},{10,11... | collective-permute-start | bytes 393224 | tf_op jit(solution)/shard_map/ppermute | solution.py:169
  151.3 24.1 %copy-start.2 = (bf16[960,256]{1,0:T(8,128)(2,1)}, bf16[960,256]{1,0:T(8,128)(2,1)S(1)}, u32[]{:S(2)}) copy-start(bf16[960,256]{1,0:T(8,128)(2,1)S(1)} %pack_outs.5.refs_2_) | copy-start | bytes 1474564
  151.3 22.0 %copy-start.29 = (f32[256,512]{1,0:T(8,128)S(1)}, f32[256,512]{1,0:T(8,128)}, u32[]{:S(2)}) copy-start(f32[256,512]{1,0:T(8,128)} %copy-done.28) | copy-start | bytes 1572868
  151.3 22.0 %copy-start.33 = (bf16[256,256]{0,1:T(8,128)(2,1)S(1)}, bf16[256,256]{0,1:T(8,128)(2,1)}, u32[]{:S(2)}) copy-start(bf16[256,256]{0,1:T(8,128)(2,1)} %copy-done.32) | copy-start | bytes 393220
  151.3 22.0 %copy-start.47 = (f32[1,2,2,128]{3,1,2,0:T(2,128)S(1)}, f32[1,2,2,128]{3,1,2,0:T(2,128)}, u32[]{:S(2)}) copy-start(f32[1,2,2,128]{3,1,2,0:T(2,128)} %copy-done.46) | copy-start | bytes 6148
  151.3 24.1 %collective-permute-start.21 = (bf16[960,256]{1,0:T(8,128)(2,1)S(1)}, bf16[960,256]{1,0:T(8,128)(2,1)S(1)}, u32[]{:S(2)}, u32[]{:S(2)}) collective-permute-start(bf16[960,256]{1,0:T(8,128)(2,1)S(1)} %pack_outs.5.refs_2_), channel_id=1, source_target_pairs={{0,1},{1,0},{2,3},{3,2},{4,5},{5,4},{6,7},{7,6},{8,9},{9,8},{10,11... | collective-permute-start | bytes 1474568 | tf_op jit(solution)/shard_map/ppermute | solution.py:193
  155.0 21.2 %copy-start.21 = (bf16[768,256]{1,0:T(8,128)(2,1)S(1)}, bf16[768,256]{1,0:T(8,128)(2,1)}, u32[]{:S(2)}) copy-start(bf16[768,256]{1,0:T(8,128)(2,1)} %copy-done.20) | copy-start | bytes 1179652
  161.2 25.1 %all-to-all-start.1 = ((bf16[32,8,128]{2,1,0:T(8,128)(2,1)}), bf16[32,8,128]{2,1,0:T(8,128)(2,1)}, u32[]{:S(2)}, u32[]{:S(2)}) async-start(bf16[32,8,128]{2,1,0:T(8,128)(2,1)} %bitcast.40), calls=%async_computation.1 | async-start | bytes 131072 | tf_op jit(solution)/shard_map/all_to_all | solution.py:38
  173.4 14.2 %copy-start.50 = (f32[256]{0:T(256)S(1)}, f32[256]{0:T(256)}, u32[]{:S(2)}) copy-start(f32[256]{0:T(256)} %param.9) | copy-start | bytes 3076
  188.5 16.0 %collective-permute-start.22 = (bf16[8,256,384]{2,1,0:T(8,128)(2,1)S(1)}, bf16[8,256,384]{2,1,0:T(8,128)(2,1)S(1)}, u32[]{:S(2)}, u32[]{:S(2)}) collective-permute-start(bf16[8,256,384]{2,1,0:T(8,128)(2,1)S(1)} %convolution_convert_fusion), channel_id=1, source_target_pairs={{0,32},{32,0},{64,96},{96,64},{128,160},{160,128},{192,224},{224,1... | collective-permute-start | bytes 4718600 | tf_op jit(solution)/shard_map/ppermute | solution.py:221
  (28 other events, 84.1 us)

commit v5 on v4

--- a/solution.py
+++ b/solution.py
@@ -39,6 +39,10 @@
     return back.reshape(heads, hsize, hsize), where
 
 
+def in_hbm(x):
+    return pltpu.with_memory_space_constraint(x, pltpu.HBM)
+
+
 def whole(shape):
     return pl.BlockSpec(shape, lambda i: (0,) * len(shape), pipeline_mode=pl.Buffered(1))
 
@@ -68,7 +72,7 @@
         in_specs=[pl.BlockSpec(memory_space=pltpu.SMEM)]
         + [whole(a.shape) for a in (*own, *swapped)],
         out_specs=whole(shape),
-        compiler_params=pltpu.CompilerParams(vmem_limit_bytes=24 << 20),
+        compiler_params=pltpu.CompilerParams(vmem_limit_bytes=12 << 20),
         name="place_outs",
     )(where, *own, *swapped)
 
@@ -86,36 +90,43 @@
         grid=(1,),
         in_specs=[pl.BlockSpec((shard, width), lambda i: (0, 3), pipeline_mode=pl.Buffered(1))] * len(pieces),
         out_specs=whole(shape),
-        compiler_params=pltpu.CompilerParams(vmem_limit_bytes=12 << 20),
+        compiler_params=pltpu.CompilerParams(vmem_limit_bytes=6 << 20),
         name="pack_outs",
-    )(*pieces)
-
-
-def project(mine, theirs, sums, pieces, places, width):
-    def kernel(mine_ref, theirs_ref, *refs):
-        weights, outs = refs[len(sums) : len(sums) + len(pieces)], refs[-2:]
-        for n, (tok, out) in enumerate(zip((mine_ref, theirs_ref), outs)):
-            total = refs[n][...] if sums else None
-            for weight, place in zip(weights, places):
+    )(*[in_hbm(p) for p in pieces])
+
+
+def project(where, toks, sums, blocks, jobs, n_z, columns):
+    def kernel(where_ref, *refs):
+        tok_refs, refs = refs[: len(toks)], refs[len(toks) :]
+        sum_refs, refs = refs[: len(sums)], refs[len(sums) :]
+        for (tok, base, lo, hi, kind), out in zip(jobs, refs[len(blocks) :]):
+            total = None if base is None else sum_refs[base][:, lo:hi]
+            for (_, offset, row, count), weight in zip(blocks, refs):
+                at = lax.rem(where_ref[0] + (offset + n_z), n_z)
                 part = lax.dot_general(
-                    tok[place], weight[...], (((0,), (0,)), ((), ())), preferred_element_type=jnp.float32
+                    tok_refs[tok][at, row : row + count, :],
+                    weight[:, lo:hi],
+                    (((0,), (0,)), ((), ())),
+                    preferred_element_type=jnp.float32,
                 )
                 total = part if total is None else total + part
-            out[...] = total
-
-    shard = pieces[0].shape[0]
-    shape = (mine.shape[2], 3 * width)
+            out[...] = total.astype(kind)
+
+    rows = toks[0].shape[2]
     return pl.pallas_call(
         kernel,
-        out_shape=[jax.ShapeDtypeStruct(shape, jnp.float32)] * 2,
+        out_shape=[jax.ShapeDtypeStruct((rows, hi - lo), kind) for _, _, lo, hi, kind in jobs],
         grid=(1,),
-        in_specs=[whole(mine.shape)] * 2
-        + [whole(shape)] * len(sums)
-        + [pl.BlockSpec((shard, 3 * width), lambda i: (0, 0), pipeline_mode=pl.Buffered(1))] * len(pieces),
-        out_specs=[whole(shape)] * 2,
-        compiler_params=pltpu.CompilerParams(vmem_limit_bytes=32 << 20),
+        in_specs=[pl.BlockSpec(memory_space=pltpu.SMEM)]
+        + [whole(a.shape) for a in (*toks, *sums)]
+        + [
+            pl.BlockSpec((count, columns), lambda i: (0, 0), pipeline_mode=pl.Buffered(1))
+            for _, _, _, count in blocks
+        ],
+        out_specs=[whole((rows, hi - lo)) for _, _, lo, hi, _ in jobs],
+        compiler_params=pltpu.CompilerParams(vmem_limit_bytes=16 << 20),
         name="project",
-    )(mine, theirs, *sums, *pieces)
+    )(where, *toks, *sums, *[block[0] if sums else in_hbm(block[0]) for block in blocks])
 
 
 def make_body(n_seq, n_dp):
@@ -148,8 +159,6 @@
 
         by_z = tokens.T.reshape(n_z, 2, shard, rows)
         by_z, _ = lax.optimization_barrier((by_z, pieces[-1]))
-        by_z = jnp.concatenate([by_z, by_z], axis=0)
-        by_z = lax.dynamic_slice_in_dim(by_z, (z + last) % n_z, n_z, axis=0)
         mine = lax.dynamic_index_in_dim(by_z, half, 1, False)
         theirs = lax.dynamic_index_in_dim(by_z, 1 - half, 1, False)
         theirs = lax.ppermute(theirs, "seq", flip)
@@ -161,25 +170,21 @@
             [1 - last, last - 1, last],
         ]
 
-        def times(toks, weight, group):
-            tok = jnp.concatenate([toks[(o + last) % n_z] for o in group], axis=0)
-            return lax.dot_general(tok, weight, (((0,), (0,)), ((), ())), preferred_element_type=f32)
-
-        def join(partial, keep):
-            sent = lax.ppermute(partial.astype(jnp.bfloat16), "seq", flip)
-            return keep + sent.astype(f32)
-
         columns = 3 * width
-        known = groups[0] + groups[1]
-        places = [(o + last) % n_z for o in known]
-        sums = project(mine, theirs, (), [pieces[o] for o in known], places, width)
-        mine_sum, theirs_sum = sums
-        final = jnp.concatenate([pieces[o] for o in groups[2]], axis=0)
-        kv_cols, q_cols = slice(0, 2 * width), slice(2 * width, columns)
-        away = theirs_sum[:, kv_cols] + times(theirs, final[:, kv_cols], groups[2])
-        kv_proj = join(away, mine_sum[:, kv_cols] + times(mine, final[:, kv_cols], groups[2]))
-        away = theirs_sum[:, q_cols] + times(theirs, final[:, q_cols], groups[2])
-        q_proj = join(away, mine_sum[:, q_cols] + times(mine, final[:, q_cols], groups[2]))
+        where = jnp.stack([z, half, core]).astype(jnp.int32)
+        toks = (mine, theirs)
+        known = [(pieces[o], o, 0, shard) for o in groups[0] + groups[1]]
+        final = [(pieces[o], o, 0, shard) for o in groups[2][:2]]
+        final += [(top, last, 0, shard // 2), (bottom, last, shard // 2, shard // 2)]
+        b16, kv = jnp.bfloat16, 2 * width
+        jobs = [(0, None, 0, columns, f32), (1, None, 0, columns, f32)]
+        sums = project(where, toks, (), known, jobs, n_z, columns)
+        (away,) = project(where, (theirs,), sums[1:], final, [(0, 0, 0, kv, b16)], n_z, columns)
+        sent = lax.ppermute(away, "seq", flip)
+        jobs = [(0, 0, 0, kv, f32), (0, 0, kv, columns, f32), (1, 1, kv, columns, b16)]
+        kept_kv, kept_q, away = project(where, toks, sums, final, jobs, n_z, columns)
+        kv_proj = kept_kv + sent.astype(f32)
+        q_proj = kept_q + lax.ppermute(away, "seq", flip).astype(f32)
 
         swaps, packs = [], []
         first, second = last // 2 - 1, last // 2 + 1
@@ -198,7 +203,6 @@
         cum = jnp.cumsum(log_decay, axis=1)
         scaled_key = (key.astype(f32) * jnp.exp(cum[:, -1:] - cum).T[:, :, None]).astype(jnp.bfloat16)
         local = jnp.einsum("thd,the->hde", scaled_key, value, preferred_element_type=f32)
-        where = jnp.stack([z, half, core]).astype(jnp.int32)
         earlier_state, where = exclusive_state(local, cum[:, -1], n_seq, where)
         outs = place_outs(where, packs, swaps, batches, n_z, shard, width)
         out_mine, out_theirs = outs[0], outs[1]

time: 232 us -> 232 us (level)
  local copies, waits for them, and re-layouts: 35.3 us -> 26.5 us
  Pallas kernels: 7.16 us -> 13.3 us
  waiting for transfers between devices: 25.8 us -> 31.9 us
  matrix products: 9.85 us -> 5.35 us
    ppermute x7, waiting for transfers between devices: 12.4 us -> 26.8 us  [layer(): ahead = lax.ppermute(ahead, 'seq', up)]
    unnamed x111 -> x81, local copies, waits for them, and re-layouts: 26.3 us -> 19.2 us
    pallas_call x1 -> x3, Pallas kernels: 4.58 us -> 9.03 us  [project(): pl.pallas_call(kernel, out_shape=[jax.ShapeDtypeStruct((rows, hi - lo), k...]
    dot_general x4 -> x0, matrix products: 4.14 us -> none  [times(): lax.dot_general(tok, weight, (((0,), (0,)), ((), ())), preferred_element_...]
    all_to_all x1, waiting for transfers between devices: 5.45 us -> 1.52 us  [exclusive_state(): back = lax.all_to_all(earlier, 'seq', 0, 0, tiled=True)]
    all_to_all x1, waiting for transfers between devices: 3.14 us -> 0.01 us  [exclusive_state(): got = lax.all_to_all(sent, 'seq', 0, 0, tiled=True)]
    all_to_all x1, starting transfers between devices: 11 us -> 14.1 us  [exclusive_state(): back = lax.all_to_all(earlier, 'seq', 0, 0, tiled=True)]
    ppermute x2, starting transfers between devices: 6.75 us -> 4.14 us  [the longest x1 2.22 us: layer(): q_proj = kept_q + lax.ppermute(away, 'seq', flip).astype(f32)]
  transfers between devices with their start and end apart: 25 -> 25, of which waited for: 9 -> 9; matrix products, arithmetic and copies ran while one was open for 14% -> 10% of each run, Pallas kernels for 3% -> 5%
where the time goes in v5:
time: 232 us; the launch traced here: 230 us
  starting transfers between devices  118 us (51%)
  waiting for transfers between devices  31.9 us (14%)
  local copies, waits for them, and re-layouts  26.5 us (11%)
  blocking collectives  24.5 us (11%)
  Pallas kernels  13.3 us (6%)
  other arithmetic  10 us (4%)
  matrix products  5.35 us (2%)
    ppermute x7, starting transfers between devices, layer(): behind = lax.ppermute(behind, 'seq', down)  37.2 us
    ppermute x7, waiting for transfers between devices, layer(): ahead = lax.ppermute(ahead, 'seq', up)  26.8 us
    all_to_all x1, blocking collectives, layer(): lax.all_to_all(keep.astype(jnp.bfloat16), 'dp', 0, 0, axis_index_groups=g...  24.5 us
    unnamed x81, local copies, waits for them, and re-layouts  19.2 us
    ppermute x7, starting transfers between devices, layer(): ahead = lax.ppermute(ahead, 'seq', up)  15.8 us
    all_to_all x1, starting transfers between devices, exclusive_state(): back = lax.all_to_all(earlier, 'seq', 0, 0, tiled=True)  14.1 us
    ppermute x1, starting transfers between devices, layer(): taken = lax.ppermute(give.astype(jnp.bfloat16), 'dp', pair_perm(n_dp))  12.9 us
    ppermute x3, starting transfers between devices, layer(): swaps.append(lax.ppermute(packs[n], 'seq', flip))  11.6 us
  transfers between devices with their start and end apart: 25, of which 9 were waited for; matrix products, arithmetic and copies ran while one was open for 10% of the time, Pallas kernels for 5%

profile of v5, /device:TPU:1, one launch (start us, length us, event | category | flops | bytes accessed | tf_op | source)
XLA Modules:
  0.0 230.0 jit_solution(9859088440555403947)
XLA Ops:
  2.0 4.4 %collective-permute-start = (bf16[192,1024]{1,0:T(8,128)(2,1)S(1)}, bf16[192,1024]{1,0:T(8,128)(2,1)S(1)}, u32[]{:S(2)}, u32[]{:S(2)}) collective-permute-start(bf16[192,1024]{1,0:T(8,128)(2,1)S(1)} %pad_maximum_fusion.refs_6_.refs_3_), channel_id=1, source_target_pairs={{0,2},{1,3},{2,4},{3,5},{4,6},{5,7},{6,8},{7,9},{8,10},{9,11},{10,... | collective-permute-start | bytes 1179656 | tf_op jit(solution)/shard_map/ppermute | solution.py:153
  6.3 9.5 %collective-permute-start.5 = (bf16[192,1024]{1,0:T(8,128)(2,1)S(1)}, bf16[192,1024]{1,0:T(8,128)(2,1)S(1)}, u32[]{:S(2)}, u32[]{:S(2)}) collective-permute-start(bf16[192,1024]{1,0:T(8,128)(2,1)S(1)} %pad_maximum_fusion.refs_6_.refs_3_), channel_id=1, source_target_pairs={{0,30},{1,31},{2,0},{3,1},{4,2},{5,3},{6,4},{7,5},{8,6},{9,7},{10,... | collective-permute-start | bytes 1179656 | tf_op jit(solution)/shard_map/ppermute | solution.py:154
  15.9 6.9 %collective-permute-done.refs_5_.refs_2_ = bf16[192,1024]{1,0:T(8,128)(2,1)S(1)} collective-permute-done((bf16[192,1024]{1,0:T(8,128)(2,1)S(1)}, bf16[192,1024]{1,0:T(8,128)(2,1)S(1)}, u32[]{:S(2)}, u32[]{:S(2)}) %collective-permute-start) | collective-permute-done | bytes 393248 | tf_op jit(solution)/shard_map/ppermute | solution.py:153
  22.7 1.9 collective-permute-start.2
  24.7 4.6 %collective-permute-start.6 = (bf16[192,1024]{1,0:T(8,128)(2,1)S(1)}, bf16[192,1024]{1,0:T(8,128)(2,1)S(1)}, u32[]{:S(2)}, u32[]{:S(2)}) collective-permute-start(bf16[192,1024]{1,0:T(8,128)(2,1)S(1)} %collective-permute-done.5.refs_7_.refs_4_), channel_id=1, source_target_pairs={{0,30},{1,31},{2,0},{3,1},{4,2},{5,3},{6,4},{7,5},{8,6},{9,7},{10,... | collective-permute-start | bytes 1179656 | tf_op jit(solution)/shard_map/ppermute | solution.py:154
  29.2 6.0 %collective-permute-done.2.refs_4_.refs_1_ = bf16[192,1024]{1,0:T(8,128)(2,1)S(1)} collective-permute-done((bf16[192,1024]{1,0:T(8,128)(2,1)S(1)}, bf16[192,1024]{1,0:T(8,128)(2,1)S(1)}, u32[]{:S(2)}, u32[]{:S(2)}) %collective-permute-start.2) | collective-permute-done | bytes 393248 | tf_op jit(solution)/shard_map/ppermute | solution.py:153
  35.2 1.9 collective-permute-start.3
  37.2 4.6 %collective-permute-start.7 = (bf16[192,1024]{1,0:T(8,128)(2,1)S(1)}, bf16[192,1024]{1,0:T(8,128)(2,1)}, u32[]{:S(2)}, u32[]{:S(2)}) collective-permute-start(bf16[192,1024]{1,0:T(8,128)(2,1)S(1)} %collective-permute-done.6.refs_8_.refs_5_), channel_id=1, source_target_pairs={{0,30},{1,31},{2,0},{3,1},{4,2},{5,3},{6,4},{7,5},{8,6},{9,7},{10,... | collective-permute-start | bytes 1179656 | tf_op jit(solution)/shard_map/ppermute | solution.py:154
  41.8 5.1 %collective-permute-done.3.refs_3_.refs_0_ = bf16[192,1024]{1,0:T(8,128)(2,1)S(1)} collective-permute-done((bf16[192,1024]{1,0:T(8,128)(2,1)S(1)}, bf16[192,1024]{1,0:T(8,128)(2,1)S(1)}, u32[]{:S(2)}, u32[]{:S(2)}) %collective-permute-start.3) | collective-permute-done | bytes 393248 | tf_op jit(solution)/shard_map/ppermute | solution.py:153
  46.9 1.9 collective-permute-start.4
  48.8 4.6 %collective-permute-start.8 = (bf16[192,1024]{1,0:T(8,128)(2,1)}, bf16[192,1024]{1,0:T(8,128)(2,1)}, u32[]{:S(2)}, u32[]{:S(2)}) collective-permute-start(bf16[192,1024]{1,0:T(8,128)(2,1)} %collective-permute-done.7.refs_9_.refs_6_), channel_id=1, source_target_pairs={{0,30},{1,31},{2,0},{3,1},{4,2},{5,3},{6,4},{7,5},{8,6},{9,7},{10,... | collective-permute-start | bytes 1179656 | tf_op jit(solution)/shard_map/ppermute | solution.py:154
  53.4 4.6 %copy.35 = bf16[256,6144]{0,1:T(8,128)(2,1)} copy(bf16[256,6144]{1,0:T(8,128)(2,1)} %param.5) | data formatting | bytes 6291456 | tf_op args[0]
  58.1 3.3 %dynamic-slice_bitcast_fusion = (bf16[16,192,256]{2,1,0:T(8,128)(2,1)}, bf16[16,192,256]{2,1,0:T(8,128)(2,1)S(1)}) fusion(bf16[16,2,192,256]{3,2,1,0:T(8,128)(2,1)} %bitcast.88, s32[]{:T(128)S(6)} %select_n.38, s32[]{:T(128)S(6)} %select_n.37), kind=kLoop, calls=%fused_computation.5 | loop fusion | bytes 6291464 | tf_op jit(solution)/shard_map/jit(dynamic_index_in_dim)/squeeze | solution.py:163
  61.4 4.6 %collective-permute-start.1 = (bf16[16,192,256]{2,1,0:T(8,128)(2,1)}, bf16[16,192,256]{2,1,0:T(8,128)(2,1)S(1)}, u32[]{:S(2)}, u32[]{:S(2)}) collective-permute-start(bf16[16,192,256]{2,1,0:T(8,128)(2,1)} %get-tuple-element.21), channel_id=1, source_target_pairs={{0,1},{1,0},{2,3},{3,2},{4,5},{5,4},{6,7},{7,6},{8,9},{9,8},{10,11... | collective-permute-start | bytes 4718600 | tf_op jit(solution)/shard_map/ppermute | solution.py:164
  66.1 1.9 collective-permute-start.9
  68.0 4.6 %collective-permute-start.11 = (bf16[192,1024]{1,0:T(8,128)(2,1)}, bf16[192,1024]{1,0:T(8,128)(2,1)}, u32[]{:S(2)}, u32[]{:S(2)}) collective-permute-start(bf16[192,1024]{1,0:T(8,128)(2,1)} %collective-permute-done.8.refs_10_.refs_2_), channel_id=1, source_target_pairs={{0,30},{1,31},{2,0},{3,1},{4,2},{5,3},{6,4},{7,5},{8,6},{9,7},{10,... | collective-permute-start | bytes 1179656 | tf_op jit(solution)/shard_map/ppermute | solution.py:154
  72.6 3.7 %collective-permute-done.9.refs_12_.refs_0_ = bf16[192,1024]{1,0:T(8,128)(2,1)S(1)} collective-permute-done((bf16[192,1024]{1,0:T(8,128)(2,1)}, bf16[192,1024]{1,0:T(8,128)(2,1)S(1)}, u32[]{:S(2)}, u32[]{:S(2)}) %collective-permute-start.9) | collective-permute-done | bytes 393248 | tf_op jit(solution)/shard_map/ppermute | solution.py:153
  76.3 1.9 collective-permute-start.10
  78.2 4.6 %collective-permute-start.12 = (bf16[192,1024]{1,0:T(8,128)(2,1)}, bf16[192,1024]{1,0:T(8,128)(2,1)}, u32[]{:S(2)}, u32[]{:S(2)}) collective-permute-start(bf16[192,1024]{1,0:T(8,128)(2,1)} %collective-permute-done.11.refs_13_.refs_3_), channel_id=1, source_target_pairs={{0,30},{1,31},{2,0},{3,1},{4,2},{5,3},{6,4},{7,5},{8,6},{9,7},{10,... | collective-permute-start | bytes 1179656 | tf_op jit(solution)/shard_map/ppermute | solution.py:154
  83.5 2.9 %collective-permute-done.10.refs_11_.refs_1_ = bf16[192,1024]{1,0:T(8,128)(2,1)} collective-permute-done((bf16[192,1024]{1,0:T(8,128)(2,1)S(1)}, bf16[192,1024]{1,0:T(8,128)(2,1)}, u32[]{:S(2)}, u32[]{:S(2)}) %collective-permute-start.10) | collective-permute-done | bytes 393248 | tf_op jit(solution)/shard_map/ppermute | solution.py:153
  86.3 1.9 collective-permute-start.13
  88.2 4.8 %collective-permute-start.14 = (bf16[192,1024]{1,0:T(8,128)(2,1)}, bf16[192,1024]{1,0:T(8,128)(2,1)}, u32[]{:S(2)}, u32[]{:S(2)}) collective-permute-start(bf16[192,1024]{1,0:T(8,128)(2,1)} %collective-permute-done.12.refs_14_.refs_2_), channel_id=1, source_target_pairs={{0,30},{1,31},{2,0},{3,1},{4,2},{5,3},{6,4},{7,5},{8,6},{9,7},{10,... | collective-permute-start | bytes 1179656 | tf_op jit(solution)/shard_map/ppermute | solution.py:154
  94.3 2.3 collective-permute-done.13.refs_4_.refs_2_.refs_0_
  96.6 1.9 collective-permute-start.15
  99.5 4.8 %collective-permute-start.16 = (bf16[96,1024]{1,0:T(8,128)(2,1)S(1)}, bf16[96,1024]{1,0:T(8,128)(2,1)S(1)}, u32[]{:S(2)}, u32[]{:S(2)}) collective-permute-start(bf16[96,1024]{1,0:T(8,128)(2,1)S(1)} %slice.62), channel_id=1, source_target_pairs={{0,30},{1,31},{2,0},{3,1},{4,2},{5,3},{6,4},{7,5},{8,6},{9,7},{10,... | collective-permute-start | bytes 589832 | tf_op jit(solution)/shard_map/ppermute | solution.py:157
  104.9 4.9 %project.3 = (f32[256,768]{1,0:T(8,128)S(1)}, f32[256,768]{1,0:T(8,128)S(1)}) custom-call(s32[3]{0:T(128)S(1)} %pad_add_fusion.where_ref, bf16[16,192,256]{2,1,0:T(8,128)(2,1)S(1)} %get-tuple-element.22.refs_0_, bf16[16,192,256]{2,1,0:T(8,128)(2,1)S(1)} %collective-permute-done.1.refs_1_.refs_0_, bf16[192,1024]{1,0:T(8,128)(2,1)} %collective-permute-done.4.refs_2_.refs_1_, ...), custom_call_target="tpu_custom_call" | custom-call | tf_op jit(solution)/shard_map/project/pallas_call | solution.py:116
  109.9 2.4 %project.5 = bf16[256,512]{1,0:T(8,128)(2,1)} custom-call(s32[3]{0:T(128)S(1)} %pad_add_fusion.where_ref, bf16[16,192,256]{2,1,0:T(8,128)(2,1)S(1)} %collective-permute-done.1.refs_1_.refs_0_, f32[256,768]{1,0:T(8,128)S(1)} %get-tuple-element.15.refs_3_.refs_1_, bf16[192,1024]{1,0:T(8,128)(2,1)S(1)} %collective-permute-done.13.refs_4_.refs_2_.refs_0_, ...), custom_call_target="tpu_custom_call" | custom-call | tf_op jit(solution)/shard_map/project/pallas_call | solution.py:116
  112.3 1.9 collective-permute-start.17
  115.0 1.4 copy.48
  116.3 1.3 exponential_bitcast_fusion
  121.7 1.7 project.4
  123.5 1.2 convert_add_fusion
  125.8 10.6 %all-to-all-start = ((bf16[32,16,128]{2,1,0:T(8,128)(2,1)}), bf16[32,16,128]{2,1,0:T(8,128)(2,1)}, u32[]{:S(2)}, u32[]{:S(2)}) async-start(bf16[32,16,128]{2,1,0:T(8,128)(2,1)} %fusion.17), calls=%async_computation | async-start | bytes 262144 | tf_op jit(solution)/shard_map/all_to_all | solution.py:28
  136.4 1.2 pack_outs.3.refs_0_
  137.7 4.7 %collective-permute-start.19 = (bf16[1344,256]{1,0:T(8,128)(2,1)S(1)}, bf16[1344,256]{1,0:T(8,128)(2,1)S(1)}, u32[]{:S(2)}, u32[]{:S(2)}) collective-permute-start(bf16[1344,256]{1,0:T(8,128)(2,1)S(1)} %pack_outs.3.refs_0_), channel_id=1, source_target_pairs={{0,1},{1,0},{2,3},{3,2},{4,5},{5,4},{6,7},{7,6},{8,9},{9,8},{10,11... | collective-permute-start | bytes 2064392 | tf_op jit(solution)/shard_map/ppermute | solution.py:198
  143.5 2.4 %collective-permute-start.20 = (bf16[768,256]{1,0:T(8,128)(2,1)S(1)}, bf16[768,256]{1,0:T(8,128)(2,1)S(1)}, u32[]{:S(2)}, u32[]{:S(2)}) collective-permute-start(bf16[768,256]{1,0:T(8,128)(2,1)S(1)} %pack_outs.4.refs_1_), channel_id=1, source_target_pairs={{0,1},{1,0},{2,3},{3,2},{4,5},{5,4},{6,7},{7,6},{8,9},{9,8},{10,11... | collective-permute-start | bytes 1179656 | tf_op jit(solution)/shard_map/ppermute | solution.py:198
  146.7 1.2 pack_outs.5.refs_2_
  147.8 4.6 %collective-permute-start.21 = (bf16[960,256]{1,0:T(8,128)(2,1)S(1)}, bf16[960,256]{1,0:T(8,128)(2,1)S(1)}, u32[]{:S(2)}, u32[]{:S(2)}) collective-permute-start(bf16[960,256]{1,0:T(8,128)(2,1)S(1)} %pack_outs.5.refs_2_), channel_id=1, source_target_pairs={{0,1},{1,0},{2,3},{3,2},{4,5},{5,4},{6,7},{7,6},{8,9},{9,8},{10,11... | collective-permute-start | bytes 1474568 | tf_op jit(solution)/shard_map/ppermute | solution.py:198
  152.4 2.2 collective-permute-start.18
  154.7 1.2 fusion.33
  157.7 14.1 %all-to-all-start.1 = ((bf16[32,8,128]{2,1,0:T(8,128)(2,1)}), bf16[32,8,128]{2,1,0:T(8,128)(2,1)}, u32[]{:S(2)}, u32[]{:S(2)}) async-start(bf16[32,8,128]{2,1,0:T(8,128)(2,1)} %bitcast.94), calls=%async_computation.1 | async-start | bytes 131072 | tf_op jit(solution)/shard_map/all_to_all | solution.py:38
  172.5 1.2 collective-permute-done.18
  173.7 2.2 fusion.2
  184.3 1.5 all-to-all-done.1
  185.9 1.4 multiply_reduce_fusion
  188.2 12.9 %collective-permute-start.22 = (bf16[8,256,384]{2,1,0:T(8,128)(2,1)S(1)}, bf16[8,256,384]{2,1,0:T(8,128)(2,1)S(1)}, u32[]{:S(2)}, u32[]{:S(2)}) collective-permute-start(bf16[8,256,384]{2,1,0:T(8,128)(2,1)S(1)} %convolution_convert_fusion), channel_id=1, source_target_pairs={{0,32},{32,0},{64,96},{96,64},{128,160},{160,128},{192,224},{224,1... | collective-permute-start | bytes 4718600 | tf_op jit(solution)/shard_map/ppermute | solution.py:225
  201.9 2.3 collective-permute-done.22
  204.6 24.5 %all_to_all.15 = bf16[8,256,384]{2,1,0:T(8,128)(2,1)S(1)} all-to-all(bf16[8,256,384]{2,1,0:T(8,128)(2,1)S(1)} %add_convert_fusion), channel_id=1, replica_groups={{0,64,128,192,256,320,384,448},{32,96,160,224,288,352,416,480},{1,65,12..., dimensions={0} | all-to-all | bytes 3145728 | tf_op jit(solution)/shard_map/all_to_all | solution.py:229
  (129 shorter events, 27.3 us)
Async XLA Ops:
  2.0 4.4 %copy-start.25 = (bf16[192,1024]{1,0:T(8,128)(2,1)}, bf16[192,1024]{1,0:T(8,128)(2,1)S(1)}, u32[]{:S(2)}) copy-start(bf16[192,1024]{1,0:T(8,128)(2,1)S(1)} %pad_maximum_fusion.refs_6_.refs_3_) | copy-start | bytes 1179652
  2.0 20.8 %collective-permute-start = (bf16[192,1024]{1,0:T(8,128)(2,1)S(1)}, bf16[192,1024]{1,0:T(8,128)(2,1)S(1)}, u32[]{:S(2)}, u32[]{:S(2)}) collective-permute-start(bf16[192,1024]{1,0:T(8,128)(2,1)S(1)} %pad_maximum_fusion.refs_6_.refs_3_), channel_id=1, source_target_pairs={{0,2},{1,3},{2,4},{3,5},{4,6},{5,7},{6,8},{7,9},{8,10},{9,11},{10,... | collective-permute-start | bytes 1179656 | tf_op jit(solution)/shard_map/ppermute | solution.py:153
  6.3 18.3 %collective-permute-start.5 = (bf16[192,1024]{1,0:T(8,128)(2,1)S(1)}, bf16[192,1024]{1,0:T(8,128)(2,1)S(1)}, u32[]{:S(2)}, u32[]{:S(2)}) collective-permute-start(bf16[192,1024]{1,0:T(8,128)(2,1)S(1)} %pad_maximum_fusion.refs_6_.refs_3_), channel_id=1, source_target_pairs={{0,30},{1,31},{2,0},{3,1},{4,2},{5,3},{6,4},{7,5},{8,6},{9,7},{10,... | collective-permute-start | bytes 1179656 | tf_op jit(solution)/shard_map/ppermute | solution.py:154
  22.7 1.9 copy-start.27
  22.7 12.5 %collective-permute-start.2 = (bf16[192,1024]{1,0:T(8,128)(2,1)S(1)}, bf16[192,1024]{1,0:T(8,128)(2,1)S(1)}, u32[]{:S(2)}, u32[]{:S(2)}) collective-permute-start(bf16[192,1024]{1,0:T(8,128)(2,1)S(1)} %collective-permute-done.refs_5_.refs_2_), channel_id=1, source_target_pairs={{0,2},{1,3},{2,4},{3,5},{4,6},{5,7},{6,8},{7,9},{8,10},{9,11},{10,... | collective-permute-start | bytes 1179656 | tf_op jit(solution)/shard_map/ppermute | solution.py:153
  24.7 10.6 %copy-start.28 = (bf16[192,1024]{1,0:T(8,128)(2,1)}, bf16[192,1024]{1,0:T(8,128)(2,1)S(1)}, u32[]{:S(2)}) copy-start(bf16[192,1024]{1,0:T(8,128)(2,1)S(1)} %collective-permute-done.5.refs_7_.refs_4_) | copy-start | bytes 1179652
  24.7 12.5 %collective-permute-start.6 = (bf16[192,1024]{1,0:T(8,128)(2,1)S(1)}, bf16[192,1024]{1,0:T(8,128)(2,1)S(1)}, u32[]{:S(2)}, u32[]{:S(2)}) collective-permute-start(bf16[192,1024]{1,0:T(8,128)(2,1)S(1)} %collective-permute-done.5.refs_7_.refs_4_), channel_id=1, source_target_pairs={{0,30},{1,31},{2,0},{3,1},{4,2},{5,3},{6,4},{7,5},{8,6},{9,7},{10,... | collective-permute-start | bytes 1179656 | tf_op jit(solution)/shard_map/ppermute | solution.py:154
  35.2 1.9 copy-start.29
  35.2 11.7 %collective-permute-start.3 = (bf16[192,1024]{1,0:T(8,128)(2,1)S(1)}, bf16[192,1024]{1,0:T(8,128)(2,1)S(1)}, u32[]{:S(2)}, u32[]{:S(2)}) collective-permute-start(bf16[192,1024]{1,0:T(8,128)(2,1)S(1)} %collective-permute-done.2.refs_4_.refs_1_), channel_id=1, source_target_pairs={{0,2},{1,3},{2,4},{3,5},{4,6},{5,7},{6,8},{7,9},{8,10},{9,11},{10,... | collective-permute-start | bytes 1179656 | tf_op jit(solution)/shard_map/ppermute | solution.py:153
  37.2 9.7 %copy-start.30 = (bf16[192,1024]{1,0:T(8,128)(2,1)}, bf16[192,1024]{1,0:T(8,128)(2,1)S(1)}, u32[]{:S(2)}) copy-start(bf16[192,1024]{1,0:T(8,128)(2,1)S(1)} %collective-permute-done.6.refs_8_.refs_5_) | copy-start | bytes 1179652
  37.2 11.6 %collective-permute-start.7 = (bf16[192,1024]{1,0:T(8,128)(2,1)S(1)}, bf16[192,1024]{1,0:T(8,128)(2,1)}, u32[]{:S(2)}, u32[]{:S(2)}) collective-permute-start(bf16[192,1024]{1,0:T(8,128)(2,1)S(1)} %collective-permute-done.6.refs_8_.refs_5_), channel_id=1, source_target_pairs={{0,30},{1,31},{2,0},{3,1},{4,2},{5,3},{6,4},{7,5},{8,6},{9,7},{10,... | collective-permute-start | bytes 1179656 | tf_op jit(solution)/shard_map/ppermute | solution.py:154
  46.9 11.2 %copy-start.31 = (bf16[192,1024]{1,0:T(8,128)(2,1)}, bf16[192,1024]{1,0:T(8,128)(2,1)S(1)}, u32[]{:S(2)}) copy-start(bf16[192,1024]{1,0:T(8,128)(2,1)S(1)} %collective-permute-done.3.refs_3_.refs_0_) | copy-start | bytes 1179652
  46.9 19.2 %collective-permute-start.4 = (bf16[192,1024]{1,0:T(8,128)(2,1)S(1)}, bf16[192,1024]{1,0:T(8,128)(2,1)}, u32[]{:S(2)}, u32[]{:S(2)}) collective-permute-start(bf16[192,1024]{1,0:T(8,128)(2,1)S(1)} %collective-permute-done.3.refs_3_.refs_0_), channel_id=1, source_target_pairs={{0,2},{1,3},{2,4},{3,5},{4,6},{5,7},{6,8},{7,9},{8,10},{9,11},{10,... | collective-permute-start | bytes 1179656 | tf_op jit(solution)/shard_map/ppermute | solution.py:153
  48.8 19.2 %collective-permute-start.8 = (bf16[192,1024]{1,0:T(8,128)(2,1)}, bf16[192,1024]{1,0:T(8,128)(2,1)}, u32[]{:S(2)}, u32[]{:S(2)}) collective-permute-start(bf16[192,1024]{1,0:T(8,128)(2,1)} %collective-permute-done.7.refs_9_.refs_6_), channel_id=1, source_target_pairs={{0,30},{1,31},{2,0},{3,1},{4,2},{5,3},{6,4},{7,5},{8,6},{9,7},{10,... | collective-permute-start | bytes 1179656 | tf_op jit(solution)/shard_map/ppermute | solution.py:154
  58.1 24.7 %copy-start.35 = (f32[2,256]{1,0:T(2,128)S(1)}, f32[2,256]{1,0:T(2,128)}, u32[]{:S(2)}) copy-start(f32[2,256]{1,0:T(2,128)} %param.8) | copy-start | bytes 6148
  61.4 43.5 %collective-permute-start.1 = (bf16[16,192,256]{2,1,0:T(8,128)(2,1)}, bf16[16,192,256]{2,1,0:T(8,128)(2,1)S(1)}, u32[]{:S(2)}, u32[]{:S(2)}) collective-permute-start(bf16[16,192,256]{2,1,0:T(8,128)(2,1)} %get-tuple-element.21), channel_id=1, source_target_pairs={{0,1},{1,0},{2,3},{3,2},{4,5},{5,4},{6,7},{7,6},{8,9},{9,8},{10,11... | collective-permute-start | bytes 4718600 | tf_op jit(solution)/shard_map/ppermute | solution.py:164
  66.1 10.2 %collective-permute-start.9 = (bf16[192,1024]{1,0:T(8,128)(2,1)}, bf16[192,1024]{1,0:T(8,128)(2,1)S(1)}, u32[]{:S(2)}, u32[]{:S(2)}) collective-permute-start(bf16[192,1024]{1,0:T(8,128)(2,1)} %collective-permute-done.4.refs_2_.refs_1_), channel_id=1, source_target_pairs={{0,2},{1,3},{2,4},{3,5},{4,6},{5,7},{6,8},{7,9},{8,10},{9,11},{10,... | collective-permute-start | bytes 1179656 | tf_op jit(solution)/shard_map/ppermute | solution.py:153
  68.0 10.2 %collective-permute-start.11 = (bf16[192,1024]{1,0:T(8,128)(2,1)}, bf16[192,1024]{1,0:T(8,128)(2,1)}, u32[]{:S(2)}, u32[]{:S(2)}) collective-permute-start(bf16[192,1024]{1,0:T(8,128)(2,1)} %collective-permute-done.8.refs_10_.refs_2_), channel_id=1, source_target_pairs={{0,30},{1,31},{2,0},{3,1},{4,2},{5,3},{6,4},{7,5},{8,6},{9,7},{10,... | collective-permute-start | bytes 1179656 | tf_op jit(solution)/shard_map/ppermute | solution.py:154
  76.3 7.2 %copy-start.32 = (bf16[192,1024]{1,0:T(8,128)(2,1)}, bf16[192,1024]{1,0:T(8,128)(2,1)S(1)}, u32[]{:S(2)}) copy-start(bf16[192,1024]{1,0:T(8,128)(2,1)S(1)} %collective-permute-done.9.refs_12_.refs_0_) | copy-start | bytes 1179652
  76.3 10.0 %collective-permute-start.10 = (bf16[192,1024]{1,0:T(8,128)(2,1)S(1)}, bf16[192,1024]{1,0:T(8,128)(2,1)}, u32[]{:S(2)}, u32[]{:S(2)}) collective-permute-start(bf16[192,1024]{1,0:T(8,128)(2,1)S(1)} %collective-permute-done.9.refs_12_.refs_0_), channel_id=1, source_target_pairs={{0,2},{1,3},{2,4},{3,5},{4,6},{5,7},{6,8},{7,9},{8,10},{9,11},{10,... | collective-permute-start | bytes 1179656 | tf_op jit(solution)/shard_map/ppermute | solution.py:153
  78.2 10.0 %collective-permute-start.12 = (bf16[192,1024]{1,0:T(8,128)(2,1)}, bf16[192,1024]{1,0:T(8,128)(2,1)}, u32[]{:S(2)}, u32[]{:S(2)}) collective-permute-start(bf16[192,1024]{1,0:T(8,128)(2,1)} %collective-permute-done.11.refs_13_.refs_3_), channel_id=1, source_target_pairs={{0,30},{1,31},{2,0},{3,1},{4,2},{5,3},{6,4},{7,5},{8,6},{9,7},{10,... | collective-permute-start | bytes 1179656 | tf_op jit(solution)/shard_map/ppermute | solution.py:154
  86.3 10.2 %collective-permute-start.13 = (bf16[192,1024]{1,0:T(8,128)(2,1)}, bf16[192,1024]{1,0:T(8,128)(2,1)S(1)}, u32[]{:S(2)}, u32[]{:S(2)}) collective-permute-start(bf16[192,1024]{1,0:T(8,128)(2,1)} %collective-permute-done.10.refs_11_.refs_1_), channel_id=1, source_target_pairs={{0,2},{1,3},{2,4},{3,5},{4,6},{5,7},{6,8},{7,9},{8,10},{9,11},{10,... | collective-permute-start | bytes 1179656 | tf_op jit(solution)/shard_map/ppermute | solution.py:153
  88.2 10.2 %collective-permute-start.14 = (bf16[192,1024]{1,0:T(8,128)(2,1)}, bf16[192,1024]{1,0:T(8,128)(2,1)}, u32[]{:S(2)}, u32[]{:S(2)}) collective-permute-start(bf16[192,1024]{1,0:T(8,128)(2,1)} %collective-permute-done.12.refs_14_.refs_2_), channel_id=1, source_target_pairs={{0,30},{1,31},{2,0},{3,1},{4,2},{5,3},{6,4},{7,5},{8,6},{9,7},{10,... | collective-permute-start | bytes 1179656 | tf_op jit(solution)/shard_map/ppermute | solution.py:154
  96.5 21.1 %copy-start = (bf16[192,1024]{1,0:T(8,128)(2,1)}, bf16[192,1024]{1,0:T(8,128)(2,1)S(1)}, u32[]{:S(2)}) copy-start(bf16[192,1024]{1,0:T(8,128)(2,1)S(1)} %collective-permute-done.13.refs_4_.refs_2_.refs_0_) | copy-start | bytes 1179652
  96.6 13.3 %collective-permute-start.15 = (bf16[96,1024]{1,0:T(8,128)(2,1)S(1)}, bf16[96,1024]{1,0:T(8,128)(2,1)S(1)}, u32[]{:S(2)}, u32[]{:S(2)}) collective-permute-start(bf16[96,1024]{1,0:T(8,128)(2,1)S(1)} %slice.61), channel_id=1, source_target_pairs={{0,2},{1,3},{2,4},{3,5},{4,6},{5,7},{6,8},{7,9},{8,10},{9,11},{10,... | collective-permute-start | bytes 589832 | tf_op jit(solution)/shard_map/ppermute | solution.py:156
  99.5 10.4 %collective-permute-start.16 = (bf16[96,1024]{1,0:T(8,128)(2,1)S(1)}, bf16[96,1024]{1,0:T(8,128)(2,1)S(1)}, u32[]{:S(2)}, u32[]{:S(2)}) collective-permute-start(bf16[96,1024]{1,0:T(8,128)(2,1)S(1)} %slice.62), channel_id=1, source_target_pairs={{0,30},{1,31},{2,0},{3,1},{4,2},{5,3},{6,4},{7,5},{8,6},{9,7},{10,... | collective-permute-start | bytes 589832 | tf_op jit(solution)/shard_map/ppermute | solution.py:157
  109.8 2.4 %copy-start.1 = (f32[256,768]{1,0:T(8,128)}, f32[256,768]{1,0:T(8,128)S(1)}, u32[]{:S(2)}) copy-start(f32[256,768]{1,0:T(8,128)S(1)} %get-tuple-element.15.refs_3_.refs_1_) | copy-start | bytes 2359300
  109.8 2.4 %copy-start.13 = (f32[256,768]{1,0:T(8,128)}, f32[256,768]{1,0:T(8,128)S(1)}, u32[]{:S(2)}) copy-start(f32[256,768]{1,0:T(8,128)S(1)} %get-tuple-element.14.refs_2_) | copy-start | bytes 2359300
  109.9 2.4 %copy-start.7 = (bf16[96,1024]{1,0:T(8,128)(2,1)}, bf16[96,1024]{1,0:T(8,128)(2,1)S(1)}, u32[]{:S(2)}) copy-start(bf16[96,1024]{1,0:T(8,128)(2,1)S(1)} %collective-permute-done.15.refs_6_.refs_4_) | copy-start | bytes 589828
  109.9 2.4 %copy-start.10 = (bf16[96,1024]{1,0:T(8,128)(2,1)}, bf16[96,1024]{1,0:T(8,128)(2,1)S(1)}, u32[]{:S(2)}) copy-start(bf16[96,1024]{1,0:T(8,128)(2,1)S(1)} %collective-permute-done.16.refs_7_.refs_5_) | copy-start | bytes 589828
  112.3 11.2 %collective-permute-start.17 = (bf16[256,512]{1,0:T(8,128)(2,1)}, bf16[256,512]{1,0:T(8,128)(2,1)}, u32[]{:S(2)}, u32[]{:S(2)}) collective-permute-start(bf16[256,512]{1,0:T(8,128)(2,1)} %project.5), channel_id=1, source_target_pairs={{0,1},{1,0},{2,3},{3,2},{4,5},{5,4},{6,7},{7,6},{8,9},{9,8},{10,11... | collective-permute-start | bytes 786440 | tf_op jit(solution)/shard_map/ppermute | solution.py:183
  124.7 11.7 %copy-start.26 = (f32[256,512]{1,0:T(8,128)}, f32[256,512]{1,0:T(8,128)S(1)}, u32[]{:S(2)}) copy-start(f32[256,512]{1,0:T(8,128)S(1)} %convert_add_fusion) | copy-start | bytes 1572868
  124.9 11.5 %copy-start.33 = (bf16[256,256]{0,1:T(8,128)(2,1)}, bf16[256,256]{0,1:T(8,128)(2,1)S(1)}, u32[]{:S(2)}) copy-start(bf16[256,256]{0,1:T(8,128)(2,1)S(1)} %copy.49) | copy-start | bytes 393220
  125.8 28.9 %all-to-all-start = ((bf16[32,16,128]{2,1,0:T(8,128)(2,1)}), bf16[32,16,128]{2,1,0:T(8,128)(2,1)}, u32[]{:S(2)}, u32[]{:S(2)}) async-start(bf16[32,16,128]{2,1,0:T(8,128)(2,1)} %fusion.17), calls=%async_computation | async-start | bytes 262144 | tf_op jit(solution)/shard_map/all_to_all | solution.py:28
  137.7 10.1 %copy-start.3 = (bf16[1344,256]{1,0:T(8,128)(2,1)}, bf16[1344,256]{1,0:T(8,128)(2,1)S(1)}, u32[]{:S(2)}) copy-start(bf16[1344,256]{1,0:T(8,128)(2,1)S(1)} %pack_outs.3.refs_0_) | copy-start | bytes 2064388
  137.7 8.2 %copy-start.9 = (bf16[96,1024]{1,0:T(8,128)(2,1)S(1)}, bf16[96,1024]{1,0:T(8,128)(2,1)}, u32[]{:S(2)}) copy-start(bf16[96,1024]{1,0:T(8,128)(2,1)} %copy-done.7) | copy-start | bytes 589828
  137.7 8.2 %copy-start.12 = (bf16[96,1024]{1,0:T(8,128)(2,1)S(1)}, bf16[96,1024]{1,0:T(8,128)(2,1)}, u32[]{:S(2)}) copy-start(bf16[96,1024]{1,0:T(8,128)(2,1)} %copy-done.10) | copy-start | bytes 589828
  137.7 38.2 %collective-permute-start.19 = (bf16[1344,256]{1,0:T(8,128)(2,1)S(1)}, bf16[1344,256]{1,0:T(8,128)(2,1)S(1)}, u32[]{:S(2)}, u32[]{:S(2)}) collective-permute-start(bf16[1344,256]{1,0:T(8,128)(2,1)S(1)} %pack_outs.3.refs_0_), channel_id=1, source_target_pairs={{0,1},{1,0},{2,3},{3,2},{4,5},{5,4},{6,7},{7,6},{8,9},{9,8},{10,11... | collective-permute-start | bytes 2064392 | tf_op jit(solution)/shard_map/ppermute | solution.py:198
  143.5 8.9 %copy-start.24 = (bf16[256,256]{1,0:T(8,128)(2,1)S(1)}, bf16[256,256]{1,0:T(8,128)(2,1)}, u32[]{:S(2)}) copy-start(bf16[256,256]{1,0:T(8,128)(2,1)} %copy-done.23) | copy-start | bytes 393220
  143.5 33.2 %collective-permute-start.20 = (bf16[768,256]{1,0:T(8,128)(2,1)S(1)}, bf16[768,256]{1,0:T(8,128)(2,1)S(1)}, u32[]{:S(2)}, u32[]{:S(2)}) collective-permute-start(bf16[768,256]{1,0:T(8,128)(2,1)S(1)} %pack_outs.4.refs_1_), channel_id=1, source_target_pairs={{0,1},{1,0},{2,3},{3,2},{4,5},{5,4},{6,7},{7,6},{8,9},{9,8},{10,11... | collective-permute-start | bytes 1179656 | tf_op jit(solution)/shard_map/ppermute | solution.py:198
  146.7 27.0 %copy-start.22 = (f32[256,256]{1,0:T(8,128)S(1)}, f32[256,256]{1,0:T(8,128)}, u32[]{:S(2)}) copy-start(f32[256,256]{1,0:T(8,128)} %copy-done.21) | copy-start | bytes 786436
  147.8 28.0 %copy-start.5 = (bf16[960,256]{1,0:T(8,128)(2,1)}, bf16[960,256]{1,0:T(8,128)(2,1)S(1)}, u32[]{:S(2)}) copy-start(bf16[960,256]{1,0:T(8,128)(2,1)S(1)} %pack_outs.5.refs_2_) | copy-start | bytes 1474564
  147.8 29.6 %collective-permute-start.21 = (bf16[960,256]{1,0:T(8,128)(2,1)S(1)}, bf16[960,256]{1,0:T(8,128)(2,1)S(1)}, u32[]{:S(2)}, u32[]{:S(2)}) collective-permute-start(bf16[960,256]{1,0:T(8,128)(2,1)S(1)} %pack_outs.5.refs_2_), channel_id=1, source_target_pairs={{0,1},{1,0},{2,3},{3,2},{4,5},{5,4},{6,7},{7,6},{8,9},{9,8},{10,11... | collective-permute-start | bytes 1474568 | tf_op jit(solution)/shard_map/ppermute | solution.py:198
  152.4 21.3 %collective-permute-start.18 = (bf16[256,256]{1,0:T(8,128)(2,1)S(1)}, bf16[256,256]{1,0:T(8,128)(2,1)}, u32[]{:S(2)}, u32[]{:S(2)}) collective-permute-start(bf16[256,256]{1,0:T(8,128)(2,1)S(1)} %copy-done.24), channel_id=1, source_target_pairs={{0,1},{1,0},{2,3},{3,2},{4,5},{5,4},{6,7},{7,6},{8,9},{9,8},{10,11... | collective-permute-start | bytes 393224 | tf_op jit(solution)/shard_map/ppermute | solution.py:187
  157.7 28.1 %all-to-all-start.1 = ((bf16[32,8,128]{2,1,0:T(8,128)(2,1)}), bf16[32,8,128]{2,1,0:T(8,128)(2,1)}, u32[]{:S(2)}, u32[]{:S(2)}) async-start(bf16[32,8,128]{2,1,0:T(8,128)(2,1)} %bitcast.94), calls=%async_computation.1 | async-start | bytes 131072 | tf_op jit(solution)/shard_map/all_to_all | solution.py:38
  173.7 12.2 %copy-start.36 = (f32[256,2]{0,1:T(2,128)S(1)}, f32[256,2]{0,1:T(2,128)}, u32[]{:S(2)}) copy-start(f32[256,2]{0,1:T(2,128)} %get-tuple-element.26) | copy-start | bytes 6148
  184.3 2.9 %copy-start.37 = (f32[256]{0:T(256)S(1)}, f32[256]{0:T(256)}, u32[]{:S(2)}) copy-start(f32[256]{0:T(256)} %param.9) | copy-start | bytes 3076
  188.2 16.0 %collective-permute-start.22 = (bf16[8,256,384]{2,1,0:T(8,128)(2,1)S(1)}, bf16[8,256,384]{2,1,0:T(8,128)(2,1)S(1)}, u32[]{:S(2)}, u32[]{:S(2)}) collective-permute-start(bf16[8,256,384]{2,1,0:T(8,128)(2,1)S(1)} %convolution_convert_fusion), channel_id=1, source_target_pairs={{0,32},{32,0},{64,96},{96,64},{128,160},{160,128},{192,224},{224,1... | collective-permute-start | bytes 4718600 | tf_op jit(solution)/shard_map/ppermute | solution.py:225
  (15 other events, 15.8 us)

commit v6 on v5

--- a/solution.py
+++ b/solution.py
@@ -146,21 +146,23 @@
 
         parts = jnp.transpose(qkv_weight, (1, 0, 2))
         own = jnp.concatenate([parts[1], parts[2], parts[0], out_weight], axis=1)
+        by_z = tokens.T.reshape(n_z, 2, shard, rows)
+        mine = lax.dynamic_index_in_dim(by_z, half, 1, False)
+        theirs = lax.dynamic_index_in_dim(by_z, 1 - half, 1, False)
+
         pieces = {0: own}
         last = n_z // 2
         ahead = behind = own
         for k in range(1, last):
             ahead = lax.ppermute(ahead, "seq", up)
             behind = lax.ppermute(behind, "seq", down)
+            if k == 1:
+                ahead, mine, theirs = lax.optimization_barrier((ahead, mine, theirs))
             pieces[-k], pieces[k] = ahead, behind
         top = lax.ppermute(ahead[: shard // 2], "seq", up)
         bottom = lax.ppermute(behind[shard // 2 :], "seq", down)
         pieces[last] = jnp.concatenate([top, bottom], axis=0)
 
-        by_z = tokens.T.reshape(n_z, 2, shard, rows)
-        by_z, _ = lax.optimization_barrier((by_z, pieces[-1]))
-        mine = lax.dynamic_index_in_dim(by_z, half, 1, False)
-        theirs = lax.dynamic_index_in_dim(by_z, 1 - half, 1, False)
         theirs = lax.ppermute(theirs, "seq", flip)
 
         inner, outer = last // 2, last - 2
@@ -174,17 +176,24 @@
         where = jnp.stack([z, half, core]).astype(jnp.int32)
         toks = (mine, theirs)
         known = [(pieces[o], o, 0, shard) for o in groups[0] + groups[1]]
-        final = [(pieces[o], o, 0, shard) for o in groups[2][:2]]
-        final += [(top, last, 0, shard // 2), (bottom, last, shard // 2, shard // 2)]
-        b16, kv = jnp.bfloat16, 2 * width
+        kv = 2 * width
         jobs = [(0, None, 0, columns, f32), (1, None, 0, columns, f32)]
-        sums = project(where, toks, (), known, jobs, n_z, columns)
-        (away,) = project(where, (theirs,), sums[1:], final, [(0, 0, 0, kv, b16)], n_z, columns)
-        sent = lax.ppermute(away, "seq", flip)
-        jobs = [(0, 0, 0, kv, f32), (0, 0, kv, columns, f32), (1, 1, kv, columns, b16)]
-        kept_kv, kept_q, away = project(where, toks, sums, final, jobs, n_z, columns)
-        kv_proj = kept_kv + sent.astype(f32)
-        q_proj = kept_q + lax.ppermute(away, "seq", flip).astype(f32)
+        mine_sum, theirs_sum = project(where, toks, (), known, jobs, n_z, columns)
+        final = jnp.concatenate([pieces[groups[2][0]], pieces[groups[2][1]], top, bottom], axis=0)
+
+        def add_final(total, tok, lo, hi):
+            picked = [lax.dynamic_index_in_dim(tok, (z + o + n_z) % n_z, 0, False) for o in groups[2]]
+            part = lax.dot_general(
+                jnp.concatenate(picked, axis=0),
+                final[:, lo:hi],
+                (((0,), (0,)), ((), ())),
+                preferred_element_type=f32,
+            )
+            return total[:, lo:hi] + part
+
+        sent = lax.ppermute(add_final(theirs_sum, theirs, 0, kv).astype(jnp.bfloat16), "seq", flip)
+        kv_proj = add_final(mine_sum, mine, 0, kv) + sent.astype(f32)
+        q_away = add_final(theirs_sum, theirs, kv, columns).astype(jnp.bfloat16)
 
         swaps, packs = [], []
         first, second = last // 2 - 1, last // 2 + 1
@@ -195,7 +204,12 @@
         )
         for n, batch in enumerate(batches):
             packs.append(pack_outs([pieces[o] for o in batch], width))
-            swaps.append(lax.ppermute(packs[n], "seq", flip))
+            if n < 2:
+                swaps.append(lax.ppermute(packs[n], "seq", flip))
+            else:
+                joined = jnp.concatenate([packs[n], q_away], axis=0)
+                swaps.append(lax.ppermute(joined, "seq", flip))
+        q_proj = add_final(mine_sum, mine, kv, columns) + swaps[2][packs[2].shape[0] :].astype(f32)
 
         key = jax.nn.silu(kv_proj[:, :width]).astype(jnp.bfloat16).reshape(rows, heads, hsize)
         value = kv_proj[:, width:].astype(jnp.bfloat16).reshape(rows, heads, hsize)

time: 232 us -> 216 us (0.931)
  local copies, waits for them, and re-layouts: 26.5 us -> 16.2 us
  Pallas kernels: 13.3 us -> 9.12 us
  starting transfers between devices: 118 us -> 114 us
  matrix products: 5.35 us -> 9.24 us
  other arithmetic: 10 us -> 7.19 us
    ppermute x7, waiting for transfers between devices: 26.8 us -> 17.4 us  [layer(): ahead = lax.ppermute(ahead, 'seq', up)]
    unnamed x81 -> x56, local copies, waits for them, and re-layouts: 19.2 us -> 10.1 us
    ppermute x3 -> x2, waiting for transfers between devices: 0.01 us -> 5.3 us  [layer(): swaps.append(lax.ppermute(packs[n], 'seq', flip))]
    ppermute x2, starting transfers between devices: 4.14 us -> 9.28 us  [the longest x1 4.65 us: layer(): lax.ppermute(add_final(theirs_sum, theirs, 0, kv).astype(jnp.bfloat16), '...]
    ppermute x3 -> x2, starting transfers between devices: 11.6 us -> 6.79 us  [layer(): swaps.append(lax.ppermute(packs[n], 'seq', flip))]
    pallas_call x3 -> x1, Pallas kernels: 9.03 us -> 4.93 us  [project(): pl.pallas_call(kernel, out_shape=[jax.ShapeDtypeStruct((rows, hi - lo), k...]
    ppermute x1, waiting for transfers between devices: 0.01 us -> 3.41 us  [layer(): theirs = lax.ppermute(theirs, 'seq', flip)]
    dot_general x0 -> x4, matrix products: none -> 2.62 us  [add_final(): lax.dot_general(jnp.concatenate(picked, axis=0), final[:, lo:hi], (((0,),...]
  transfers between devices with their start and end apart: 25 -> 24, of which waited for: 9 -> 10; matrix products, arithmetic and copies ran while one was open for 10% -> 10% of each run, Pallas kernels for 5% -> 4%
where the time goes in v6:
time: 216 us; the launch traced here: 215 us
  starting transfers between devices  114 us (53%)
  waiting for transfers between devices  33.6 us (16%)
  blocking collectives  24.1 us (11%)
  local copies, waits for them, and re-layouts  16.2 us (8%)
  matrix products  9.24 us (4%)
  Pallas kernels  9.12 us (4%)
  other arithmetic  7.19 us (3%)
    ppermute x7, starting transfers between devices, layer(): behind = lax.ppermute(behind, 'seq', down)  36.9 us
    all_to_all x1, blocking collectives, layer(): lax.all_to_all(keep.astype(jnp.bfloat16), 'dp', 0, 0, axis_index_groups=g...  24.1 us
    ppermute x7, waiting for transfers between devices, layer(): ahead = lax.ppermute(ahead, 'seq', up)  17.4 us
    ppermute x7, starting transfers between devices, layer(): ahead = lax.ppermute(ahead, 'seq', up)  15.8 us
    all_to_all x1, starting transfers between devices, exclusive_state(): back = lax.all_to_all(earlier, 'seq', 0, 0, tiled=True)  11.7 us
    ppermute x1, starting transfers between devices, layer(): taken = lax.ppermute(give.astype(jnp.bfloat16), 'dp', pair_perm(n_dp))  11.7 us
    all_to_all x1, starting transfers between devices, exclusive_state(): got = lax.all_to_all(sent, 'seq', 0, 0, tiled=True)  11 us
    unnamed x56, local copies, waits for them, and re-layouts  10.1 us
  transfers between devices with their start and end apart: 24, of which 10 were waited for; matrix products, arithmetic and copies ran while one was open for 10% of the time, Pallas kernels for 4%

profile of v6, /device:TPU:1, one launch (start us, length us, event | category | flops | bytes accessed | tf_op | source)
XLA Modules:
  0.0 214.6 jit_solution(9719469681625943517)
XLA Ops:
  0.0 1.0 slice_bitcast_fusion.6
  2.0 4.4 %collective-permute-start = (bf16[192,1024]{1,0:T(8,128)(2,1)S(1)}, bf16[192,1024]{1,0:T(8,128)(2,1)S(1)}, u32[]{:S(2)}, u32[]{:S(2)}) collective-permute-start(bf16[192,1024]{1,0:T(8,128)(2,1)S(1)} %pad_maximum_fusion.1.refs_6_.refs_3_), channel_id=1, source_target_pairs={{0,2},{1,3},{2,4},{3,5},{4,6},{5,7},{6,8},{7,9},{8,10},{9,11},{10,... | collective-permute-start | bytes 1179656 | tf_op jit(solution)/shard_map/ppermute | solution.py:157
  6.3 9.5 %collective-permute-start.5 = (bf16[192,1024]{1,0:T(8,128)(2,1)S(1)}, bf16[192,1024]{1,0:T(8,128)(2,1)S(1)}, u32[]{:S(2)}, u32[]{:S(2)}) collective-permute-start(bf16[192,1024]{1,0:T(8,128)(2,1)S(1)} %pad_maximum_fusion.1.refs_6_.refs_3_), channel_id=1, source_target_pairs={{0,30},{1,31},{2,0},{3,1},{4,2},{5,3},{6,4},{7,5},{8,6},{9,7},{10,... | collective-permute-start | bytes 1179656 | tf_op jit(solution)/shard_map/ppermute | solution.py:158
  15.9 4.7 %copy.38 = bf16[256,6144]{0,1:T(8,128)(2,1)} copy(bf16[256,6144]{1,0:T(8,128)(2,1)} %param.5) | data formatting | bytes 6291456 | tf_op args[0]
  20.6 3.4 %dynamic-slice_bitcast_fusion = (bf16[16,192,256]{2,1,0:T(8,128)(2,1)}, bf16[16,192,256]{2,1,0:T(8,128)(2,1)S(1)}) fusion(bf16[16,2,192,256]{3,2,1,0:T(8,128)(2,1)} %bitcast.95, s32[]{:T(128)S(6)} %select_n.87, s32[]{:T(128)S(6)} %select_n.86), kind=kLoop, calls=%fused_computation.5 | loop fusion | bytes 6291464 | tf_op jit(solution)/shard_map/jit(dynamic_index_in_dim)/squeeze | solution.py:151
  24.0 1.9 collective-permute-start.2
  25.9 4.6 %collective-permute-start.6 = (bf16[192,1024]{1,0:T(8,128)(2,1)S(1)}, bf16[192,1024]{1,0:T(8,128)(2,1)S(1)}, u32[]{:S(2)}, u32[]{:S(2)}) collective-permute-start(bf16[192,1024]{1,0:T(8,128)(2,1)S(1)} %collective-permute-done.5.refs_7_.refs_4_), channel_id=1, source_target_pairs={{0,30},{1,31},{2,0},{3,1},{4,2},{5,3},{6,4},{7,5},{8,6},{9,7},{10,... | collective-permute-start | bytes 1179656 | tf_op jit(solution)/shard_map/ppermute | solution.py:158
  30.5 6.3 %collective-permute-done.2.refs_4_.refs_1_ = bf16[192,1024]{1,0:T(8,128)(2,1)S(1)} collective-permute-done((bf16[192,1024]{1,0:T(8,128)(2,1)S(1)}, bf16[192,1024]{1,0:T(8,128)(2,1)S(1)}, u32[]{:S(2)}, u32[]{:S(2)}) %collective-permute-start.2) | collective-permute-done | bytes 393248 | tf_op jit(solution)/shard_map/ppermute | solution.py:157
  36.8 1.9 collective-permute-start.3
  38.7 4.6 %collective-permute-start.7 = (bf16[192,1024]{1,0:T(8,128)(2,1)S(1)}, bf16[192,1024]{1,0:T(8,128)(2,1)S(1)}, u32[]{:S(2)}, u32[]{:S(2)}) collective-permute-start(bf16[192,1024]{1,0:T(8,128)(2,1)S(1)} %collective-permute-done.6.refs_8_.refs_5_), channel_id=1, source_target_pairs={{0,30},{1,31},{2,0},{3,1},{4,2},{5,3},{6,4},{7,5},{8,6},{9,7},{10,... | collective-permute-start | bytes 1179656 | tf_op jit(solution)/shard_map/ppermute | solution.py:158
  43.3 5.4 %collective-permute-done.3.refs_3_.refs_0_ = bf16[192,1024]{1,0:T(8,128)(2,1)S(1)} collective-permute-done((bf16[192,1024]{1,0:T(8,128)(2,1)S(1)}, bf16[192,1024]{1,0:T(8,128)(2,1)S(1)}, u32[]{:S(2)}, u32[]{:S(2)}) %collective-permute-start.3) | collective-permute-done | bytes 393248 | tf_op jit(solution)/shard_map/ppermute | solution.py:157
  48.7 1.9 collective-permute-start.4
  50.7 4.6 %collective-permute-start.8 = (bf16[192,1024]{1,0:T(8,128)(2,1)S(1)}, bf16[192,1024]{1,0:T(8,128)(2,1)}, u32[]{:S(2)}, u32[]{:S(2)}) collective-permute-start(bf16[192,1024]{1,0:T(8,128)(2,1)S(1)} %collective-permute-done.7.refs_9_.refs_6_), channel_id=1, source_target_pairs={{0,30},{1,31},{2,0},{3,1},{4,2},{5,3},{6,4},{7,5},{8,6},{9,7},{10,... | collective-permute-start | bytes 1179656 | tf_op jit(solution)/shard_map/ppermute | solution.py:158
  55.3 4.7 %collective-permute-start.1 = (bf16[16,192,256]{2,1,0:T(8,128)(2,1)}, bf16[16,192,256]{2,1,0:T(8,128)(2,1)S(1)}, u32[]{:S(2)}, u32[]{:S(2)}) collective-permute-start(bf16[16,192,256]{2,1,0:T(8,128)(2,1)} %get-tuple-element.13), channel_id=1, source_target_pairs={{0,1},{1,0},{2,3},{3,2},{4,5},{5,4},{6,7},{7,6},{8,9},{9,8},{10,11... | collective-permute-start | bytes 4718600 | tf_op jit(solution)/shard_map/ppermute | solution.py:166
  60.0 1.9 collective-permute-start.9
  61.9 4.6 %collective-permute-start.11 = (bf16[192,1024]{1,0:T(8,128)(2,1)}, bf16[192,1024]{1,0:T(8,128)(2,1)}, u32[]{:S(2)}, u32[]{:S(2)}) collective-permute-start(bf16[192,1024]{1,0:T(8,128)(2,1)} %collective-permute-done.8.refs_10_.refs_2_), channel_id=1, source_target_pairs={{0,30},{1,31},{2,0},{3,1},{4,2},{5,3},{6,4},{7,5},{8,6},{9,7},{10,... | collective-permute-start | bytes 1179656 | tf_op jit(solution)/shard_map/ppermute | solution.py:158
  68.3 2.0 collective-permute-done.9.refs_12_.refs_0_
  70.4 1.9 collective-permute-start.10
  72.3 4.6 %collective-permute-start.12 = (bf16[192,1024]{1,0:T(8,128)(2,1)}, bf16[192,1024]{1,0:T(8,128)(2,1)}, u32[]{:S(2)}, u32[]{:S(2)}) collective-permute-start(bf16[192,1024]{1,0:T(8,128)(2,1)} %collective-permute-done.11.refs_13_.refs_3_), channel_id=1, source_target_pairs={{0,30},{1,31},{2,0},{3,1},{4,2},{5,3},{6,4},{7,5},{8,6},{9,7},{10,... | collective-permute-start | bytes 1179656 | tf_op jit(solution)/shard_map/ppermute | solution.py:158
  77.0 3.6 %collective-permute-done.10.refs_11_.refs_1_ = bf16[192,1024]{1,0:T(8,128)(2,1)} collective-permute-done((bf16[192,1024]{1,0:T(8,128)(2,1)}, bf16[192,1024]{1,0:T(8,128)(2,1)}, u32[]{:S(2)}, u32[]{:S(2)}) %collective-permute-start.10) | collective-permute-done | bytes 393248 | tf_op jit(solution)/shard_map/ppermute | solution.py:157
  80.6 1.9 collective-permute-start.13
  82.5 4.6 %collective-permute-start.14 = (bf16[192,1024]{1,0:T(8,128)(2,1)}, bf16[192,1024]{1,0:T(8,128)(2,1)}, u32[]{:S(2)}, u32[]{:S(2)}) collective-permute-start(bf16[192,1024]{1,0:T(8,128)(2,1)} %collective-permute-done.12.refs_14_.refs_2_), channel_id=1, source_target_pairs={{0,30},{1,31},{2,0},{3,1},{4,2},{5,3},{6,4},{7,5},{8,6},{9,7},{10,... | collective-permute-start | bytes 1179656 | tf_op jit(solution)/shard_map/ppermute | solution.py:158
  88.2 3.4 %collective-permute-done.1.refs_1_ = bf16[16,192,256]{2,1,0:T(8,128)(2,1)S(1)} collective-permute-done((bf16[16,192,256]{2,1,0:T(8,128)(2,1)}, bf16[16,192,256]{2,1,0:T(8,128)(2,1)S(1)}, u32[]{:S(2)}, u32[]{:S(2)}) %collective-permute-start.1) | collective-permute-done | bytes 1572896 | tf_op jit(solution)/shard_map/ppermute | solution.py:166
  91.7 4.9 %project.1 = (f32[256,768]{1,0:T(8,128)S(1)}, f32[256,768]{1,0:T(8,128)S(1)}) custom-call(s32[3]{0:T(128)S(1)} %pad_add_fusion.where_ref, bf16[16,192,256]{2,1,0:T(8,128)(2,1)S(1)} %get-tuple-element.12.refs_0_, bf16[16,192,256]{2,1,0:T(8,128)(2,1)S(1)} %collective-permute-done.1.refs_1_, bf16[192,1024]{1,0:T(8,128)(2,1)} %copy-done.12, ...), custom_call_target="tpu_custom_call" | custom-call | tf_op jit(solution)/shard_map/project/pallas_call | solution.py:116
  96.6 1.9 collective-permute-start.15
  99.5 4.6 %collective-permute-start.16 = (bf16[96,1024]{1,0:T(8,128)(2,1)S(1)}, bf16[96,1024]{1,0:T(8,128)(2,1)S(1)}, u32[]{:S(2)}, u32[]{:S(2)}) collective-permute-start(bf16[96,1024]{1,0:T(8,128)(2,1)S(1)} %slice.92), channel_id=1, source_target_pairs={{0,30},{1,31},{2,0},{3,1},{4,2},{5,3},{6,4},{7,5},{8,6},{9,7},{10,... | collective-permute-start | bytes 589832 | tf_op jit(solution)/shard_map/ppermute | solution.py:163
  104.1 1.0 constant_dynamic-update-slice_fusion.2
  105.2 1.5 collective-permute-done.16
  107.5 4.7 %collective-permute-start.17 = (bf16[256,512]{1,0:T(8,128)(2,1)S(1)}, bf16[256,512]{1,0:T(8,128)(2,1)S(1)}, u32[]{:S(2)}, u32[]{:S(2)}) collective-permute-start(bf16[256,512]{1,0:T(8,128)(2,1)S(1)} %add_convert_fusion.1), channel_id=1, source_target_pairs={{0,1},{1,0},{2,3},{3,2},{4,5},{5,4},{6,7},{7,6},{8,9},{9,8},{10,11... | collective-permute-start | bytes 786440 | tf_op jit(solution)/shard_map/ppermute | solution.py:194
  112.9 1.1 pack_outs.3.refs_2_
  114.5 1.6 collective-permute-done.17
  117.3 11.0 %all-to-all-start = ((bf16[32,16,128]{2,1,0:T(8,128)(2,1)}), bf16[32,16,128]{2,1,0:T(8,128)(2,1)S(1)}, u32[]{:S(2)}, u32[]{:S(2)}) async-start(bf16[32,16,128]{2,1,0:T(8,128)(2,1)} %fusion.29), calls=%async_computation | async-start | bytes 262144 | tf_op jit(solution)/shard_map/all_to_all | solution.py:28
  129.2 4.6 %collective-permute-start.18 = (bf16[1216,256]{1,0:T(8,128)(2,1)}, bf16[1216,256]{1,0:T(8,128)(2,1)S(1)}, u32[]{:S(2)}, u32[]{:S(2)}) collective-permute-start(bf16[1216,256]{1,0:T(8,128)(2,1)} %pad_maximum_fusion), channel_id=1, source_target_pairs={{0,1},{1,0},{2,3},{3,2},{4,5},{5,4},{6,7},{7,6},{8,9},{9,8},{10,11... | collective-permute-start | bytes 1867784 | tf_op jit(solution)/shard_map/ppermute | solution.py:211
  134.5 1.2 pack_outs.4.refs_0_
  135.7 2.1 collective-permute-start.19
  137.9 1.1 pack_outs.5.refs_1_
  139.0 4.6 %collective-permute-start.20 = (bf16[768,256]{1,0:T(8,128)(2,1)S(1)}, bf16[768,256]{1,0:T(8,128)(2,1)S(1)}, u32[]{:S(2)}, u32[]{:S(2)}) collective-permute-start(bf16[768,256]{1,0:T(8,128)(2,1)S(1)} %pack_outs.5.refs_1_), channel_id=1, source_target_pairs={{0,1},{1,0},{2,3},{3,2},{4,5},{5,4},{6,7},{7,6},{8,9},{9,8},{10,11... | collective-permute-start | bytes 1179656 | tf_op jit(solution)/shard_map/ppermute | solution.py:208
  145.0 11.7 %all-to-all-start.1 = ((bf16[32,8,128]{2,1,0:T(8,128)(2,1)}), bf16[32,8,128]{2,1,0:T(8,128)(2,1)}, u32[]{:S(2)}, u32[]{:S(2)}) async-start(bf16[32,8,128]{2,1,0:T(8,128)(2,1)} %bitcast.40), calls=%async_computation.1 | async-start | bytes 131072 | tf_op jit(solution)/shard_map/all_to_all | solution.py:38
  156.7 1.5 fusion.37
  158.9 2.1 fusion.2
  161.0 5.3 %collective-permute-done.20.refs_4_ = bf16[768,256]{1,0:T(8,128)(2,1)S(1)} collective-permute-done((bf16[768,256]{1,0:T(8,128)(2,1)S(1)}, bf16[768,256]{1,0:T(8,128)(2,1)S(1)}, u32[]{:S(2)}, u32[]{:S(2)}) %collective-permute-start.20) | collective-permute-done | bytes 393248 | tf_op jit(solution)/shard_map/ppermute | solution.py:208
  167.1 1.6 copy-done
  168.7 2.1 all-to-all-done.1
  170.8 1.2 multiply_reduce_fusion
  172.2 2.3 %convolution_convert_fusion = bf16[8,256,384]{2,1,0:T(8,128)(2,1)S(1)} fusion(bf16[2,8,384,256]{3,2,1,0:T(8,128)(2,1)} %copy-done, bf16[256,256]{1,0:T(8,128)(2,1)S(1)} %copy.49), kind=kOutput, calls=%fused_computation.1 | convolution fusion | flops 403439616 | bytes 3276800 | tf_op jit(solution)/shard_map/itg,idg->itd/dot_general | solution.py:238
  174.5 11.7 %collective-permute-start.21 = (bf16[8,256,384]{2,1,0:T(8,128)(2,1)S(1)}, bf16[8,256,384]{2,1,0:T(8,128)(2,1)S(1)}, u32[]{:S(2)}, u32[]{:S(2)}) collective-permute-start(bf16[8,256,384]{2,1,0:T(8,128)(2,1)S(1)} %convolution_convert_fusion), channel_id=1, source_target_pairs={{0,32},{32,0},{64,96},{96,64},{128,160},{160,128},{192,224},{224,1... | collective-permute-start | bytes 4718600 | tf_op jit(solution)/shard_map/ppermute | solution.py:239
  186.9 2.3 %collective-permute-done.21 = bf16[8,256,384]{2,1,0:T(8,128)(2,1)S(1)} collective-permute-done((bf16[8,256,384]{2,1,0:T(8,128)(2,1)S(1)}, bf16[8,256,384]{2,1,0:T(8,128)(2,1)S(1)}, u32[]{:S(2)}, u32[]{:S(2)}) %collective-permute-start.21) | collective-permute-done | bytes 1572896 | tf_op jit(solution)/shard_map/ppermute | solution.py:239
  189.6 24.1 %all_to_all.15 = bf16[8,256,384]{2,1,0:T(8,128)(2,1)S(1)} all-to-all(bf16[8,256,384]{2,1,0:T(8,128)(2,1)S(1)} %add_convert_fusion), channel_id=1, replica_groups={{0,64,128,192,256,320,384,448},{32,96,160,224,288,352,416,480},{1,65,12..., dimensions={0} | all-to-all | bytes 3145728 | tf_op jit(solution)/shard_map/all_to_all | solution.py:243
  (108 shorter events, 14.6 us)
Async XLA Ops:
  2.0 18.6 %copy-start.3 = (bf16[192,1024]{1,0:T(8,128)(2,1)}, bf16[192,1024]{1,0:T(8,128)(2,1)S(1)}, u32[]{:S(2)}) copy-start(bf16[192,1024]{1,0:T(8,128)(2,1)S(1)} %pad_maximum_fusion.1.refs_6_.refs_3_) | copy-start | bytes 1179652
  2.0 22.0 %collective-permute-start = (bf16[192,1024]{1,0:T(8,128)(2,1)S(1)}, bf16[192,1024]{1,0:T(8,128)(2,1)S(1)}, u32[]{:S(2)}, u32[]{:S(2)}) collective-permute-start(bf16[192,1024]{1,0:T(8,128)(2,1)S(1)} %pad_maximum_fusion.1.refs_6_.refs_3_), channel_id=1, source_target_pairs={{0,2},{1,3},{2,4},{3,5},{4,6},{5,7},{6,8},{7,9},{8,10},{9,11},{10,... | collective-permute-start | bytes 1179656 | tf_op jit(solution)/shard_map/ppermute | solution.py:157
  6.3 19.5 %collective-permute-start.5 = (bf16[192,1024]{1,0:T(8,128)(2,1)S(1)}, bf16[192,1024]{1,0:T(8,128)(2,1)S(1)}, u32[]{:S(2)}, u32[]{:S(2)}) collective-permute-start(bf16[192,1024]{1,0:T(8,128)(2,1)S(1)} %pad_maximum_fusion.1.refs_6_.refs_3_), channel_id=1, source_target_pairs={{0,30},{1,31},{2,0},{3,1},{4,2},{5,3},{6,4},{7,5},{8,6},{9,7},{10,... | collective-permute-start | bytes 1179656 | tf_op jit(solution)/shard_map/ppermute | solution.py:158
  20.6 46.0 %copy-start.22 = (f32[2,256]{1,0:T(2,128)S(1)}, f32[2,256]{1,0:T(2,128)}, u32[]{:S(2)}) copy-start(f32[2,256]{1,0:T(2,128)} %param.8) | copy-start | bytes 6148
  24.0 26.7 %copy-start.6 = (bf16[192,1024]{1,0:T(8,128)(2,1)}, bf16[192,1024]{1,0:T(8,128)(2,1)S(1)}, u32[]{:S(2)}) copy-start(bf16[192,1024]{1,0:T(8,128)(2,1)S(1)} %collective-permute-done.refs_5_.refs_2_) | copy-start | bytes 1179652
  24.0 12.8 %collective-permute-start.2 = (bf16[192,1024]{1,0:T(8,128)(2,1)S(1)}, bf16[192,1024]{1,0:T(8,128)(2,1)S(1)}, u32[]{:S(2)}, u32[]{:S(2)}) collective-permute-start(bf16[192,1024]{1,0:T(8,128)(2,1)S(1)} %collective-permute-done.refs_5_.refs_2_), channel_id=1, source_target_pairs={{0,2},{1,3},{2,4},{3,5},{4,6},{5,7},{6,8},{7,9},{8,10},{9,11},{10,... | collective-permute-start | bytes 1179656 | tf_op jit(solution)/shard_map/ppermute | solution.py:157
  25.9 24.8 %copy-start.7 = (bf16[192,1024]{1,0:T(8,128)(2,1)}, bf16[192,1024]{1,0:T(8,128)(2,1)S(1)}, u32[]{:S(2)}) copy-start(bf16[192,1024]{1,0:T(8,128)(2,1)S(1)} %collective-permute-done.5.refs_7_.refs_4_) | copy-start | bytes 1179652
  25.9 12.8 %collective-permute-start.6 = (bf16[192,1024]{1,0:T(8,128)(2,1)S(1)}, bf16[192,1024]{1,0:T(8,128)(2,1)S(1)}, u32[]{:S(2)}, u32[]{:S(2)}) collective-permute-start(bf16[192,1024]{1,0:T(8,128)(2,1)S(1)} %collective-permute-done.5.refs_7_.refs_4_), channel_id=1, source_target_pairs={{0,30},{1,31},{2,0},{3,1},{4,2},{5,3},{6,4},{7,5},{8,6},{9,7},{10,... | collective-permute-start | bytes 1179656 | tf_op jit(solution)/shard_map/ppermute | solution.py:158
  36.8 18.5 %copy-start.8 = (bf16[192,1024]{1,0:T(8,128)(2,1)}, bf16[192,1024]{1,0:T(8,128)(2,1)S(1)}, u32[]{:S(2)}) copy-start(bf16[192,1024]{1,0:T(8,128)(2,1)S(1)} %collective-permute-done.2.refs_4_.refs_1_) | copy-start | bytes 1179652
  36.8 12.0 %collective-permute-start.3 = (bf16[192,1024]{1,0:T(8,128)(2,1)S(1)}, bf16[192,1024]{1,0:T(8,128)(2,1)S(1)}, u32[]{:S(2)}, u32[]{:S(2)}) collective-permute-start(bf16[192,1024]{1,0:T(8,128)(2,1)S(1)} %collective-permute-done.2.refs_4_.refs_1_), channel_id=1, source_target_pairs={{0,2},{1,3},{2,4},{3,5},{4,6},{5,7},{6,8},{7,9},{8,10},{9,11},{10,... | collective-permute-start | bytes 1179656 | tf_op jit(solution)/shard_map/ppermute | solution.py:157
  38.7 12.0 %copy-start.9 = (bf16[192,1024]{1,0:T(8,128)(2,1)}, bf16[192,1024]{1,0:T(8,128)(2,1)S(1)}, u32[]{:S(2)}) copy-start(bf16[192,1024]{1,0:T(8,128)(2,1)S(1)} %collective-permute-done.6.refs_8_.refs_5_) | copy-start | bytes 1179652
  38.7 11.9 %collective-permute-start.7 = (bf16[192,1024]{1,0:T(8,128)(2,1)S(1)}, bf16[192,1024]{1,0:T(8,128)(2,1)S(1)}, u32[]{:S(2)}, u32[]{:S(2)}) collective-permute-start(bf16[192,1024]{1,0:T(8,128)(2,1)S(1)} %collective-permute-done.6.refs_8_.refs_5_), channel_id=1, source_target_pairs={{0,30},{1,31},{2,0},{3,1},{4,2},{5,3},{6,4},{7,5},{8,6},{9,7},{10,... | collective-permute-start | bytes 1179656 | tf_op jit(solution)/shard_map/ppermute | solution.py:158
  48.7 11.2 %copy-start.10 = (bf16[192,1024]{1,0:T(8,128)(2,1)}, bf16[192,1024]{1,0:T(8,128)(2,1)S(1)}, u32[]{:S(2)}) copy-start(bf16[192,1024]{1,0:T(8,128)(2,1)S(1)} %collective-permute-done.3.refs_3_.refs_0_) | copy-start | bytes 1179652
  48.7 11.2 %collective-permute-start.4 = (bf16[192,1024]{1,0:T(8,128)(2,1)S(1)}, bf16[192,1024]{1,0:T(8,128)(2,1)S(1)}, u32[]{:S(2)}, u32[]{:S(2)}) collective-permute-start(bf16[192,1024]{1,0:T(8,128)(2,1)S(1)} %collective-permute-done.3.refs_3_.refs_0_), channel_id=1, source_target_pairs={{0,2},{1,3},{2,4},{3,5},{4,6},{5,7},{6,8},{7,9},{8,10},{9,11},{10,... | collective-permute-start | bytes 1179656 | tf_op jit(solution)/shard_map/ppermute | solution.py:157
  50.7 9.3 %copy-start.11 = (bf16[192,1024]{1,0:T(8,128)(2,1)}, bf16[192,1024]{1,0:T(8,128)(2,1)S(1)}, u32[]{:S(2)}) copy-start(bf16[192,1024]{1,0:T(8,128)(2,1)S(1)} %collective-permute-done.7.refs_9_.refs_6_) | copy-start | bytes 1179652
  50.7 11.2 %collective-permute-start.8 = (bf16[192,1024]{1,0:T(8,128)(2,1)S(1)}, bf16[192,1024]{1,0:T(8,128)(2,1)}, u32[]{:S(2)}, u32[]{:S(2)}) collective-permute-start(bf16[192,1024]{1,0:T(8,128)(2,1)S(1)} %collective-permute-done.7.refs_9_.refs_6_), channel_id=1, source_target_pairs={{0,30},{1,31},{2,0},{3,1},{4,2},{5,3},{6,4},{7,5},{8,6},{9,7},{10,... | collective-permute-start | bytes 1179656 | tf_op jit(solution)/shard_map/ppermute | solution.py:158
  55.3 36.3 %collective-permute-start.1 = (bf16[16,192,256]{2,1,0:T(8,128)(2,1)}, bf16[16,192,256]{2,1,0:T(8,128)(2,1)S(1)}, u32[]{:S(2)}, u32[]{:S(2)}) collective-permute-start(bf16[16,192,256]{2,1,0:T(8,128)(2,1)} %get-tuple-element.13), channel_id=1, source_target_pairs={{0,1},{1,0},{2,3},{3,2},{4,5},{5,4},{6,7},{7,6},{8,9},{9,8},{10,11... | collective-permute-start | bytes 4718600 | tf_op jit(solution)/shard_map/ppermute | solution.py:166
  60.0 17.0 %copy-start.12 = (bf16[192,1024]{1,0:T(8,128)(2,1)}, bf16[192,1024]{1,0:T(8,128)(2,1)S(1)}, u32[]{:S(2)}) copy-start(bf16[192,1024]{1,0:T(8,128)(2,1)S(1)} %collective-permute-done.4.refs_2_.refs_1_) | copy-start | bytes 1179652
  60.0 10.4 %collective-permute-start.9 = (bf16[192,1024]{1,0:T(8,128)(2,1)S(1)}, bf16[192,1024]{1,0:T(8,128)(2,1)}, u32[]{:S(2)}, u32[]{:S(2)}) collective-permute-start(bf16[192,1024]{1,0:T(8,128)(2,1)S(1)} %collective-permute-done.4.refs_2_.refs_1_), channel_id=1, source_target_pairs={{0,2},{1,3},{2,4},{3,5},{4,6},{5,7},{6,8},{7,9},{8,10},{9,11},{10,... | collective-permute-start | bytes 1179656 | tf_op jit(solution)/shard_map/ppermute | solution.py:157
  61.9 10.4 %collective-permute-start.11 = (bf16[192,1024]{1,0:T(8,128)(2,1)}, bf16[192,1024]{1,0:T(8,128)(2,1)}, u32[]{:S(2)}, u32[]{:S(2)}) collective-permute-start(bf16[192,1024]{1,0:T(8,128)(2,1)} %collective-permute-done.8.refs_10_.refs_2_), channel_id=1, source_target_pairs={{0,30},{1,31},{2,0},{3,1},{4,2},{5,3},{6,4},{7,5},{8,6},{9,7},{10,... | collective-permute-start | bytes 1179656 | tf_op jit(solution)/shard_map/ppermute | solution.py:158
  67.6 0.6 copy-start.20
  70.4 10.2 %collective-permute-start.10 = (bf16[192,1024]{1,0:T(8,128)(2,1)}, bf16[192,1024]{1,0:T(8,128)(2,1)}, u32[]{:S(2)}, u32[]{:S(2)}) collective-permute-start(bf16[192,1024]{1,0:T(8,128)(2,1)} %collective-permute-done.9.refs_12_.refs_0_), channel_id=1, source_target_pairs={{0,2},{1,3},{2,4},{3,5},{4,6},{5,7},{6,8},{7,9},{8,10},{9,11},{10,... | collective-permute-start | bytes 1179656 | tf_op jit(solution)/shard_map/ppermute | solution.py:157
  72.3 10.2 %collective-permute-start.12 = (bf16[192,1024]{1,0:T(8,128)(2,1)}, bf16[192,1024]{1,0:T(8,128)(2,1)}, u32[]{:S(2)}, u32[]{:S(2)}) collective-permute-start(bf16[192,1024]{1,0:T(8,128)(2,1)} %collective-permute-done.11.refs_13_.refs_3_), channel_id=1, source_target_pairs={{0,30},{1,31},{2,0},{3,1},{4,2},{5,3},{6,4},{7,5},{8,6},{9,7},{10,... | collective-permute-start | bytes 1179656 | tf_op jit(solution)/shard_map/ppermute | solution.py:158
  80.6 16.0 %collective-permute-start.13 = (bf16[192,1024]{1,0:T(8,128)(2,1)}, bf16[192,1024]{1,0:T(8,128)(2,1)S(1)}, u32[]{:S(2)}, u32[]{:S(2)}) collective-permute-start(bf16[192,1024]{1,0:T(8,128)(2,1)} %collective-permute-done.10.refs_11_.refs_1_), channel_id=1, source_target_pairs={{0,2},{1,3},{2,4},{3,5},{4,6},{5,7},{6,8},{7,9},{8,10},{9,11},{10,... | collective-permute-start | bytes 1179656 | tf_op jit(solution)/shard_map/ppermute | solution.py:157
  82.5 16.0 %collective-permute-start.14 = (bf16[192,1024]{1,0:T(8,128)(2,1)}, bf16[192,1024]{1,0:T(8,128)(2,1)}, u32[]{:S(2)}, u32[]{:S(2)}) collective-permute-start(bf16[192,1024]{1,0:T(8,128)(2,1)} %collective-permute-done.12.refs_14_.refs_2_), channel_id=1, source_target_pairs={{0,30},{1,31},{2,0},{3,1},{4,2},{5,3},{6,4},{7,5},{8,6},{9,7},{10,... | collective-permute-start | bytes 1179656 | tf_op jit(solution)/shard_map/ppermute | solution.py:158
  88.2 25.9 %copy-start.16 = (bf16[192,256]{1,0:T(8,128)(2,1)}, bf16[192,256]{1,0:T(8,128)(2,1)S(1)}, u32[]{:S(2)}) copy-start(bf16[192,256]{1,0:T(8,128)(2,1)S(1)} %get-tuple-element.21) | copy-start | bytes 294916
  88.2 25.9 %copy-start.17 = (bf16[192,256]{1,0:T(8,128)(2,1)}, bf16[192,256]{1,0:T(8,128)(2,1)S(1)}, u32[]{:S(2)}) copy-start(bf16[192,256]{1,0:T(8,128)(2,1)S(1)} %get-tuple-element.22) | copy-start | bytes 294916
  88.2 25.9 %copy-start.18 = (bf16[192,256]{1,0:T(8,128)(2,1)}, bf16[192,256]{1,0:T(8,128)(2,1)S(1)}, u32[]{:S(2)}) copy-start(bf16[192,256]{1,0:T(8,128)(2,1)S(1)} %get-tuple-element.23) | copy-start | bytes 294916
  96.6 19.5 %copy-start.2 = (f32[256,768]{1,0:T(8,128)}, f32[256,768]{1,0:T(8,128)S(1)}, u32[]{:S(2)}) copy-start(f32[256,768]{1,0:T(8,128)S(1)} %get-tuple-element.15) | copy-start | bytes 2359300
  96.6 10.1 %copy-start.4 = (bf16[192,1024]{1,0:T(8,128)(2,1)}, bf16[192,1024]{1,0:T(8,128)(2,1)S(1)}, u32[]{:S(2)}) copy-start(bf16[192,1024]{1,0:T(8,128)(2,1)S(1)} %collective-permute-done.13.refs_0_) | copy-start | bytes 1179652
  96.6 8.5 %collective-permute-start.15 = (bf16[96,1024]{1,0:T(8,128)(2,1)S(1)}, bf16[96,1024]{1,0:T(8,128)(2,1)S(1)}, u32[]{:S(2)}, u32[]{:S(2)}) collective-permute-start(bf16[96,1024]{1,0:T(8,128)(2,1)S(1)} %slice.91), channel_id=1, source_target_pairs={{0,2},{1,3},{2,4},{3,5},{4,6},{5,7},{6,8},{7,9},{8,10},{9,11},{10,... | collective-permute-start | bytes 589832 | tf_op jit(solution)/shard_map/ppermute | solution.py:162
  99.5 7.2 %collective-permute-start.16 = (bf16[96,1024]{1,0:T(8,128)(2,1)S(1)}, bf16[96,1024]{1,0:T(8,128)(2,1)S(1)}, u32[]{:S(2)}, u32[]{:S(2)}) collective-permute-start(bf16[96,1024]{1,0:T(8,128)(2,1)S(1)} %slice.92), channel_id=1, source_target_pairs={{0,30},{1,31},{2,0},{3,1},{4,2},{5,3},{6,4},{7,5},{8,6},{9,7},{10,... | collective-permute-start | bytes 589832 | tf_op jit(solution)/shard_map/ppermute | solution.py:163
  106.7 9.5 %copy-start.14 = (bf16[576,1024]{1,0:T(8,128)(2,1)}, bf16[576,1024]{1,0:T(8,128)(2,1)S(1)}, u32[]{:S(2)}) copy-start(bf16[576,1024]{1,0:T(8,128)(2,1)S(1)} %constant_dynamic-update-slice_fusion) | copy-start | bytes 3538948
  107.5 8.6 %collective-permute-start.17 = (bf16[256,512]{1,0:T(8,128)(2,1)S(1)}, bf16[256,512]{1,0:T(8,128)(2,1)S(1)}, u32[]{:S(2)}, u32[]{:S(2)}) collective-permute-start(bf16[256,512]{1,0:T(8,128)(2,1)S(1)} %add_convert_fusion.1), channel_id=1, source_target_pairs={{0,1},{1,0},{2,3},{3,2},{4,5},{5,4},{6,7},{7,6},{8,9},{9,8},{10,11... | collective-permute-start | bytes 786440 | tf_op jit(solution)/shard_map/ppermute | solution.py:194
  114.5 2.1 copy-start.19
  116.2 12.1 %copy-start.5 = (f32[256,512]{1,0:T(8,128)}, f32[256,512]{1,0:T(8,128)S(1)}, u32[]{:S(2)}) copy-start(f32[256,512]{1,0:T(8,128)S(1)} %convert_add_fusion) | copy-start | bytes 1572868
  117.3 26.3 %all-to-all-start = ((bf16[32,16,128]{2,1,0:T(8,128)(2,1)}), bf16[32,16,128]{2,1,0:T(8,128)(2,1)S(1)}, u32[]{:S(2)}, u32[]{:S(2)}) async-start(bf16[32,16,128]{2,1,0:T(8,128)(2,1)} %fusion.29), calls=%async_computation | async-start | bytes 262144 | tf_op jit(solution)/shard_map/all_to_all | solution.py:28
  129.2 27.5 %collective-permute-start.18 = (bf16[1216,256]{1,0:T(8,128)(2,1)}, bf16[1216,256]{1,0:T(8,128)(2,1)S(1)}, u32[]{:S(2)}, u32[]{:S(2)}) collective-permute-start(bf16[1216,256]{1,0:T(8,128)(2,1)} %pad_maximum_fusion), channel_id=1, source_target_pairs={{0,1},{1,0},{2,3},{3,2},{4,5},{5,4},{6,7},{7,6},{8,9},{9,8},{10,11... | collective-permute-start | bytes 1867784 | tf_op jit(solution)/shard_map/ppermute | solution.py:211
  135.7 25.3 %collective-permute-start.19 = (bf16[1344,256]{1,0:T(8,128)(2,1)S(1)}, bf16[1344,256]{1,0:T(8,128)(2,1)S(1)}, u32[]{:S(2)}, u32[]{:S(2)}) collective-permute-start(bf16[1344,256]{1,0:T(8,128)(2,1)S(1)} %pack_outs.4.refs_0_), channel_id=1, source_target_pairs={{0,1},{1,0},{2,3},{3,2},{4,5},{5,4},{6,7},{7,6},{8,9},{9,8},{10,11... | collective-permute-start | bytes 2064392 | tf_op jit(solution)/shard_map/ppermute | solution.py:208
  139.0 27.4 %collective-permute-start.20 = (bf16[768,256]{1,0:T(8,128)(2,1)S(1)}, bf16[768,256]{1,0:T(8,128)(2,1)S(1)}, u32[]{:S(2)}, u32[]{:S(2)}) collective-permute-start(bf16[768,256]{1,0:T(8,128)(2,1)S(1)} %pack_outs.5.refs_1_), channel_id=1, source_target_pairs={{0,1},{1,0},{2,3},{3,2},{4,5},{5,4},{6,7},{7,6},{8,9},{9,8},{10,11... | collective-permute-start | bytes 1179656 | tf_op jit(solution)/shard_map/ppermute | solution.py:208
  144.4 14.6 %copy-start.21 = (f32[1,2,2,128]{3,1,2,0:T(2,128)S(1)}, f32[1,2,2,128]{3,1,2,0:T(2,128)}, u32[]{:S(2)}) copy-start(f32[1,2,2,128]{3,1,2,0:T(2,128)} %copy-done.20) | copy-start | bytes 6148
  145.0 25.8 %all-to-all-start.1 = ((bf16[32,8,128]{2,1,0:T(8,128)(2,1)}), bf16[32,8,128]{2,1,0:T(8,128)(2,1)}, u32[]{:S(2)}, u32[]{:S(2)}) async-start(bf16[32,8,128]{2,1,0:T(8,128)(2,1)} %bitcast.40), calls=%async_computation.1 | async-start | bytes 131072 | tf_op jit(solution)/shard_map/all_to_all | solution.py:38
  158.3 0.7 copy-start.15
  161.0 9.8 %copy-start.13 = (f32[256,2,128]{0,2,1:T(8,128)S(1)}, f32[256,2,128]{0,2,1:T(8,128)}, u32[]{:S(2)}) copy-start(f32[256,2,128]{0,2,1:T(8,128)} %fusion.2) | copy-start | bytes 786436
  161.0 11.0 %copy-start.23 = (f32[256]{0:T(256)S(1)}, f32[256]{0:T(256)}, u32[]{:S(2)}) copy-start(f32[256]{0:T(256)} %param.9) | copy-start | bytes 3076
  167.1 1.6 copy-start
  172.2 14.0 %copy-start.1 = (bf16[2,8,384,256]{3,2,1,0:T(8,128)(2,1)S(1)}, bf16[2,8,384,256]{3,2,1,0:T(8,128)(2,1)}, u32[]{:S(2)}) copy-start(bf16[2,8,384,256]{3,2,1,0:T(8,128)(2,1)} %copy-done) | copy-start | bytes 9437188
  174.5 14.7 %collective-permute-start.21 = (bf16[8,256,384]{2,1,0:T(8,128)(2,1)S(1)}, bf16[8,256,384]{2,1,0:T(8,128)(2,1)S(1)}, u32[]{:S(2)}, u32[]{:S(2)}) collective-permute-start(bf16[8,256,384]{2,1,0:T(8,128)(2,1)S(1)} %convolution_convert_fusion), channel_id=1, source_target_pairs={{0,32},{32,0},{64,96},{96,64},{128,160},{160,128},{192,224},{224,1... | collective-permute-start | bytes 4718600 | tf_op jit(solution)/shard_map/ppermute | solution.py:239

commit v7 on v6

--- a/solution.py
+++ b/solution.py
@@ -126,7 +126,7 @@
         out_specs=[whole((rows, hi - lo)) for _, _, lo, hi, _ in jobs],
         compiler_params=pltpu.CompilerParams(vmem_limit_bytes=16 << 20),
         name="project",
-    )(where, *toks, *sums, *[block[0] if sums else in_hbm(block[0]) for block in blocks])
+    )(where, *toks, *sums, *[in_hbm(block[0]) for block in blocks])
 
 
 def make_body(n_seq, n_dp):
@@ -174,11 +174,14 @@
 
         columns = 3 * width
         where = jnp.stack([z, half, core]).astype(jnp.int32)
-        toks = (mine, theirs)
         known = [(pieces[o], o, 0, shard) for o in groups[0] + groups[1]]
         kv = 2 * width
-        jobs = [(0, None, 0, columns, f32), (1, None, 0, columns, f32)]
-        mine_sum, theirs_sum = project(where, toks, (), known, jobs, n_z, columns)
+        inner_count = len(groups[0])
+        full = (0, None, 0, columns, f32)
+        sums = project(where, (mine,), (), known[:inner_count], [full], n_z, columns)
+        (theirs_sum,) = project(where, (theirs,), (), known, [full], n_z, columns)
+        full = (0, 0, 0, columns, f32)
+        (mine_sum,) = project(where, (mine,), sums, known[inner_count:], [full], n_z, columns)
         final = jnp.concatenate([pieces[groups[2][0]], pieces[groups[2][1]], top, bottom], axis=0)
 
         def add_final(total, tok, lo, hi):

time: 216 us -> 220 us (1.019)
  waiting for transfers between devices: 33.6 us -> 29 us
  Pallas kernels: 9.12 us -> 13.1 us
  local copies, waits for them, and re-layouts: 16.2 us -> 18.9 us
    pallas_call x1 -> x3, Pallas kernels: 4.93 us -> 8.35 us  [project(): pl.pallas_call(kernel, out_shape=[jax.ShapeDtypeStruct((rows, hi - lo), k...]
    ppermute x1, waiting for transfers between devices: 3.41 us -> 0.01 us  [layer(): theirs = lax.ppermute(theirs, 'seq', flip)]
    all_to_all x1, waiting for transfers between devices: 2.07 us -> 4.98 us  [exclusive_state(): back = lax.all_to_all(earlier, 'seq', 0, 0, tiled=True)]
    ppermute x2, waiting for transfers between devices: 5.3 us -> 2.6 us  [layer(): swaps.append(lax.ppermute(packs[n], 'seq', flip))]
    unnamed x56 -> x54, local copies, waits for them, and re-layouts: 10.1 us -> 10.6 us
  transfers between devices with their start and end apart: 24 -> 24, of which waited for: 10 -> 9; matrix products, arithmetic and copies ran while one was open for 10% -> 12% of each run, Pallas kernels for 4% -> 6%
where the time goes in v7:
time: 220 us; the launch traced here: 218 us
  starting transfers between devices  116 us (53%)
  waiting for transfers between devices  29 us (13%)
  blocking collectives  24.1 us (11%)
  local copies, waits for them, and re-layouts  18.9 us (9%)
  Pallas kernels  13.1 us (6%)
  other arithmetic  8.56 us (4%)
  matrix products  8.29 us (4%)
    ppermute x7, starting transfers between devices, layer(): behind = lax.ppermute(behind, 'seq', down)  36.9 us
    all_to_all x1, blocking collectives, layer(): lax.all_to_all(keep.astype(jnp.bfloat16), 'dp', 0, 0, axis_index_groups=g...  24.1 us
    ppermute x7, waiting for transfers between devices, layer(): ahead = lax.ppermute(ahead, 'seq', up)  16.8 us
    ppermute x7, starting transfers between devices, layer(): ahead = lax.ppermute(ahead, 'seq', up)  15.8 us
    ppermute x1, starting transfers between devices, layer(): taken = lax.ppermute(give.astype(jnp.bfloat16), 'dp', pair_perm(n_dp))  13.4 us
    all_to_all x1, starting transfers between devices, exclusive_state(): back = lax.all_to_all(earlier, 'seq', 0, 0, tiled=True)  11.6 us
    all_to_all x1, starting transfers between devices, exclusive_state(): got = lax.all_to_all(sent, 'seq', 0, 0, tiled=True)  10.9 us
    unnamed x54, local copies, waits for them, and re-layouts  10.6 us
  transfers between devices with their start and end apart: 24, of which 9 were waited for; matrix products, arithmetic and copies ran while one was open for 12% of the time, Pallas kernels for 6%

profile of v7, /device:TPU:1, one launch (start us, length us, event | category | flops | bytes accessed | tf_op | source)
XLA Modules:
  0.0 218.5 jit_solution(15840983358061508481)
XLA Ops:
  2.0 4.4 %collective-permute-start = (bf16[192,1024]{1,0:T(8,128)(2,1)S(1)}, bf16[192,1024]{1,0:T(8,128)(2,1)S(1)}, u32[]{:S(2)}, u32[]{:S(2)}) collective-permute-start(bf16[192,1024]{1,0:T(8,128)(2,1)S(1)} %pad_maximum_fusion.1.refs_5_.refs_3_), channel_id=1, source_target_pairs={{0,2},{1,3},{2,4},{3,5},{4,6},{5,7},{6,8},{7,9},{8,10},{9,11},{10,... | collective-permute-start | bytes 1179656 | tf_op jit(solution)/shard_map/ppermute | solution.py:157
  6.3 9.5 %collective-permute-start.4 = (bf16[192,1024]{1,0:T(8,128)(2,1)S(1)}, bf16[192,1024]{1,0:T(8,128)(2,1)S(1)}, u32[]{:S(2)}, u32[]{:S(2)}) collective-permute-start(bf16[192,1024]{1,0:T(8,128)(2,1)S(1)} %pad_maximum_fusion.1.refs_5_.refs_3_), channel_id=1, source_target_pairs={{0,30},{1,31},{2,0},{3,1},{4,2},{5,3},{6,4},{7,5},{8,6},{9,7},{10,... | collective-permute-start | bytes 1179656 | tf_op jit(solution)/shard_map/ppermute | solution.py:158
  15.9 4.7 %copy.38 = bf16[256,6144]{0,1:T(8,128)(2,1)} copy(bf16[256,6144]{1,0:T(8,128)(2,1)} %param.5) | data formatting | bytes 6291456 | tf_op args[0]
  20.6 3.4 %dynamic-slice_bitcast_fusion = (bf16[16,192,256]{2,1,0:T(8,128)(2,1)}, bf16[16,192,256]{2,1,0:T(8,128)(2,1)S(1)}) fusion(bf16[16,2,192,256]{3,2,1,0:T(8,128)(2,1)} %bitcast.95, s32[]{:T(128)S(6)} %select_n.87, s32[]{:T(128)S(6)} %select_n.86), kind=kLoop, calls=%fused_computation.5 | loop fusion | bytes 6291464 | tf_op jit(solution)/shard_map/jit(dynamic_index_in_dim)/squeeze | solution.py:151
  23.9 1.9 collective-permute-start.1
  25.9 4.6 %collective-permute-start.5 = (bf16[192,1024]{1,0:T(8,128)(2,1)S(1)}, bf16[192,1024]{1,0:T(8,128)(2,1)S(1)}, u32[]{:S(2)}, u32[]{:S(2)}) collective-permute-start(bf16[192,1024]{1,0:T(8,128)(2,1)S(1)} %collective-permute-done.4.refs_6_.refs_4_), channel_id=1, source_target_pairs={{0,30},{1,31},{2,0},{3,1},{4,2},{5,3},{6,4},{7,5},{8,6},{9,7},{10,... | collective-permute-start | bytes 1179656 | tf_op jit(solution)/shard_map/ppermute | solution.py:158
  30.5 6.3 %collective-permute-done.1.refs_3_.refs_1_ = bf16[192,1024]{1,0:T(8,128)(2,1)S(1)} collective-permute-done((bf16[192,1024]{1,0:T(8,128)(2,1)S(1)}, bf16[192,1024]{1,0:T(8,128)(2,1)S(1)}, u32[]{:S(2)}, u32[]{:S(2)}) %collective-permute-start.1) | collective-permute-done | bytes 393248 | tf_op jit(solution)/shard_map/ppermute | solution.py:157
  36.8 1.9 collective-permute-start.2
  38.7 4.6 %collective-permute-start.6 = (bf16[192,1024]{1,0:T(8,128)(2,1)S(1)}, bf16[192,1024]{1,0:T(8,128)(2,1)S(1)}, u32[]{:S(2)}, u32[]{:S(2)}) collective-permute-start(bf16[192,1024]{1,0:T(8,128)(2,1)S(1)} %collective-permute-done.5.refs_7_.refs_5_), channel_id=1, source_target_pairs={{0,30},{1,31},{2,0},{3,1},{4,2},{5,3},{6,4},{7,5},{8,6},{9,7},{10,... | collective-permute-start | bytes 1179656 | tf_op jit(solution)/shard_map/ppermute | solution.py:158
  43.3 5.4 %collective-permute-done.2.refs_2_.refs_0_ = bf16[192,1024]{1,0:T(8,128)(2,1)S(1)} collective-permute-done((bf16[192,1024]{1,0:T(8,128)(2,1)S(1)}, bf16[192,1024]{1,0:T(8,128)(2,1)S(1)}, u32[]{:S(2)}, u32[]{:S(2)}) %collective-permute-start.2) | collective-permute-done | bytes 393248 | tf_op jit(solution)/shard_map/ppermute | solution.py:157
  48.7 1.9 collective-permute-start.3
  50.7 4.6 %collective-permute-start.7 = (bf16[192,1024]{1,0:T(8,128)(2,1)S(1)}, bf16[192,1024]{1,0:T(8,128)(2,1)}, u32[]{:S(2)}, u32[]{:S(2)}) collective-permute-start(bf16[192,1024]{1,0:T(8,128)(2,1)S(1)} %collective-permute-done.6.refs_8_.refs_6_), channel_id=1, source_target_pairs={{0,30},{1,31},{2,0},{3,1},{4,2},{5,3},{6,4},{7,5},{8,6},{9,7},{10,... | collective-permute-start | bytes 1179656 | tf_op jit(solution)/shard_map/ppermute | solution.py:158
  55.3 4.7 %collective-permute-start.16 = (bf16[16,192,256]{2,1,0:T(8,128)(2,1)}, bf16[16,192,256]{2,1,0:T(8,128)(2,1)S(1)}, u32[]{:S(2)}, u32[]{:S(2)}) collective-permute-start(bf16[16,192,256]{2,1,0:T(8,128)(2,1)} %get-tuple-element.12), channel_id=1, source_target_pairs={{0,1},{1,0},{2,3},{3,2},{4,5},{5,4},{6,7},{7,6},{8,9},{9,8},{10,11... | collective-permute-start | bytes 4718600 | tf_op jit(solution)/shard_map/ppermute | solution.py:166
  60.0 1.9 collective-permute-start.8
  61.9 4.6 %collective-permute-start.10 = (bf16[192,1024]{1,0:T(8,128)(2,1)}, bf16[192,1024]{1,0:T(8,128)(2,1)}, u32[]{:S(2)}, u32[]{:S(2)}) collective-permute-start(bf16[192,1024]{1,0:T(8,128)(2,1)} %collective-permute-done.7.refs_9_.refs_2_), channel_id=1, source_target_pairs={{0,30},{1,31},{2,0},{3,1},{4,2},{5,3},{6,4},{7,5},{8,6},{9,7},{10,... | collective-permute-start | bytes 1179656 | tf_op jit(solution)/shard_map/ppermute | solution.py:158
  68.3 2.0 collective-permute-done.8.refs_3_.refs_11_.refs_0_
  70.4 1.9 collective-permute-start.9
  72.3 4.6 %collective-permute-start.11 = (bf16[192,1024]{1,0:T(8,128)(2,1)}, bf16[192,1024]{1,0:T(8,128)(2,1)}, u32[]{:S(2)}, u32[]{:S(2)}) collective-permute-start(bf16[192,1024]{1,0:T(8,128)(2,1)} %collective-permute-done.10.refs_4_.refs_12_.refs_3_), channel_id=1, source_target_pairs={{0,30},{1,31},{2,0},{3,1},{4,2},{5,3},{6,4},{7,5},{8,6},{9,7},{10,... | collective-permute-start | bytes 1179656 | tf_op jit(solution)/shard_map/ppermute | solution.py:158
  77.6 3.0 %collective-permute-done.9.refs_2_.refs_10_.refs_1_ = bf16[192,1024]{1,0:T(8,128)(2,1)} collective-permute-done((bf16[192,1024]{1,0:T(8,128)(2,1)}, bf16[192,1024]{1,0:T(8,128)(2,1)}, u32[]{:S(2)}, u32[]{:S(2)}) %collective-permute-start.9) | collective-permute-done | bytes 393248 | tf_op jit(solution)/shard_map/ppermute | solution.py:157
  80.6 1.9 collective-permute-start.12
  82.5 4.6 %collective-permute-start.13 = (bf16[192,1024]{1,0:T(8,128)(2,1)}, bf16[192,1024]{1,0:T(8,128)(2,1)}, u32[]{:S(2)}, u32[]{:S(2)}) collective-permute-start(bf16[192,1024]{1,0:T(8,128)(2,1)} %collective-permute-done.11.refs_5_.refs_13_.refs_2_), channel_id=1, source_target_pairs={{0,30},{1,31},{2,0},{3,1},{4,2},{5,3},{6,4},{7,5},{8,6},{9,7},{10,... | collective-permute-start | bytes 1179656 | tf_op jit(solution)/shard_map/ppermute | solution.py:158
  88.9 2.9 %project.3.refs_1_ = f32[256,768]{1,0:T(8,128)S(1)} custom-call(s32[3]{0:T(128)S(1)} %pad_add_fusion.where_ref, bf16[16,192,256]{2,1,0:T(8,128)(2,1)S(1)} %get-tuple-element.10.refs_0_, bf16[192,1024]{1,0:T(8,128)(2,1)} %copy-done.9, bf16[192,1024]{1,0:T(8,128)(2,1)} %copy-done.7, bf16[192,1024]{1,0:T(8,128)(2,1)} %copy-done.5, bf16[192,1024]{1,0:T(8,128)(2,1)} %copy-done.3, ...), custom_call_target="tpu_custom_call" | custom-call | tf_op jit(solution)/shard_map/project/pallas_call | solution.py:116
  91.8 3.6 %project.5 = f32[256,768]{1,0:T(8,128)S(1)} custom-call(s32[3]{0:T(128)S(1)} %pad_add_fusion.where_ref, bf16[16,192,256]{2,1,0:T(8,128)(2,1)S(1)} %collective-permute-done.16.refs_0_, bf16[192,1024]{1,0:T(8,128)(2,1)} %copy-done.9, bf16[192,1024]{1,0:T(8,128)(2,1)} %copy-done.7, bf16[192,1024]{1,0:T(8,128)(2,1)} %copy-done.5, bf16[192,1024]{1,0:T(8,128)(2,1)} %copy-done.3, ...), custom_call_target="tpu_custom_call" | custom-call | tf_op jit(solution)/shard_map/project/pallas_call | solution.py:116
  95.4 1.9 project.4
  98.2 1.9 collective-permute-start.14
  101.1 4.6 %collective-permute-start.15 = (bf16[96,1024]{1,0:T(8,128)(2,1)S(1)}, bf16[96,1024]{1,0:T(8,128)(2,1)S(1)}, u32[]{:S(2)}, u32[]{:S(2)}) collective-permute-start(bf16[96,1024]{1,0:T(8,128)(2,1)S(1)} %slice.93), channel_id=1, source_target_pairs={{0,30},{1,31},{2,0},{3,1},{4,2},{5,3},{6,4},{7,5},{8,6},{9,7},{10,... | collective-permute-start | bytes 589832 | tf_op jit(solution)/shard_map/ppermute | solution.py:163
  106.7 1.0 constant_dynamic-update-slice_fusion.2
  109.0 4.5 %collective-permute-start.17 = (bf16[256,512]{1,0:T(8,128)(2,1)S(1)}, bf16[256,512]{1,0:T(8,128)(2,1)S(1)}, u32[]{:S(2)}, u32[]{:S(2)}) collective-permute-start(bf16[256,512]{1,0:T(8,128)(2,1)S(1)} %fusion.6), channel_id=1, source_target_pairs={{0,1},{1,0},{2,3},{3,2},{4,5},{5,4},{6,7},{7,6},{8,9},{9,8},{10,11... | collective-permute-start | bytes 786440 | tf_op jit(solution)/shard_map/ppermute | solution.py:197
  114.3 1.1 pack_outs.3.refs_2_
  115.9 1.8 collective-permute-done.17
  118.9 10.9 %all-to-all-start = ((bf16[32,16,128]{2,1,0:T(8,128)(2,1)}), bf16[32,16,128]{2,1,0:T(8,128)(2,1)}, u32[]{:S(2)}, u32[]{:S(2)}) async-start(bf16[32,16,128]{2,1,0:T(8,128)(2,1)} %fusion.38), calls=%async_computation | async-start | bytes 262144 | tf_op jit(solution)/shard_map/all_to_all | solution.py:28
  130.7 4.6 %collective-permute-start.18 = (bf16[1216,256]{1,0:T(8,128)(2,1)}, bf16[1216,256]{1,0:T(8,128)(2,1)}, u32[]{:S(2)}, u32[]{:S(2)}) collective-permute-start(bf16[1216,256]{1,0:T(8,128)(2,1)} %pad_maximum_fusion), channel_id=1, source_target_pairs={{0,1},{1,0},{2,3},{3,2},{4,5},{5,4},{6,7},{7,6},{8,9},{9,8},{10,11... | collective-permute-start | bytes 1867784 | tf_op jit(solution)/shard_map/ppermute | solution.py:214
  136.0 1.2 pack_outs.4.refs_0_
  137.2 2.2 %collective-permute-start.19 = (bf16[1344,256]{1,0:T(8,128)(2,1)S(1)}, bf16[1344,256]{1,0:T(8,128)(2,1)S(1)}, u32[]{:S(2)}, u32[]{:S(2)}) collective-permute-start(bf16[1344,256]{1,0:T(8,128)(2,1)S(1)} %pack_outs.4.refs_0_), channel_id=1, source_target_pairs={{0,1},{1,0},{2,3},{3,2},{4,5},{5,4},{6,7},{7,6},{8,9},{9,8},{10,11... | collective-permute-start | bytes 2064392 | tf_op jit(solution)/shard_map/ppermute | solution.py:211
  139.4 1.1 pack_outs.5.refs_1_
  140.5 4.6 %collective-permute-start.20 = (bf16[768,256]{1,0:T(8,128)(2,1)S(1)}, bf16[768,256]{1,0:T(8,128)(2,1)S(1)}, u32[]{:S(2)}, u32[]{:S(2)}) collective-permute-start(bf16[768,256]{1,0:T(8,128)(2,1)S(1)} %pack_outs.5.refs_1_), channel_id=1, source_target_pairs={{0,1},{1,0},{2,3},{3,2},{4,5},{5,4},{6,7},{7,6},{8,9},{9,8},{10,11... | collective-permute-start | bytes 1179656 | tf_op jit(solution)/shard_map/ppermute | solution.py:211
  145.9 1.2 fusion.53
  148.2 11.6 %all-to-all-start.1 = ((bf16[32,8,128]{2,1,0:T(8,128)(2,1)}), bf16[32,8,128]{2,1,0:T(8,128)(2,1)S(1)}, u32[]{:S(2)}, u32[]{:S(2)}) async-start(bf16[32,8,128]{2,1,0:T(8,128)(2,1)} %bitcast.40), calls=%async_computation.1 | async-start | bytes 131072 | tf_op jit(solution)/shard_map/all_to_all | solution.py:38
  159.7 2.1 fusion.35
  161.9 1.4 fusion.2
  163.4 2.6 %collective-permute-done.20.refs_4_ = bf16[768,256]{1,0:T(8,128)(2,1)S(1)} collective-permute-done((bf16[768,256]{1,0:T(8,128)(2,1)S(1)}, bf16[768,256]{1,0:T(8,128)(2,1)S(1)}, u32[]{:S(2)}, u32[]{:S(2)}) %collective-permute-start.20) | collective-permute-done | bytes 393248 | tf_op jit(solution)/shard_map/ppermute | solution.py:211
  166.0 1.3 place_outs.1
  167.3 1.6 copy-done
  168.9 5.0 %all-to-all-done.1 = bf16[32,8,128]{2,1,0:T(8,128)(2,1)S(1)} async-done(((bf16[32,8,128]{2,1,0:T(8,128)(2,1)}), bf16[32,8,128]{2,1,0:T(8,128)(2,1)S(1)}, u32[]{:S(2)}, u32[]{:S(2)}) %all-to-all-start.1) | async-done | bytes 65568 | tf_op jit(solution)/shard_map/all_to_all | solution.py:38
  174.4 2.3 %convolution_convert_fusion = bf16[8,256,384]{2,1,0:T(8,128)(2,1)S(1)} fusion(bf16[2,8,384,256]{3,2,1,0:T(8,128)(2,1)} %copy-done, bf16[256,256]{1,0:T(8,128)(2,1)S(1)} %copy.49), kind=kOutput, calls=%fused_computation.1 | convolution fusion | flops 403439616 | bytes 3276800 | tf_op jit(solution)/shard_map/itg,idg->itd/dot_general | solution.py:241
  176.7 13.4 %collective-permute-start.21 = (bf16[8,256,384]{2,1,0:T(8,128)(2,1)S(1)}, bf16[8,256,384]{2,1,0:T(8,128)(2,1)S(1)}, u32[]{:S(2)}, u32[]{:S(2)}) collective-permute-start(bf16[8,256,384]{2,1,0:T(8,128)(2,1)S(1)} %convolution_convert_fusion), channel_id=1, source_target_pairs={{0,32},{32,0},{64,96},{96,64},{128,160},{160,128},{192,224},{224,1... | collective-permute-start | bytes 4718600 | tf_op jit(solution)/shard_map/ppermute | solution.py:242
  190.8 2.3 %collective-permute-done.21 = bf16[8,256,384]{2,1,0:T(8,128)(2,1)S(1)} collective-permute-done((bf16[8,256,384]{2,1,0:T(8,128)(2,1)S(1)}, bf16[8,256,384]{2,1,0:T(8,128)(2,1)S(1)}, u32[]{:S(2)}, u32[]{:S(2)}) %collective-permute-start.21) | collective-permute-done | bytes 1572896 | tf_op jit(solution)/shard_map/ppermute | solution.py:242
  193.5 24.1 %all_to_all.15 = bf16[8,256,384]{2,1,0:T(8,128)(2,1)S(1)} all-to-all(bf16[8,256,384]{2,1,0:T(8,128)(2,1)S(1)} %add_convert_fusion), channel_id=1, replica_groups={{0,64,128,192,256,320,384,448},{32,96,160,224,288,352,416,480},{1,65,12..., dimensions={0} | all-to-all | bytes 3145728 | tf_op jit(solution)/shard_map/all_to_all | solution.py:246
  (108 shorter events, 18.6 us)
Async XLA Ops:
  2.0 18.6 %copy-start.2 = (bf16[192,1024]{1,0:T(8,128)(2,1)}, bf16[192,1024]{1,0:T(8,128)(2,1)S(1)}, u32[]{:S(2)}) copy-start(bf16[192,1024]{1,0:T(8,128)(2,1)S(1)} %pad_maximum_fusion.1.refs_5_.refs_3_) | copy-start | bytes 1179652
  2.0 22.0 %collective-permute-start = (bf16[192,1024]{1,0:T(8,128)(2,1)S(1)}, bf16[192,1024]{1,0:T(8,128)(2,1)S(1)}, u32[]{:S(2)}, u32[]{:S(2)}) collective-permute-start(bf16[192,1024]{1,0:T(8,128)(2,1)S(1)} %pad_maximum_fusion.1.refs_5_.refs_3_), channel_id=1, source_target_pairs={{0,2},{1,3},{2,4},{3,5},{4,6},{5,7},{6,8},{7,9},{8,10},{9,11},{10,... | collective-permute-start | bytes 1179656 | tf_op jit(solution)/shard_map/ppermute | solution.py:157
  6.3 19.5 %collective-permute-start.4 = (bf16[192,1024]{1,0:T(8,128)(2,1)S(1)}, bf16[192,1024]{1,0:T(8,128)(2,1)S(1)}, u32[]{:S(2)}, u32[]{:S(2)}) collective-permute-start(bf16[192,1024]{1,0:T(8,128)(2,1)S(1)} %pad_maximum_fusion.1.refs_5_.refs_3_), channel_id=1, source_target_pairs={{0,30},{1,31},{2,0},{3,1},{4,2},{5,3},{6,4},{7,5},{8,6},{9,7},{10,... | collective-permute-start | bytes 1179656 | tf_op jit(solution)/shard_map/ppermute | solution.py:158
  20.6 45.9 %copy-start.21 = (f32[2,256]{1,0:T(2,128)S(1)}, f32[2,256]{1,0:T(2,128)}, u32[]{:S(2)}) copy-start(f32[2,256]{1,0:T(2,128)} %param.8) | copy-start | bytes 6148
  23.9 26.7 %copy-start.3 = (bf16[192,1024]{1,0:T(8,128)(2,1)}, bf16[192,1024]{1,0:T(8,128)(2,1)S(1)}, u32[]{:S(2)}) copy-start(bf16[192,1024]{1,0:T(8,128)(2,1)S(1)} %collective-permute-done.refs_4_.refs_2_) | copy-start | bytes 1179652
  23.9 12.8 %collective-permute-start.1 = (bf16[192,1024]{1,0:T(8,128)(2,1)S(1)}, bf16[192,1024]{1,0:T(8,128)(2,1)S(1)}, u32[]{:S(2)}, u32[]{:S(2)}) collective-permute-start(bf16[192,1024]{1,0:T(8,128)(2,1)S(1)} %collective-permute-done.refs_4_.refs_2_), channel_id=1, source_target_pairs={{0,2},{1,3},{2,4},{3,5},{4,6},{5,7},{6,8},{7,9},{8,10},{9,11},{10,... | collective-permute-start | bytes 1179656 | tf_op jit(solution)/shard_map/ppermute | solution.py:157
  25.9 24.8 %copy-start.4 = (bf16[192,1024]{1,0:T(8,128)(2,1)}, bf16[192,1024]{1,0:T(8,128)(2,1)S(1)}, u32[]{:S(2)}) copy-start(bf16[192,1024]{1,0:T(8,128)(2,1)S(1)} %collective-permute-done.4.refs_6_.refs_4_) | copy-start | bytes 1179652
  25.9 12.8 %collective-permute-start.5 = (bf16[192,1024]{1,0:T(8,128)(2,1)S(1)}, bf16[192,1024]{1,0:T(8,128)(2,1)S(1)}, u32[]{:S(2)}, u32[]{:S(2)}) collective-permute-start(bf16[192,1024]{1,0:T(8,128)(2,1)S(1)} %collective-permute-done.4.refs_6_.refs_4_), channel_id=1, source_target_pairs={{0,30},{1,31},{2,0},{3,1},{4,2},{5,3},{6,4},{7,5},{8,6},{9,7},{10,... | collective-permute-start | bytes 1179656 | tf_op jit(solution)/shard_map/ppermute | solution.py:158
  36.8 18.5 %copy-start.5 = (bf16[192,1024]{1,0:T(8,128)(2,1)}, bf16[192,1024]{1,0:T(8,128)(2,1)S(1)}, u32[]{:S(2)}) copy-start(bf16[192,1024]{1,0:T(8,128)(2,1)S(1)} %collective-permute-done.1.refs_3_.refs_1_) | copy-start | bytes 1179652
  36.8 12.0 %collective-permute-start.2 = (bf16[192,1024]{1,0:T(8,128)(2,1)S(1)}, bf16[192,1024]{1,0:T(8,128)(2,1)S(1)}, u32[]{:S(2)}, u32[]{:S(2)}) collective-permute-start(bf16[192,1024]{1,0:T(8,128)(2,1)S(1)} %collective-permute-done.1.refs_3_.refs_1_), channel_id=1, source_target_pairs={{0,2},{1,3},{2,4},{3,5},{4,6},{5,7},{6,8},{7,9},{8,10},{9,11},{10,... | collective-permute-start | bytes 1179656 | tf_op jit(solution)/shard_map/ppermute | solution.py:157
  38.7 12.0 %copy-start.6 = (bf16[192,1024]{1,0:T(8,128)(2,1)}, bf16[192,1024]{1,0:T(8,128)(2,1)S(1)}, u32[]{:S(2)}) copy-start(bf16[192,1024]{1,0:T(8,128)(2,1)S(1)} %collective-permute-done.5.refs_7_.refs_5_) | copy-start | bytes 1179652
  38.7 11.9 %collective-permute-start.6 = (bf16[192,1024]{1,0:T(8,128)(2,1)S(1)}, bf16[192,1024]{1,0:T(8,128)(2,1)S(1)}, u32[]{:S(2)}, u32[]{:S(2)}) collective-permute-start(bf16[192,1024]{1,0:T(8,128)(2,1)S(1)} %collective-permute-done.5.refs_7_.refs_5_), channel_id=1, source_target_pairs={{0,30},{1,31},{2,0},{3,1},{4,2},{5,3},{6,4},{7,5},{8,6},{9,7},{10,... | collective-permute-start | bytes 1179656 | tf_op jit(solution)/shard_map/ppermute | solution.py:158
  48.7 11.2 %copy-start.7 = (bf16[192,1024]{1,0:T(8,128)(2,1)}, bf16[192,1024]{1,0:T(8,128)(2,1)S(1)}, u32[]{:S(2)}) copy-start(bf16[192,1024]{1,0:T(8,128)(2,1)S(1)} %collective-permute-done.2.refs_2_.refs_0_) | copy-start | bytes 1179652
  48.7 11.2 %collective-permute-start.3 = (bf16[192,1024]{1,0:T(8,128)(2,1)S(1)}, bf16[192,1024]{1,0:T(8,128)(2,1)S(1)}, u32[]{:S(2)}, u32[]{:S(2)}) collective-permute-start(bf16[192,1024]{1,0:T(8,128)(2,1)S(1)} %collective-permute-done.2.refs_2_.refs_0_), channel_id=1, source_target_pairs={{0,2},{1,3},{2,4},{3,5},{4,6},{5,7},{6,8},{7,9},{8,10},{9,11},{10,... | collective-permute-start | bytes 1179656 | tf_op jit(solution)/shard_map/ppermute | solution.py:157
  50.7 9.3 %copy-start.8 = (bf16[192,1024]{1,0:T(8,128)(2,1)}, bf16[192,1024]{1,0:T(8,128)(2,1)S(1)}, u32[]{:S(2)}) copy-start(bf16[192,1024]{1,0:T(8,128)(2,1)S(1)} %collective-permute-done.6.refs_8_.refs_6_) | copy-start | bytes 1179652
  50.7 11.2 %collective-permute-start.7 = (bf16[192,1024]{1,0:T(8,128)(2,1)S(1)}, bf16[192,1024]{1,0:T(8,128)(2,1)}, u32[]{:S(2)}, u32[]{:S(2)}) collective-permute-start(bf16[192,1024]{1,0:T(8,128)(2,1)S(1)} %collective-permute-done.6.refs_8_.refs_6_), channel_id=1, source_target_pairs={{0,30},{1,31},{2,0},{3,1},{4,2},{5,3},{6,4},{7,5},{8,6},{9,7},{10,... | collective-permute-start | bytes 1179656 | tf_op jit(solution)/shard_map/ppermute | solution.py:158
  55.3 36.5 %collective-permute-start.16 = (bf16[16,192,256]{2,1,0:T(8,128)(2,1)}, bf16[16,192,256]{2,1,0:T(8,128)(2,1)S(1)}, u32[]{:S(2)}, u32[]{:S(2)}) collective-permute-start(bf16[16,192,256]{2,1,0:T(8,128)(2,1)} %get-tuple-element.12), channel_id=1, source_target_pairs={{0,1},{1,0},{2,3},{3,2},{4,5},{5,4},{6,7},{7,6},{8,9},{9,8},{10,11... | collective-permute-start | bytes 4718600 | tf_op jit(solution)/shard_map/ppermute | solution.py:166
  60.0 28.7 %copy-start.9 = (bf16[192,1024]{1,0:T(8,128)(2,1)}, bf16[192,1024]{1,0:T(8,128)(2,1)S(1)}, u32[]{:S(2)}) copy-start(bf16[192,1024]{1,0:T(8,128)(2,1)S(1)} %collective-permute-done.3.refs_1_) | copy-start | bytes 1179652
  60.0 10.4 %collective-permute-start.8 = (bf16[192,1024]{1,0:T(8,128)(2,1)S(1)}, bf16[192,1024]{1,0:T(8,128)(2,1)}, u32[]{:S(2)}, u32[]{:S(2)}) collective-permute-start(bf16[192,1024]{1,0:T(8,128)(2,1)S(1)} %collective-permute-done.3.refs_1_), channel_id=1, source_target_pairs={{0,2},{1,3},{2,4},{3,5},{4,6},{5,7},{6,8},{7,9},{8,10},{9,11},{10,... | collective-permute-start | bytes 1179656 | tf_op jit(solution)/shard_map/ppermute | solution.py:157
  61.9 10.4 %collective-permute-start.10 = (bf16[192,1024]{1,0:T(8,128)(2,1)}, bf16[192,1024]{1,0:T(8,128)(2,1)}, u32[]{:S(2)}, u32[]{:S(2)}) collective-permute-start(bf16[192,1024]{1,0:T(8,128)(2,1)} %collective-permute-done.7.refs_9_.refs_2_), channel_id=1, source_target_pairs={{0,30},{1,31},{2,0},{3,1},{4,2},{5,3},{6,4},{7,5},{8,6},{9,7},{10,... | collective-permute-start | bytes 1179656 | tf_op jit(solution)/shard_map/ppermute | solution.py:158
  67.6 0.6 copy-start.19
  70.4 10.2 %collective-permute-start.9 = (bf16[192,1024]{1,0:T(8,128)(2,1)}, bf16[192,1024]{1,0:T(8,128)(2,1)}, u32[]{:S(2)}, u32[]{:S(2)}) collective-permute-start(bf16[192,1024]{1,0:T(8,128)(2,1)} %collective-permute-done.8.refs_3_.refs_11_.refs_0_), channel_id=1, source_target_pairs={{0,2},{1,3},{2,4},{3,5},{4,6},{5,7},{6,8},{7,9},{8,10},{9,11},{10,... | collective-permute-start | bytes 1179656 | tf_op jit(solution)/shard_map/ppermute | solution.py:157
  72.3 10.2 %collective-permute-start.11 = (bf16[192,1024]{1,0:T(8,128)(2,1)}, bf16[192,1024]{1,0:T(8,128)(2,1)}, u32[]{:S(2)}, u32[]{:S(2)}) collective-permute-start(bf16[192,1024]{1,0:T(8,128)(2,1)} %collective-permute-done.10.refs_4_.refs_12_.refs_3_), channel_id=1, source_target_pairs={{0,30},{1,31},{2,0},{3,1},{4,2},{5,3},{6,4},{7,5},{8,6},{9,7},{10,... | collective-permute-start | bytes 1179656 | tf_op jit(solution)/shard_map/ppermute | solution.py:158
  80.6 16.7 %collective-permute-start.12 = (bf16[192,1024]{1,0:T(8,128)(2,1)}, bf16[192,1024]{1,0:T(8,128)(2,1)}, u32[]{:S(2)}, u32[]{:S(2)}) collective-permute-start(bf16[192,1024]{1,0:T(8,128)(2,1)} %collective-permute-done.9.refs_2_.refs_10_.refs_1_), channel_id=1, source_target_pairs={{0,2},{1,3},{2,4},{3,5},{4,6},{5,7},{6,8},{7,9},{8,10},{9,11},{10,... | collective-permute-start | bytes 1179656 | tf_op jit(solution)/shard_map/ppermute | solution.py:157
  82.5 17.7 %collective-permute-start.13 = (bf16[192,1024]{1,0:T(8,128)(2,1)}, bf16[192,1024]{1,0:T(8,128)(2,1)}, u32[]{:S(2)}, u32[]{:S(2)}) collective-permute-start(bf16[192,1024]{1,0:T(8,128)(2,1)} %collective-permute-done.11.refs_5_.refs_13_.refs_2_), channel_id=1, source_target_pairs={{0,30},{1,31},{2,0},{3,1},{4,2},{5,3},{6,4},{7,5},{8,6},{9,7},{10,... | collective-permute-start | bytes 1179656 | tf_op jit(solution)/shard_map/ppermute | solution.py:158
  88.8 26.6 %copy-start.14 = (bf16[192,256]{1,0:T(8,128)(2,1)}, bf16[192,256]{1,0:T(8,128)(2,1)S(1)}, u32[]{:S(2)}) copy-start(bf16[192,256]{1,0:T(8,128)(2,1)S(1)} %get-tuple-element.20) | copy-start | bytes 294916
  88.8 26.6 %copy-start.15 = (bf16[192,256]{1,0:T(8,128)(2,1)}, bf16[192,256]{1,0:T(8,128)(2,1)S(1)}, u32[]{:S(2)}) copy-start(bf16[192,256]{1,0:T(8,128)(2,1)S(1)} %get-tuple-element.21) | copy-start | bytes 294916
  88.8 26.6 %copy-start.16 = (bf16[192,256]{1,0:T(8,128)(2,1)}, bf16[192,256]{1,0:T(8,128)(2,1)S(1)}, u32[]{:S(2)}) copy-start(bf16[192,256]{1,0:T(8,128)(2,1)S(1)} %get-tuple-element.22) | copy-start | bytes 294916
  98.2 9.5 %collective-permute-start.14 = (bf16[96,1024]{1,0:T(8,128)(2,1)S(1)}, bf16[96,1024]{1,0:T(8,128)(2,1)S(1)}, u32[]{:S(2)}, u32[]{:S(2)}) collective-permute-start(bf16[96,1024]{1,0:T(8,128)(2,1)S(1)} %slice.92), channel_id=1, source_target_pairs={{0,2},{1,3},{2,4},{3,5},{4,6},{5,7},{6,8},{7,9},{8,10},{9,11},{10,... | collective-permute-start | bytes 589832 | tf_op jit(solution)/shard_map/ppermute | solution.py:162
  101.1 7.2 %collective-permute-start.15 = (bf16[96,1024]{1,0:T(8,128)(2,1)S(1)}, bf16[96,1024]{1,0:T(8,128)(2,1)S(1)}, u32[]{:S(2)}, u32[]{:S(2)}) collective-permute-start(bf16[96,1024]{1,0:T(8,128)(2,1)S(1)} %slice.93), channel_id=1, source_target_pairs={{0,30},{1,31},{2,0},{3,1},{4,2},{5,3},{6,4},{7,5},{8,6},{9,7},{10,... | collective-permute-start | bytes 589832 | tf_op jit(solution)/shard_map/ppermute | solution.py:163
  108.3 7.1 %copy-start.12 = (bf16[576,1024]{1,0:T(8,128)(2,1)}, bf16[576,1024]{1,0:T(8,128)(2,1)S(1)}, u32[]{:S(2)}) copy-start(bf16[576,1024]{1,0:T(8,128)(2,1)S(1)} %constant_dynamic-update-slice_fusion) | copy-start | bytes 3538948
  109.0 8.6 %collective-permute-start.17 = (bf16[256,512]{1,0:T(8,128)(2,1)S(1)}, bf16[256,512]{1,0:T(8,128)(2,1)S(1)}, u32[]{:S(2)}, u32[]{:S(2)}) collective-permute-start(bf16[256,512]{1,0:T(8,128)(2,1)S(1)} %fusion.6), channel_id=1, source_target_pairs={{0,1},{1,0},{2,3},{3,2},{4,5},{5,4},{6,7},{7,6},{8,9},{9,8},{10,11... | collective-permute-start | bytes 786440 | tf_op jit(solution)/shard_map/ppermute | solution.py:197
  115.9 2.1 copy-start.18
  117.8 17.5 %copy-start.10 = (f32[256,512]{1,0:T(8,128)}, f32[256,512]{1,0:T(8,128)S(1)}, u32[]{:S(2)}) copy-start(f32[256,512]{1,0:T(8,128)S(1)} %fusion.7) | copy-start | bytes 1572868
  118.0 17.3 %copy-start.11 = (bf16[256,256]{0,1:T(8,128)(2,1)}, bf16[256,256]{0,1:T(8,128)(2,1)S(1)}, u32[]{:S(2)}) copy-start(bf16[256,256]{0,1:T(8,128)(2,1)S(1)} %copy.54) | copy-start | bytes 393220
  118.9 26.2 %all-to-all-start = ((bf16[32,16,128]{2,1,0:T(8,128)(2,1)}), bf16[32,16,128]{2,1,0:T(8,128)(2,1)}, u32[]{:S(2)}, u32[]{:S(2)}) async-start(bf16[32,16,128]{2,1,0:T(8,128)(2,1)} %fusion.38), calls=%async_computation | async-start | bytes 262144 | tf_op jit(solution)/shard_map/all_to_all | solution.py:28
  130.7 29.0 %collective-permute-start.18 = (bf16[1216,256]{1,0:T(8,128)(2,1)}, bf16[1216,256]{1,0:T(8,128)(2,1)}, u32[]{:S(2)}, u32[]{:S(2)}) collective-permute-start(bf16[1216,256]{1,0:T(8,128)(2,1)} %pad_maximum_fusion), channel_id=1, source_target_pairs={{0,1},{1,0},{2,3},{3,2},{4,5},{5,4},{6,7},{7,6},{8,9},{9,8},{10,11... | collective-permute-start | bytes 1867784 | tf_op jit(solution)/shard_map/ppermute | solution.py:214
  137.2 26.2 %collective-permute-start.19 = (bf16[1344,256]{1,0:T(8,128)(2,1)S(1)}, bf16[1344,256]{1,0:T(8,128)(2,1)S(1)}, u32[]{:S(2)}, u32[]{:S(2)}) collective-permute-start(bf16[1344,256]{1,0:T(8,128)(2,1)S(1)} %pack_outs.4.refs_0_), channel_id=1, source_target_pairs={{0,1},{1,0},{2,3},{3,2},{4,5},{5,4},{6,7},{7,6},{8,9},{9,8},{10,11... | collective-permute-start | bytes 2064392 | tf_op jit(solution)/shard_map/ppermute | solution.py:211
  140.5 25.5 %collective-permute-start.20 = (bf16[768,256]{1,0:T(8,128)(2,1)S(1)}, bf16[768,256]{1,0:T(8,128)(2,1)S(1)}, u32[]{:S(2)}, u32[]{:S(2)}) collective-permute-start(bf16[768,256]{1,0:T(8,128)(2,1)S(1)} %pack_outs.5.refs_1_), channel_id=1, source_target_pairs={{0,1},{1,0},{2,3},{3,2},{4,5},{5,4},{6,7},{7,6},{8,9},{9,8},{10,11... | collective-permute-start | bytes 1179656 | tf_op jit(solution)/shard_map/ppermute | solution.py:211
  147.5 14.4 %copy-start.20 = (f32[1,2,2,128]{3,1,2,0:T(2,128)S(1)}, f32[1,2,2,128]{3,1,2,0:T(2,128)}, u32[]{:S(2)}) copy-start(f32[1,2,2,128]{3,1,2,0:T(2,128)} %copy-done.19) | copy-start | bytes 6148
  148.2 25.8 %all-to-all-start.1 = ((bf16[32,8,128]{2,1,0:T(8,128)(2,1)}), bf16[32,8,128]{2,1,0:T(8,128)(2,1)S(1)}, u32[]{:S(2)}, u32[]{:S(2)}) async-start(bf16[32,8,128]{2,1,0:T(8,128)(2,1)} %bitcast.40), calls=%async_computation.1 | async-start | bytes 131072 | tf_op jit(solution)/shard_map/all_to_all | solution.py:38
  163.3 10.6 %copy-start.13 = (bf16[32,2,8,128]{3,2,1,0:T(8,128)(2,1)S(1)}, bf16[32,2,8,128]{3,2,1,0:T(8,128)(2,1)}, u32[]{:S(2)}) copy-start(bf16[32,2,8,128]{3,2,1,0:T(8,128)(2,1)} %fusion.35) | copy-start | bytes 393220
  163.3 10.6 %copy-start.17 = (f32[256,2]{0,1:T(2,128)S(1)}, f32[256,2]{0,1:T(2,128)}, u32[]{:S(2)}) copy-start(f32[256,2]{0,1:T(2,128)} %get-tuple-element.26) | copy-start | bytes 6148
  163.4 10.8 %copy-start.22 = (f32[256]{0:T(256)S(1)}, f32[256]{0:T(256)}, u32[]{:S(2)}) copy-start(f32[256]{0:T(256)} %param.9) | copy-start | bytes 3076
  167.3 1.6 copy-start
  174.4 15.7 %copy-start.1 = (bf16[2,8,384,256]{3,2,1,0:T(8,128)(2,1)S(1)}, bf16[2,8,384,256]{3,2,1,0:T(8,128)(2,1)}, u32[]{:S(2)}) copy-start(bf16[2,8,384,256]{3,2,1,0:T(8,128)(2,1)} %copy-done) | copy-start | bytes 9437188
  176.7 16.4 %collective-permute-start.21 = (bf16[8,256,384]{2,1,0:T(8,128)(2,1)S(1)}, bf16[8,256,384]{2,1,0:T(8,128)(2,1)S(1)}, u32[]{:S(2)}, u32[]{:S(2)}) collective-permute-start(bf16[8,256,384]{2,1,0:T(8,128)(2,1)S(1)} %convolution_convert_fusion), channel_id=1, source_target_pairs={{0,32},{32,0},{64,96},{96,64},{128,160},{160,128},{192,224},{224,1... | collective-permute-start | bytes 4718600 | tf_op jit(solution)/shard_map/ppermute | solution.py:242
